TPU v7x, 32 devices: a whole 2x2x4 slice. The times are simulated.
32 devices in a mesh: fibre: 2 (over y), chan: 4 (over z), tm: 2 (over x), win: 2 (over core).
Axes of the slice: x: 2, y: 2, z: 4, core: 2. Of those that a mesh axis runs over, the one named last changes fastest.
Arguments:
- records: bfloat16 [64, 16, 16384], P(('fibre', 'chan'), 'win', 'tm'), parts along dimension 0, may hold values from -32 to 32, as said below
- filter_taps: bfloat16 [64], replicated, may hold values from -0.75 to 0.75
- segment_end: int32 [32], P(('fibre', 'win')), parts along dimension 0, may hold values from 8192 to 16384, as said below
- pair_mask: int32 [8, 3], P(('fibre', 'chan')), parts along dimension 0, may hold values 0 or 1
Outputs:
- correlation: float32 [3, 8, 64, 3840], P(None, 'win', ('fibre', 'chan', 'tm')), parts along dimension 2
There are 2 independent parts, one for each index of `fibre`. A program takes and returns all parts, laid end to end along the dimension named above; an argument that names none is the same for every part. Nothing has to cross between parts.
Inputs may be any that keep to these rules, and one draw needn't show every extreme that they name: `records`: samples are clipped at the recorder's full scale. `segment_end`: samples of a window at or after this index are missing; some window is complete and some keeps only its first half.
All inputs are finite; a program needn't handle non-finite values. No bound on the sum of `pair_mask` on one device may be relied on, other than what follows from the above.
Results may differ from a plain program's by a relative error of at most 0.0047.
Values may be sent and summed in bfloat16 or wider, within the bound.
No kernel may reach another device: no remote copies, remote signals or barrier semaphores. Data moves between devices by JAX's collectives and lax.ppermute only.
A program may use at most 128 MiB of HBM per device.

v0:
```python
import math

import jax
import jax.numpy as jnp
from jax import lax
from jax.sharding import PartitionSpec as P

MAXLAG = 1920
BAND = 64


EPSILON = 1e-06
HIGHEST = lax.Precision.HIGHEST


def from_behind(array, axis, by):
    count = lax.axis_size(axis)
    pairs = [(i, i + by) for i in range(count) if 0 <= i + by < count]
    return lax.ppermute(array, axis, pairs)


def passed_along(array, axis, by):
    count = lax.axis_size(axis)
    return lax.ppermute(array, axis, [(i, (i + by) % count) for i in range(count)])


def phasor_table(row_count, col_count, period):
    first_index = lax.broadcasted_iota(jnp.int32, (row_count, col_count), 0)
    second_index = lax.broadcasted_iota(jnp.int32, (row_count, col_count), 1)
    angle_table = 2.0 * math.pi / period * (first_index * second_index % period).astype(jnp.float32)
    return (jnp.cos(angle_table), jnp.sin(angle_table))


def product(pattern, first_arg, second_arg):
    return jnp.einsum(pattern, first_arg, second_arg, precision=HIGHEST)


def decimation_table(filter_taps):
    tap_count = filter_taps.shape[0]
    quarter = tap_count // 4
    grouped = filter_taps.astype(jnp.float32).reshape(quarter, 4)[:, ::-1]
    grid_shape = (quarter + 128, 128, quarter)
    row_group = lax.broadcasted_iota(jnp.int32, grid_shape, 0)
    column = lax.broadcasted_iota(jnp.int32, grid_shape, 1)
    within = lax.broadcasted_iota(jnp.int32, grid_shape, 2)
    select = (column - row_group + quarter == within).astype(jnp.float32)
    band_table = product("ucm,mv->uvc", select, grouped)
    return band_table.reshape(4 * (quarter + 128), 128).astype(jnp.bfloat16)


def decimate(records, segment_end, filter_taps):
    channels, windows, length = records.shape
    tap_count = filter_taps.shape[0]
    position = lax.axis_index("tm") * length + lax.broadcasted_iota(jnp.int32, (1, 1, length), 2)
    retained = jnp.where(position < segment_end[None, :, None], records, jnp.zeros_like(records))
    earlier = from_behind(retained[:, :, length - tap_count :], "tm", 1)
    blocks = retained.reshape(channels, windows, length // 512, 512)
    leading = jnp.concatenate(
        [earlier[:, :, None, :], blocks[:, :, :-1, 512 - tap_count :]], axis=2
    )
    joined = jnp.concatenate([leading, blocks], axis=3)
    output = jnp.einsum(
        "cwbr,rn->cwbn", joined, decimation_table(filter_taps), preferred_element_type=jnp.float32
    )
    return output.reshape(channels, windows, length // 4).astype(jnp.bfloat16)


def whiten(timeline):
    channels, windows, span_len = timeline.shape
    stride_rows = span_len // 128
    band_part = BAND // stride_rows
    signal = timeline.astype(jnp.float32).reshape(channels, windows, stride_rows, 128)
    cos_small, sin_small = phasor_table(stride_rows, stride_rows, stride_rows)
    first_re = product("qa,cwab->cwqb", cos_small, signal)
    first_im = -product("qa,cwab->cwqb", sin_small, signal)
    cos_twist, sin_twist = phasor_table(stride_rows, 128, span_len)
    turned_re = first_re * cos_twist + first_im * sin_twist
    turned_im = first_im * cos_twist - first_re * sin_twist
    cos_large, sin_large = phasor_table(64, 128, 128)
    spec_re = product("cwqb,pb->cwqp", turned_re, cos_large) + product(
        "cwqb,pb->cwqp", turned_im, sin_large
    )
    spec_im = product("cwqb,pb->cwqp", turned_im, cos_large) - product(
        "cwqb,pb->cwqp", turned_re, sin_large
    )
    spec_power = spec_re * spec_re + spec_im * spec_im
    banded_shape = (channels, windows, stride_rows, stride_rows, band_part)
    energy = jnp.mean(spec_power.reshape(banded_shape), axis=(2, 4), keepdims=True)
    divisor = jnp.sqrt(energy + EPSILON)
    bin_index = lax.broadcasted_iota(jnp.int32, (stride_rows, 64), 0) * 64 + lax.broadcasted_iota(
        jnp.int32, (stride_rows, 64), 1
    )
    nonzero = (bin_index > 0).astype(jnp.float32)
    white_re = (spec_re.reshape(banded_shape) / divisor).reshape(
        channels, windows, stride_rows, 64
    ) * nonzero
    white_im = (spec_im.reshape(banded_shape) / divisor).reshape(
        channels, windows, stride_rows, 64
    ) * nonzero
    stacked = jnp.stack([white_re, white_im], axis=2)
    return stacked.reshape(channels, windows, 2, span_len // 2).astype(jnp.bfloat16)


def cross_spectrum(own_block, remote):

    def contract(remote_part, own_part):
        return jnp.einsum("jwk,iwk->jik", remote_part, own_part, preferred_element_type=jnp.float32)

    real_part = contract(remote[:, :, 0], own_block[:, :, 0]) + contract(
        remote[:, :, 1], own_block[:, :, 1]
    )
    imag_part = contract(remote[:, :, 0], own_block[:, :, 1]) - contract(
        remote[:, :, 1], own_block[:, :, 0]
    )
    return jnp.stack([real_part, imag_part], axis=2)


def lag_window(flat, max_lag):
    total = flat.shape[-1]
    return jnp.concatenate([flat[..., total - max_lag :], flat[..., :max_lag]], axis=-1)


def lag_domain(cross, max_lag):
    pair_rows = cross.shape[0]
    owned = cross.shape[1]
    bin_count = cross.shape[3]
    stride_rows = 2 * bin_count // 128
    spectral_grid = cross.reshape(pair_rows, owned, 2, stride_rows, 64)
    grid_re = spectral_grid[:, :, 0]
    grid_im = spectral_grid[:, :, 1]
    cos_large, sin_large = phasor_table(64, 128, 128)
    first_re = product("nmqp,pb->nmqb", grid_re, cos_large) - product(
        "nmqp,pb->nmqb", grid_im, sin_large
    )
    first_im = product("nmqp,pb->nmqb", grid_re, sin_large) + product(
        "nmqp,pb->nmqb", grid_im, cos_large
    )
    cos_twist, sin_twist = phasor_table(stride_rows, 128, 2 * bin_count)
    turned_re = first_re * cos_twist - first_im * sin_twist
    turned_im = first_re * sin_twist + first_im * cos_twist
    cos_small, sin_small = phasor_table(stride_rows, stride_rows, stride_rows)
    circular = product("aq,nmqb->nmab", cos_small, turned_re) - product(
        "aq,nmqb->nmab", sin_small, turned_im
    )
    flat = circular.reshape(pair_rows, owned, stride_rows * 128)
    lagged = lag_window(flat, max_lag)
    return lagged


def stack_pairs(own_block, remote):
    cross = cross_spectrum(own_block, remote)
    return lax.psum_scatter(lag_domain(cross, MAXLAG), "win", scatter_dimension=0, tiled=True)


def shards(records, filter_taps, segment_end, pair_mask):
    decimated = decimate(records, segment_end, filter_taps)
    own_block = whiten(lax.all_to_all(decimated, "tm", split_axis=0, concat_axis=2, tiled=True))
    whole_block = lax.all_gather(own_block, "tm", axis=0, tiled=True)
    reach = (pair_mask.shape[1] - 1) // 2
    lag_count = 2 * MAXLAG
    windows_all = own_block.shape[1] * lax.axis_size("win")
    weights = pair_mask[0].astype(jnp.float32) / math.sqrt(windows_all * own_block.shape[3])
    result = jnp.zeros(
        (
            2 * reach + 1,
            whole_block.shape[0] // lax.axis_size("win"),
            own_block.shape[0],
            lag_count,
        ),
        jnp.float32,
    )

    def place(current, lagged, offset_index):
        weight = lax.dynamic_index_in_dim(weights, offset_index, 0, keepdims=False)
        return lax.dynamic_update_slice(current, (lagged * weight)[None], (offset_index, 0, 0, 0))

    def record_offset(current, remote, offset_index):
        return place(current, stack_pairs(own_block, remote), offset_index)

    moving = passed_along(whole_block, "chan", -reach)

    def forward_turn(turn_index, loop_state):
        moving_block, current = loop_state
        current = record_offset(current, moving_block, 2 * reach - turn_index)
        moving_block = passed_along(moving_block, "chan", 1)
        return (moving_block, current)

    moving, result = lax.fori_loop(0, 2 * reach, forward_turn, (moving, result))
    result = record_offset(result, moving, 0)
    return result


def solution(mesh):
    placed = (
        P(("fibre", "chan"), "win", "tm"),
        P(),
        P(("fibre", "win")),
        P(("fibre", "chan"), None),
    )
    return jax.shard_map(
        shards,
        mesh=mesh,
        in_specs=placed,
        out_specs=P(None, "win", ("fibre", "chan", "tm"), None),
        check_vma=False,
    )
```

profile of v0, /device:TPU:1, one launch (start us, length us, event | category | flops | bytes accessed | tf_op | source)
XLA Modules:
  0.0 279.8 jit_solution(10900393456889094847)
XLA Ops:
  9.5 3.9 %collective-permute-start.1 = (bf16[8,8,64]{2,1,0:T(8,128)(2,1)S(1)}, bf16[8,8,64]{2,1,0:T(8,128)(2,1)S(1)}, u32[]{:S(2)}, u32[]{:S(2)}) collective-permute-start(bf16[8,8,64]{2,1,0:T(8,128)(2,1)S(1)} %slice.114), channel_id=1, source_target_pairs={{0,2},{1,3},{4,6},{5,7},{8,10},{9,11},{12,14},{13,15},{16,18},{17,... | collective-permute-start | bytes 24584 | tf_op jit(solution)/shard_map/ppermute | solution.py:19
  20.5 3.8 %all-to-all-done = bf16[8,8,2048]{2,1,0:T(8,128)(2,1)S(1)} async-done(((bf16[8,8,2048]{2,1,0:T(8,128)(2,1)}), bf16[8,8,2048]{2,1,0:T(8,128)(2,1)S(1)}, u32[]{:S(2)}, u32[]{:S(2)}) %all-to-all-start) | async-done | bytes 262176 | tf_op jit(solution)/shard_map/all_to_all | solution.py:157
  29.8 6.4 %all_gather.3 = bf16[8,8,2,2048]{3,1,2,0:T(8,128)(2,1)S(1)} all-gather(bf16[4,8,2,2048]{3,1,2,0:T(8,128)(2,1)S(1)} %pad_maximum_fusion.2), channel_id=1, replica_groups=mesh['fibre'=2,'chan'=4,'tm'=2,'win'=2] {'tm'}, dimensions={0}, use_global_device_ids=true | all-gather | bytes 786432 | tf_op jit(solution)/shard_map/all_gather | solution.py:158
  39.5 4.6 %copy.52 = bf16[4,8,2,2048]{1,0,3,2:T(4,128)(2,1)} copy(bf16[4,8,2,2048]{3,1,2,0:T(8,128)(2,1)S(1)} %pad_maximum_fusion.2) | data formatting | bytes 524288 | tf_op jit(solution)/shard_map/while | solution.py:188
  50.1 153.9 %while.18 = (s32[]{:T(128)}, bf16[8,8,2,2048]{3,1,2,0:T(8,128)(2,1)S(1)}, f32[3,4,4,3840]{3,2,1,0:T(4,128)}, bf16[4,8,2,2048]{1,0,3,2:T(4,128)(2,1)}, f32[3]{0:T...) while((s32[]{:T(128)}, ...), condition=%wide.region_4.5_spmd, body=%wide.region_2.4_spmd.sunk | while | flops 509673472 | bytes 53478252 | solution.py:188
  60.8 7.3 %copy.84 = bf16[8,8,2,2048]{1,0,3,2:T(8,128)(2,1)} copy(bf16[8,8,2,2048]{3,1,2,0:T(8,128)(2,1)S(1)} %copy.93) | data formatting | bytes 1048576 | tf_op jit(solution)/shard_map
  68.1 7.2 %fusion.291 = f32[2048,4,8]{2,1,0:T(4,128)} fusion(bf16[8,8,2,2048]{1,0,3,2:T(8,128)(2,1)} %copy.84, bf16[4,8,2,2048]{1,0,3,2:T(4,128)(2,1)} %get-tuple-element.264), kind=kOutput, calls=%fused_computation.2.clone.1 | convolution fusion | flops 1048576 | bytes 6553600 | tf_op jit(solution)/shard_map/while/body/eval_jaxpr/jwk,iwk->jik/dot_general | solution.py:107
  75.3 6.0 %fusion.288 = f32[2048,4,8]{2,1,0:T(4,128)} fusion(bf16[8,8,2,2048]{1,0,3,2:T(8,128)(2,1)S(1)} %copy-done, bf16[4,8,2,2048]{1,0,3,2:T(4,128)(2,1)} %get-tuple-element.264), kind=kOutput, calls=%fused_computation.3.clone.1 | convolution fusion | flops 1048576 | bytes 6553600 | tf_op jit(solution)/shard_map/while/body/eval_jaxpr/jwk,iwk->jik/dot_general | solution.py:107
  81.3 6.5 %fusion.289 = f32[2048,4,8]{2,1,0:T(4,128)} fusion(f32[2048,4,8]{2,1,0:T(4,128)} %fusion.288, bf16[8,8,2,2048]{1,0,3,2:T(8,128)(2,1)S(1)} %copy-done, bf16[4,8,2,2048]{1,0,3,2:T(4,128)(2,1)S(1)} %copy-done.1), kind=kOutput, calls=%fused_computation.6.clone.1 | convolution fusion | flops 1114112 | bytes 6815744 | tf_op jit(solution)/shard_map/while/body/eval_jaxpr/jwk,iwk->jik/dot_general | solution.py:107
  92.9 8.3 %fusion.292 = f32[2048,4,8]{2,1,0:T(4,128)} fusion(f32[2048,4,8]{2,1,0:T(4,128)} %fusion.291, bf16[8,8,2,2048]{1,0,3,2:T(8,128)(2,1)} %copy.84, bf16[4,8,2,2048]{1,0,3,2:T(4,128)(2,1)} %get-tuple-element.264), kind=kOutput, calls=%fused_computation.7.clone.1 | convolution fusion | flops 1114112 | bytes 10747904 | tf_op jit(solution)/shard_map/while/body/eval_jaxpr/jwk,iwk->jik/dot_general | solution.py:107
  110.7 20.8 %all-reduce.9.cloned.1.call-done = f32[8,4,3840]{2,1,0:T(4,128)} async-done(((f32[8,4,3840]{2,1,0:T(4,128)}), f32[8,4,3840]{2,1,0:T(4,128)}) %all-reduce.9.cloned.1.call-update) | async-done | bytes 491536 | tf_op jit(solution)/shard_map/while
  133.8 7.3 %copy.84 = bf16[8,8,2,2048]{1,0,3,2:T(8,128)(2,1)} copy(bf16[8,8,2,2048]{3,1,2,0:T(8,128)(2,1)S(1)} %copy.93) | data formatting | bytes 1048576 | tf_op jit(solution)/shard_map
  141.2 7.2 %fusion.291 = f32[2048,4,8]{2,1,0:T(4,128)} fusion(bf16[8,8,2,2048]{1,0,3,2:T(8,128)(2,1)} %copy.84, bf16[4,8,2,2048]{1,0,3,2:T(4,128)(2,1)} %get-tuple-element.264), kind=kOutput, calls=%fused_computation.2.clone.1 | convolution fusion | flops 1048576 | bytes 6553600 | tf_op jit(solution)/shard_map/while/body/eval_jaxpr/jwk,iwk->jik/dot_general | solution.py:107
  148.4 6.0 %fusion.288 = f32[2048,4,8]{2,1,0:T(4,128)} fusion(bf16[8,8,2,2048]{1,0,3,2:T(8,128)(2,1)S(1)} %copy-done, bf16[4,8,2,2048]{1,0,3,2:T(4,128)(2,1)} %get-tuple-element.264), kind=kOutput, calls=%fused_computation.3.clone.1 | convolution fusion | flops 1048576 | bytes 6553600 | tf_op jit(solution)/shard_map/while/body/eval_jaxpr/jwk,iwk->jik/dot_general | solution.py:107
  154.4 6.5 %fusion.289 = f32[2048,4,8]{2,1,0:T(4,128)} fusion(f32[2048,4,8]{2,1,0:T(4,128)} %fusion.288, bf16[8,8,2,2048]{1,0,3,2:T(8,128)(2,1)S(1)} %copy-done, bf16[4,8,2,2048]{1,0,3,2:T(4,128)(2,1)S(1)} %copy-done.1), kind=kOutput, calls=%fused_computation.6.clone.1 | convolution fusion | flops 1114112 | bytes 6815744 | tf_op jit(solution)/shard_map/while/body/eval_jaxpr/jwk,iwk->jik/dot_general | solution.py:107
  165.9 8.3 %fusion.292 = f32[2048,4,8]{2,1,0:T(4,128)} fusion(f32[2048,4,8]{2,1,0:T(4,128)} %fusion.291, bf16[8,8,2,2048]{1,0,3,2:T(8,128)(2,1)} %copy.84, bf16[4,8,2,2048]{1,0,3,2:T(4,128)(2,1)} %get-tuple-element.264), kind=kOutput, calls=%fused_computation.7.clone.1 | convolution fusion | flops 1114112 | bytes 10747904 | tf_op jit(solution)/shard_map/while/body/eval_jaxpr/jwk,iwk->jik/dot_general | solution.py:107
  185.3 16.5 %all-reduce.9.cloned.1.call-done = f32[8,4,3840]{2,1,0:T(4,128)} async-done(((f32[8,4,3840]{2,1,0:T(4,128)}), f32[8,4,3840]{2,1,0:T(4,128)}) %all-reduce.9.cloned.1.call-update) | async-done | bytes 491536 | tf_op jit(solution)/shard_map/while
  204.0 7.3 %copy.53 = bf16[8,8,2,2048]{1,0,3,2:T(8,128)(2,1)} copy(bf16[8,8,2,2048]{3,1,2,0:T(8,128)(2,1)S(1)} %get-tuple-element.168) | data formatting | bytes 1048576 | tf_op jit(solution)/shard_map/while | solution.py:188
  211.3 7.2 %fusion.92 = f32[2048,4,8]{2,1,0:T(4,128)} fusion(bf16[4,8,2048]{1,0,2:T(4,128)(2,1)} %bitcast.235, bf16[8,8,2,2048]{1,0,3,2:T(8,128)(2,1)} %copy.53), kind=kOutput, calls=%fused_computation.104 | convolution fusion | flops 1048576 | bytes 6553600 | tf_op jit(solution)/shard_map/jwk,iwk->jik/dot_general | solution.py:107
  218.6 4.2 %fusion.93 = f32[2048,4,8]{2,1,0:T(4,128)} fusion(bf16[4,8,2048]{1,0,2:T(4,128)(2,1)S(1)} %bitcast.233, bf16[8,8,2,2048]{1,0,3,2:T(8,128)(2,1)S(1)} %copy-done.2), kind=kOutput, calls=%fused_computation.105 | convolution fusion | flops 1048576 | bytes 6553600 | tf_op jit(solution)/shard_map/jwk,iwk->jik/dot_general | solution.py:107
  222.8 6.4 %fusion.94 = f32[2048,4,8]{2,1,0:T(4,128)} fusion(f32[2048,4,8]{2,1,0:T(4,128)} %fusion.93, bf16[4,8,2048]{1,0,2:T(4,128)(2,1)S(1)} %bitcast.236, bf16[8,8,2,2048]{1,0,3,2:T(8,128)(2,1)S(1)} %copy-done.2), kind=kOutput, calls=%fused_computation.106 | convolution fusion | flops 1114112 | bytes 6815744 | tf_op jit(solution)/shard_map/jwk,iwk->jik/dot_general | solution.py:107
  235.0 7.7 %fusion.95 = f32[2048,4,8]{2,1,0:T(4,128)} fusion(f32[2048,4,8]{2,1,0:T(4,128)} %fusion.92, bf16[4,8,2048]{1,0,2:T(4,128)(2,1)S(1)} %bitcast.234, bf16[8,8,2,2048]{1,0,3,2:T(8,128)(2,1)} %copy.53), kind=kOutput, calls=%fused_computation.107 | convolution fusion | flops 1114112 | bytes 8781824 | tf_op jit(solution)/shard_map/jwk,iwk->jik/dot_general | solution.py:107
  242.8 3.9 %copy.60 = f32[8,4,32,64]{3,2,1,0:T(8,128)S(1)} copy(f32[8,4,32,64]{0,1,3,2:T(4,128)} %bitcast.237) | data formatting | bytes 524288 | tf_op jit(solution)/shard_map/squeeze | solution.py:130
  251.8 18.4 %all-reduce.7.cloned.1.call-done = f32[8,4,3840]{2,1,0:T(4,128)} async-done(((f32[8,4,3840]{2,1,0:T(4,128)}), f32[8,4,3840]{2,1,0:T(4,128)}) %all-reduce.7.cloned.1.call-update) | async-done | bytes 491536
  (114 shorter events, 69.6 us)
Async XLA Ops:
  9.5 5.8 %collective-permute-start.1 = (bf16[8,8,64]{2,1,0:T(8,128)(2,1)S(1)}, bf16[8,8,64]{2,1,0:T(8,128)(2,1)S(1)}, u32[]{:S(2)}, u32[]{:S(2)}) collective-permute-start(bf16[8,8,64]{2,1,0:T(8,128)(2,1)S(1)} %slice.114), channel_id=1, source_target_pairs={{0,2},{1,3},{4,6},{5,7},{8,10},{9,11},{12,14},{13,15},{16,18},{17,... | collective-permute-start | bytes 24584 | tf_op jit(solution)/shard_map/ppermute | solution.py:19
  16.9 7.5 %all-to-all-start = ((bf16[8,8,2048]{2,1,0:T(8,128)(2,1)}), bf16[8,8,2048]{2,1,0:T(8,128)(2,1)S(1)}, u32[]{:S(2)}, u32[]{:S(2)}) async-start(bf16[8,8,2048]{2,1,0:T(8,128)(2,1)} %convert_element_type.148), calls=%async_computation | async-start | bytes 524288 | tf_op jit(solution)/shard_map/all_to_all | solution.py:157
  27.1 12.4 %copy-start.6 = (s32[1,3]{1,0:T(1,128)S(1)}, s32[1,3]{1,0:T(1,128)}, u32[]{:S(2)}) copy-start(s32[1,3]{1,0:T(1,128)} %param.9) | copy-start | bytes 40
  36.1 13.0 %collective-permute-start.2 = (bf16[8,8,2,2048]{3,1,2,0:T(8,128)(2,1)S(1)}, bf16[8,8,2,2048]{3,1,2,0:T(8,128)(2,1)S(1)}, u32[]{:S(2)}, u32[]{:S(2)}) collective-permute-start(bf16[8,8,2,2048]{3,1,2,0:T(8,128)(2,1)S(1)} %all_gather.3), channel_id=1, source_target_pairs={{0,12},{4,0},{8,4},{12,8},{1,13},{5,1},{9,5},{13,9},{2,14},{6,2},{... | collective-permute-start | bytes 1572872 | tf_op jit(solution)/shard_map/ppermute | solution.py:24
  39.5 10.6 %copy-start.7 = (u32[32]{0:T(128)S(1)}, u32[32]{0:T(128)}, u32[]{:S(2)}) copy-start(u32[32]{0:T(128)} %constant.236) | copy-start | bytes 388
  60.7 70.8 %all-reduce.9.cloned.1.call-start = ((), (), s32[]{:S(2)}) async-start(), calls=%async_computation.2 | async-start | bytes 983040 | tf_op jit(solution)/shard_map/while
  68.1 7.2 %copy-start = (bf16[8,8,2,2048]{1,0,3,2:T(8,128)(2,1)S(1)}, bf16[8,8,2,2048]{1,0,3,2:T(8,128)(2,1)}, u32[]{:S(2)}) copy-start(bf16[8,8,2,2048]{1,0,3,2:T(8,128)(2,1)} %copy.84) | copy-start | bytes 1572868 | tf_op jit(solution)/shard_map/while
  75.3 6.0 %copy-start.1 = (bf16[4,8,2,2048]{1,0,3,2:T(4,128)(2,1)S(1)}, bf16[4,8,2,2048]{1,0,3,2:T(4,128)(2,1)}, u32[]{:S(2)}) copy-start(bf16[4,8,2,2048]{1,0,3,2:T(4,128)(2,1)} %get-tuple-element.264) | copy-start | bytes 786436 | tf_op jit(solution)/shard_map/while
  108.7 25.1 %collective-permute-start = (bf16[8,8,2,2048]{3,1,2,0:T(8,128)(2,1)S(1)}, bf16[8,8,2,2048]{3,1,2,0:T(8,128)(2,1)S(1)}, u32[]{:S(2)}, u32[]{:S(2)}) collective-permute-start(bf16[8,8,2,2048]{3,1,2,0:T(8,128)(2,1)S(1)} %copy.93), channel_id=1, source_target_pairs={{0,4},{4,8},{8,12},{12,0},{1,5},{5,9},{9,13},{13,1},{2,6},{6,10},{... | collective-permute-start | bytes 1572872 | tf_op jit(solution)/shard_map/while/body/eval_jaxpr/ppermute | solution.py:24
  133.8 68.0 %all-reduce.9.cloned.1.call-start = ((), (), s32[]{:S(2)}) async-start(), calls=%async_computation.2 | async-start | bytes 983040 | tf_op jit(solution)/shard_map/while
  141.2 7.2 %copy-start = (bf16[8,8,2,2048]{1,0,3,2:T(8,128)(2,1)S(1)}, bf16[8,8,2,2048]{1,0,3,2:T(8,128)(2,1)}, u32[]{:S(2)}) copy-start(bf16[8,8,2,2048]{1,0,3,2:T(8,128)(2,1)} %copy.84) | copy-start | bytes 1572868 | tf_op jit(solution)/shard_map/while
  148.4 6.0 %copy-start.1 = (bf16[4,8,2,2048]{1,0,3,2:T(4,128)(2,1)S(1)}, bf16[4,8,2,2048]{1,0,3,2:T(4,128)(2,1)}, u32[]{:S(2)}) copy-start(bf16[4,8,2,2048]{1,0,3,2:T(4,128)(2,1)} %get-tuple-element.264) | copy-start | bytes 786436 | tf_op jit(solution)/shard_map/while
  181.7 22.2 %collective-permute-start = (bf16[8,8,2,2048]{3,1,2,0:T(8,128)(2,1)S(1)}, bf16[8,8,2,2048]{3,1,2,0:T(8,128)(2,1)S(1)}, u32[]{:S(2)}, u32[]{:S(2)}) collective-permute-start(bf16[8,8,2,2048]{3,1,2,0:T(8,128)(2,1)S(1)} %copy.93), channel_id=1, source_target_pairs={{0,4},{4,8},{8,12},{12,0},{1,5},{5,9},{9,13},{13,1},{2,6},{6,10},{... | collective-permute-start | bytes 1572872 | tf_op jit(solution)/shard_map/while/body/eval_jaxpr/ppermute | solution.py:24
  204.0 66.2 %all-reduce.7.cloned.1.call-start = ((), (), s32[]{:S(2)}) async-start(), calls=%async_computation.1 | async-start | bytes 983040
  211.3 7.3 %copy-start.2 = (bf16[8,8,2,2048]{1,0,3,2:T(8,128)(2,1)S(1)}, bf16[8,8,2,2048]{1,0,3,2:T(8,128)(2,1)}, u32[]{:S(2)}) copy-start(bf16[8,8,2,2048]{1,0,3,2:T(8,128)(2,1)} %copy.53) | copy-start | bytes 1572868
  211.3 7.3 %copy-start.3 = (bf16[4,8,32,64]{1,0,3,2:T(4,128)(2,1)S(1)}, bf16[4,8,32,64]{1,0,3,2:T(4,128)(2,1)}, u32[]{:S(2)}) copy-start(bf16[4,8,32,64]{1,0,3,2:T(4,128)(2,1)} %copy.75) | copy-start | bytes 393220
  218.6 4.2 %copy-start.4 = (bf16[4,8,32,64]{1,0,3,2:T(4,128)(2,1)S(1)}, bf16[4,8,32,64]{1,0,3,2:T(4,128)(2,1)}, u32[]{:S(2)}) copy-start(bf16[4,8,32,64]{1,0,3,2:T(4,128)(2,1)} %copy.74) | copy-start | bytes 393220
  242.8 3.9 %copy-start.5 = (f32[8,4,32,128]{3,2,1,0:T(8,128)S(1)}, f32[8,4,32,128]{3,2,1,0:T(8,128)}, u32[]{:S(2)}) copy-start(f32[8,4,32,128]{3,2,1,0:T(8,128)} %fusion.134) | copy-start | bytes 1572868
Sparse Core Ops, SparseCore 0:
  108.8 22.6 all-reduce.8
  181.9 19.8 all-reduce.8
Sparse Core Ops, SparseCore 1:
  250.7 19.5 all-reduce.6
where the time goes:
time: 282 us; the launch traced here: 280 us
  matrix products  100 us (35%)
  local copies, waits for them, and re-layouts  61.5 us (22%)
  waiting for transfers between devices  59.6 us (21%)
  between operations  16.1 us (6%)
  starting transfers between devices  12.4 us (4%)
  loops' own time  12.2 us (4%)
  other arithmetic  11.6 us (4%)
  blocking collectives  6.38 us (2%)
    dot_general x12, matrix products, contract(): jnp.einsum('jwk,iwk->jik', remote_part, own_part, preferred_element_type=...  81.6 us
    while x4, waiting for transfers between devices  37.3 us
    unnamed x2, waiting for transfers between devices  18.5 us
    dot_general x25, matrix products, product(): return jnp.einsum(pattern, first_arg, second_arg, precision=HIGHEST)  17.7 us
    another operation x4, local copies, waits for them, and re-layouts  14.8 us
    another operation x1, loops' own time, shards(): moving, result = lax.fori_loop(0, 2 * reach, forward_turn, (moving, result))  12.2 us
    while x2, local copies, waits for them, and re-layouts, shards(): moving, result = lax.fori_loop(0, 2 * reach, forward_turn, (moving, result))  11.9 us
    squeeze x3, local copies, waits for them, and re-layouts, lag_domain(): grid_im = spectral_grid[:, :, 1]  11 us
  transfers between devices with their start and end apart: 8, of which 4 were waited for; matrix products, arithmetic and copies ran while one was open for 7% of the time, Pallas kernels for 0%

commit v1 on v0

v1 whole, which is shorter than its diff:
```python
import functools
import math

import jax
import jax.numpy as jnp
import numpy as np
from jax import lax
from jax.experimental import pallas as pl
from jax.experimental.pallas import tpu as pltpu
from jax.sharding import PartitionSpec as P

MAXLAG = 1920
BAND = 64
EPSILON = 1e-06

LANES = 128
ROWS = 32
RESIDUES = ROWS // 2 + 1
BLOCK = 4 * LANES
SUB = 8
F32 = jnp.float32
BF16 = jnp.bfloat16
VMEM = pltpu.VMEM


def halves(table):
    high = table.astype(np.float32).astype(jnp.bfloat16)
    low = (table - high.astype(np.float64)).astype(np.float32).astype(jnp.bfloat16)
    return np.stack([high, low])


def forward_table():
    angle = 2.0 * np.pi / LANES * (np.outer(np.arange(LANES), np.arange(LANES)) % LANES)
    cos, sin = np.cos(angle), np.sin(angle)
    return halves(np.block([[cos, -sin], [sin, cos]]))


def inverse_table():
    angle = 2.0 * np.pi / LANES * (np.outer(np.arange(LANES), np.arange(LANES)) % LANES)
    cos, sin = np.cos(angle), np.sin(angle)
    return halves(np.block([[cos, sin], [-sin, cos]]))


def twist_table():
    angle = 2.0 * np.pi / (ROWS * LANES) * np.outer(np.arange(RESIDUES), np.arange(LANES))
    both = np.stack([np.cos(angle), np.sin(angle)]).astype(np.float32)
    return np.ascontiguousarray(np.broadcast_to(both[:, :, None, :], (2, RESIDUES, SUB, LANES)))


def band_table():
    place = np.arange(LANES)
    place = np.minimum(place, LANES - 1 - place)
    band = place // (BAND // ROWS)
    return (band[:, None] == band[None, :]).astype(np.float32).astype(jnp.bfloat16)


def turn(value, k, n):
    real, imag = value
    c, s = math.cos(2 * math.pi * k / n), math.sin(2 * math.pi * k / n)
    if 8 * k == n:
        return ((real + imag) * c, (imag - real) * c)
    if 8 * k == 3 * n:
        return ((imag - real) * s, -(real + imag) * s)
    return (real * c + imag * s, imag * c - real * s)


def real_transform(x):
    n = len(x)
    if n == 2:
        return [(x[0] + x[1], None), (x[0] - x[1], None)]
    even, odd = real_transform(x[0::2]), real_transform(x[1::2])
    out = [None] * (n // 2 + 1)
    out[0] = (even[0][0] + odd[0][0], None)
    out[n // 2] = (even[0][0] - odd[0][0], None)
    for k in range(1, n // 4):
        er, ei = even[k]
        tr, ti = turn(odd[k], k, n)
        out[k] = (er + tr, ei + ti)
        out[n // 2 - k] = (er - tr, ti - ei)
    out[n // 4] = (even[n // 4][0], -odd[n // 4][0])
    return out


def real_inverse(x):
    n = 2 * (len(x) - 1)
    if n == 2:
        return [x[0][0] + x[1][0], x[0][0] - x[1][0]]
    even, odd = [None] * (n // 4 + 1), [None] * (n // 4 + 1)
    even[0] = (x[0][0] + x[n // 2][0], None)
    odd[0] = (x[0][0] - x[n // 2][0], None)
    for k in range(1, n // 4):
        ar, ai = x[k]
        br, bi = x[n // 2 - k]
        even[k] = (ar + br, ai - bi)
        dr, di = turn((ar - br, -(ai + bi)), k, n)
        odd[k] = (dr, -di)
    even[n // 4] = (2.0 * x[n // 4][0], None)
    odd[n // 4] = (-2.0 * x[n // 4][1], None)
    a, b = real_inverse(even), real_inverse(odd)
    return [v for pair in zip(a, b) for v in pair]


def split(value):
    high = value.astype(BF16)
    return high, (value - high.astype(F32)).astype(BF16)


def three_pass(high, low, table_ref):
    def dot(a, b):
        return jnp.dot(a, b, preferred_element_type=F32)

    return dot(high, table_ref[0]) + dot(low, table_ref[0]) + dot(high, table_ref[1])


def decimate_kernel(place_ref, end_ref, base_ref, rec_ref, keep_ref, send_ref, lhs_ref):
    channels, windows, length = rec_ref.shape
    half = channels // 2
    rows = half * windows
    blocks = length // BLOCK
    tap_table = pltpu.roll(
        jnp.broadcast_to(base_ref[...], (LANES, BLOCK + LANES)), 0, 1, stride=4, stride_axis=0
    ).astype(BF16)
    row = lax.broadcasted_iota(jnp.int32, (windows, BLOCK), 0)
    lane = lax.broadcasted_iota(jnp.int32, (windows, BLOCK), 1)
    end = jnp.zeros((windows, BLOCK), jnp.int32)
    for w in range(windows):
        end = jnp.where(row == w, end_ref[w], end)
    end = end - place_ref[0] * length - lane
    for h, out_ref in ((0, keep_ref), (1, send_ref)):
        side = place_ref[1] if h == 0 else 1 - place_ref[1]
        lhs_ref[h, 0, :, 0:LANES] = jnp.zeros((rows, LANES), BF16)
        lhs_ref[h, blocks, :, LANES:] = jnp.zeros((rows, BLOCK), BF16)
        for b in range(blocks):
            x = rec_ref[pl.ds(side * half, half), :, b * BLOCK : (b + 1) * BLOCK].astype(F32)
            x = jnp.where((end > b * BLOCK)[None], x, 0.0)
            x = x.reshape(rows, BLOCK).astype(BF16)
            lhs_ref[h, b, :, LANES:] = x
            lhs_ref[h, b + 1, :, 0:LANES] = x[:, BLOCK - LANES :]
        out = lax.dot_general(
            lhs_ref[h].reshape((blocks + 1) * rows, BLOCK + LANES),
            tap_table,
            (((1,), (1,)), ((), ())),
            preferred_element_type=F32,
        )
        out_ref[...] = out.reshape(blocks + 1, half, windows, LANES).astype(BF16)


def decimate(records, filter_taps, segment_end, place):
    channels, windows, length = records.shape
    taps = filter_taps.shape[0]
    reverse = filter_taps.astype(F32)[::-1]
    base = jnp.pad(reverse, (LANES + 4 - taps, BLOCK - 4)).reshape(1, BLOCK + LANES)
    blocks = length // BLOCK
    piece = jax.ShapeDtypeStruct((blocks + 1, channels // 2, windows, LANES), BF16)
    return pl.pallas_call(
        decimate_kernel,
        out_shape=(piece, piece),
        in_specs=[
            pl.BlockSpec(memory_space=pltpu.SMEM),
            pl.BlockSpec(memory_space=pltpu.SMEM),
            pl.BlockSpec(memory_space=VMEM),
            pl.BlockSpec(memory_space=VMEM),
        ],
        out_specs=(pl.BlockSpec(memory_space=VMEM),) * 2,
        scratch_shapes=[VMEM((2, blocks + 1, channels // 2 * windows, BLOCK + LANES), BF16)],
        compiler_params=pltpu.CompilerParams(vmem_limit_bytes=24 << 20),
        cost_estimate=pl.CostEstimate(
            flops=2 * records.size // 4 * BLOCK, bytes_accessed=3 * records.size, transcendentals=0
        ),
        name="decimate",
    )(place, segment_end, base, records)


def spectra(segments, flags, tables, work, store):
    twist_ref, dft_ref, band_ref = tables
    high_ref, low_ref, spec_ref, power_ref = work
    depth, groups = segments[0].shape[0] - 1, segments[0].shape[1]

    def first(g, carry):
        x = []
        for s in range(len(segments)):
            for r in range(depth):
                value = segments[s][r, g].astype(F32)
                if r == 0:
                    value = value + segments[s - 1][depth, g].astype(F32) * flags[s]
                x.append(value)
        for q, (real, imag) in enumerate(real_transform(x)):
            if q == 0:
                turned = (real, jnp.zeros_like(real))
            else:
                cos, sin = twist_ref[0, q], twist_ref[1, q]
                if imag is None:
                    turned = (real * cos, -(real * sin))
                else:
                    turned = (real * cos + imag * sin, imag * cos - real * sin)
            for part in range(2):
                high, low = split(turned[part])
                high_ref[g, q, :, part * LANES : (part + 1) * LANES] = high
                low_ref[g, q, :, part * LANES : (part + 1) * LANES] = low
        return carry

    lax.fori_loop(0, groups, first, 0)
    count = groups * RESIDUES * SUB
    spec = three_pass(
        high_ref[...].reshape(count, 2 * LANES), low_ref[...].reshape(count, 2 * LANES), dft_ref
    )
    spec_ref[...] = spec.reshape(groups, RESIDUES, SUB, 2 * LANES)
    lower = (lax.broadcasted_iota(jnp.int32, (SUB, LANES), 1) < LANES // 2).astype(F32)

    def powers(g, carry):
        ends = inner = None
        for q in range(RESIDUES):
            real, imag = spec_ref[g, q, :, :LANES], spec_ref[g, q, :, LANES:]
            power = real * real + imag * imag
            if q in (0, RESIDUES - 1):
                ends = power if ends is None else ends + power
            else:
                inner = power if inner is None else inner + power
        power_ref[g] = inner + ends * lower
        return carry

    lax.fori_loop(0, groups, powers, 0)
    high, low = split(power_ref[...].reshape(groups * SUB, LANES))
    energy = jnp.dot(high, band_ref[...], preferred_element_type=F32) + jnp.dot(
        low, band_ref[...], preferred_element_type=F32
    )
    power_ref[...] = lax.rsqrt(energy * (1.0 / BAND) + EPSILON).reshape(groups, SUB, LANES)
    lane = lax.broadcasted_iota(jnp.int32, (SUB, LANES), 1)
    nonzero = (lane > 0).astype(F32)

    def whiten(g, carry):
        scale = power_ref[g]
        for q in range(RESIDUES):
            factor = scale
            if q == 0:
                factor = scale * lower * nonzero
            elif q == RESIDUES - 1:
                factor = scale * lower
            for part in range(2):
                value = spec_ref[g, q, :, part * LANES : (part + 1) * LANES]
                store(part, g, q, (value * factor).astype(BF16))
        return carry

    lax.fori_loop(0, groups, whiten, 0)


def gather_rows(values):
    row = lax.broadcasted_iota(jnp.int32, (SUB, LANES), 0)
    step = SUB // 2
    while step:
        lower = (row % (2 * step)) < step
        values = [
            jnp.where(lower, a, b) + pltpu.roll(jnp.where(lower, b, a), step, 0)
            if step == SUB // 2
            else jnp.where(lower, a, b) + swap(jnp.where(lower, b, a), step, lower)
            for a, b in zip(values[:step], values[step:])
        ]
        step //= 2
    return values[0]


def swap(value, step, lower):
    return jnp.where(lower, pltpu.roll(value, SUB - step, 0), pltpu.roll(value, step, 0))


def correlate(own_load, remote_load, chunks, owned, remotes, tables, work, weight, lag_ref):
    twist_ref, inverse_ref = tables
    high_ref, low_ref, sum_ref = work
    pair_groups = remotes * owned // SUB

    def cross(q, carry):
        own = [[[own_load(c, p, i, q).astype(F32) for p in range(2)] for i in range(owned)] for c in range(chunks)]
        for group in range(pair_groups):
            real, imag = [], []
            for pair in range(group * SUB, (group + 1) * SUB):
                j, i = pair // owned, pair % owned
                re = im = None
                for c in range(chunks):
                    ar, ai = own[c][i]
                    br, bi = (remote_load(c, p, j, q).astype(F32) for p in range(2))
                    r = ar * br + ai * bi
                    m = ai * br - ar * bi
                    re = r if re is None else re + r
                    im = m if im is None else im + m
                real.append(re)
                imag.append(im)
            for part, values in enumerate((real, imag)):
                high, low = split(gather_rows(values))
                high_ref[group, q, :, part * LANES : (part + 1) * LANES] = high
                low_ref[group, q, :, part * LANES : (part + 1) * LANES] = low
        return carry

    lax.fori_loop(0, RESIDUES, cross, 0)
    count = pair_groups * RESIDUES * SUB
    total = three_pass(
        high_ref[...].reshape(count, 2 * LANES), low_ref[...].reshape(count, 2 * LANES), inverse_ref
    )
    sum_ref[...] = total.reshape(pair_groups, RESIDUES, SUB, 2 * LANES)
    lag_rows = MAXLAG // LANES
    per = SUB // owned

    def lags(group, carry):
        x = []
        for q in range(RESIDUES):
            real, imag = sum_ref[group, q, :, :LANES], sum_ref[group, q, :, LANES:]
            if q == 0:
                x.append((real, None))
                continue
            cos, sin = twist_ref[0, q], twist_ref[1, q]
            turned = real * cos - imag * sin
            if q == RESIDUES - 1:
                x.append((turned, None))
            else:
                x.append((0.5 * turned, 0.5 * (real * sin + imag * cos)))
        out = real_inverse(x)
        for place, a in enumerate((*range(ROWS - lag_rows, ROWS), *range(lag_rows))):
            value = out[a] * weight
            for j in range(per):
                lag_ref[group * per + j, :, place * LANES : (place + 1) * LANES] = value[
                    j * owned : (j + 1) * owned
                ]
        return carry

    lax.fori_loop(0, pair_groups, lags, 0)


def write_out(lag_ref, out_ref, offset, sem):
    copy = pltpu.make_async_copy(lag_ref, out_ref.at[offset], sem)
    copy.start()
    copy.wait()


def flags_of(place_ref, span):
    t = place_ref[0]
    return [((t + s) % span != 0).astype(F32) for s in range(span)]


def whiten_kernel(span, place_ref, *refs):
    pieces = refs[: 2 * span]
    twist_ref, dft_ref, band_ref, white_ref = refs[2 * span : 2 * span + 4]
    work = refs[2 * span + 4 :]
    flags = flags_of(place_ref, span)
    for c in range(2):

        def store(part, g, q, value, c=c):
            white_ref[c, part, g, q] = value

        spectra(pieces[c * span : (c + 1) * span], flags, (twist_ref, dft_ref, band_ref), work, store)


def own_pairs_kernel(
    owned, offset, scale, place_ref, mask_ref, white_ref, other_ref, twist_ref, inverse_ref,
    own_ref, out_ref, high_ref, low_ref, sum_ref, lag_ref, sem,
):
    groups = white_ref.shape[2]
    first = place_ref[0] * owned
    inside = lax.rem(first, groups)
    here = lax.div(first, groups) == place_ref[1]

    @pl.when(here)
    def _():
        own_ref[...] = white_ref[:, :, pl.ds(inside, owned)]

    @pl.when(jnp.logical_not(here))
    def _():
        for c in range(2):
            own_ref[c] = other_ref[1 - c, :, pl.ds(inside, owned)]

    correlate(
        lambda c, p, i, q: own_ref[c, p, i, q],
        lambda c, p, j, q: white_ref[c, p, j, q],
        2, owned, groups, (twist_ref, inverse_ref), (high_ref, low_ref, sum_ref),
        mask_ref[0, offset].astype(F32) * scale, lag_ref,
    )
    write_out(lag_ref, out_ref, offset, sem)


def far_pairs_kernel(span, owned, offset, scale, place_ref, mask_ref, *refs):
    pieces = refs[: 2 * span]
    own_ref, twist_ref, dft_ref, band_ref, inverse_ref, _, out_ref = refs[2 * span : 2 * span + 7]
    (
        white_ref, zhigh_ref, zlow_ref, spec_ref, power_ref, high_ref, low_ref, sum_ref, lag_ref, sem,
    ) = refs[2 * span + 7 :]
    flags = flags_of(place_ref, span)
    groups = white_ref.shape[2]
    for c in range(2):

        def store(part, g, q, value, c=c):
            white_ref[c, part, g, q] = value

        spectra(
            pieces[c * span : (c + 1) * span], flags, (twist_ref, dft_ref, band_ref),
            (zhigh_ref, zlow_ref, spec_ref, power_ref), store,
        )
    correlate(
        lambda c, p, i, q: own_ref[c, p, i, q],
        lambda c, p, j, q: white_ref[c, p, j, q],
        2, owned, groups, (twist_ref, inverse_ref), (high_ref, low_ref, sum_ref),
        mask_ref[0, offset].astype(F32) * scale, lag_ref,
    )
    write_out(lag_ref, out_ref, offset, sem)


def spectra_work(groups):
    return [
        VMEM((groups, RESIDUES, SUB, 2 * LANES), BF16),
        VMEM((groups, RESIDUES, SUB, 2 * LANES), BF16),
        VMEM((groups, RESIDUES, SUB, 2 * LANES), F32),
        VMEM((groups, SUB, LANES), F32),
    ]


def lag_work(groups, owned):
    pair_groups = groups * owned // SUB
    return [
        VMEM((pair_groups, RESIDUES, SUB, 2 * LANES), BF16),
        VMEM((pair_groups, RESIDUES, SUB, 2 * LANES), BF16),
        VMEM((pair_groups, RESIDUES, SUB, 2 * LANES), F32),
        VMEM((groups, owned, 2 * MAXLAG), F32),
        pltpu.SemaphoreType.DMA,
    ]


def params(microseconds):
    return dict(
        compiler_params=pltpu.CompilerParams(vmem_limit_bytes=16 << 20),
        cost_estimate=pl.CostEstimate(
            flops=int(microseconds * 1e9), bytes_accessed=1 << 20, transcendentals=0
        ),
    )


def shards(records, filter_taps, segment_end, pair_mask):
    span = lax.axis_size("tm")
    owned = records.shape[0] // span
    groups = records.shape[0] // 2
    reach = (pair_mask.shape[1] - 1) // 2
    windows = 2 * records.shape[1]
    scale = 1.0 / math.sqrt(windows * ROWS * LANES // 2)
    place = jnp.stack([lax.axis_index("tm"), lax.axis_index("win")]).astype(jnp.int32)
    twist, dft, inverse, band = (
        jnp.asarray(t) for t in (twist_table(), forward_table(), inverse_table(), band_table())
    )
    smem, vmem = pl.BlockSpec(memory_space=pltpu.SMEM), pl.BlockSpec(memory_space=VMEM)
    anywhere = pl.BlockSpec(memory_space=pl.ANY)

    def permute(array, axis, by):
        count = lax.axis_size(axis)
        return lax.ppermute(array, axis, [(i, (i + by) % count) for i in range(count)])

    def segments(chunk):
        return [chunk] + [permute(chunk, "tm", -s) for s in range(1, span)]

    keep, send = decimate(records, filter_taps, segment_end, place)
    chunks = [keep, permute(send, "win", 1)]
    up = down = chunks
    moved = []
    for _ in range(reach):
        up = [permute(chunk, "chan", 1) for chunk in up]
        down = [permute(chunk, "chan", -1) for chunk in down]
        moved.append((up, down))
    white = pl.pallas_call(
        functools.partial(whiten_kernel, span),
        out_shape=jax.ShapeDtypeStruct((2, 2, groups, RESIDUES, SUB, LANES), BF16),
        in_specs=[smem] + [vmem] * (2 * span + 3),
        out_specs=vmem,
        scratch_shapes=spectra_work(groups),
        name="whiten",
        **params(3),
    )(place, *segments(chunks[0]), *segments(chunks[1]), twist, dft, band)
    other = permute(white, "win", 1)
    own, out = pl.pallas_call(
        functools.partial(own_pairs_kernel, owned, reach, scale),
        out_shape=(
            jax.ShapeDtypeStruct((2, 2, owned, RESIDUES, SUB, LANES), BF16),
            jax.ShapeDtypeStruct((2 * reach + 1, groups, owned, 2 * MAXLAG), F32),
        ),
        in_specs=[smem, smem] + [vmem] * 4,
        out_specs=(vmem, anywhere),
        scratch_shapes=lag_work(groups, owned),
        name="own_pairs",
        **params(2),
    )(place, pair_mask, white, other, twist, inverse)
    for step, sides in enumerate(moved):
        for side, far in zip((-1, 1), sides):
            offset = reach + side * (step + 1)
            out = pl.pallas_call(
                functools.partial(far_pairs_kernel, span, owned, offset, scale),
                out_shape=jax.ShapeDtypeStruct(out.shape, out.dtype),
                in_specs=[smem, smem] + [vmem] * (2 * span + 5) + [anywhere],
                out_specs=anywhere,
                scratch_shapes=[VMEM((2, 2, groups, RESIDUES, SUB, LANES), BF16)]
                + spectra_work(groups)
                + lag_work(groups, owned),
                input_output_aliases={2 * span + 7: 0},
                name="far_pairs",
                **params(4),
            )(place, pair_mask, *segments(far[0]), *segments(far[1]), own, twist, dft, band, inverse, out)
    return out


def solution(mesh):
    placed = (
        P(("fibre", "chan"), "win", "tm"),
        P(),
        P(("fibre", "win")),
        P(("fibre", "chan"), None),
    )
    return jax.shard_map(
        shards,
        mesh=mesh,
        in_specs=placed,
        out_specs=P(None, "win", ("fibre", "chan", "tm"), None),
        check_vma=False,
    )
```

time: 282 us -> 48.6 us (0.17)
  the two profiles are of different devices: /device:TPU:1 before, /device:TPU:0 now
where the time goes in v1:
time: 48.6 us; the launch traced here: 48.5 us
  starting transfers between devices  18.7 us (38%)
  Pallas kernels  17.1 us (35%)
  waiting for transfers between devices  9.84 us (20%)
  local copies, waits for them, and re-layouts  2.66 us (5%)
    ppermute x12, starting transfers between devices, permute(): lax.ppermute(array, axis, [(i, (i + by) % count) for i in range(count)])  18.7 us
    pallas_call x2, Pallas kernels, shards(): pl.pallas_call(functools.partial(far_pairs_kernel, span, owned, offset, s...  10.2 us
    ppermute x12, waiting for transfers between devices, permute(): lax.ppermute(array, axis, [(i, (i + by) % count) for i in range(count)])  9.84 us
    pallas_call x1, Pallas kernels, shards(): pl.pallas_call(functools.partial(whiten_kernel, span), out_shape=jax.Shap...  2.89 us
    pallas_call x1, Pallas kernels, shards(): pl.pallas_call(functools.partial(own_pairs_kernel, owned, reach, scale),...  2.83 us
    unnamed x16, local copies, waits for them, and re-layouts  2.48 us
    pallas_call x1, Pallas kernels, decimate(): pl.pallas_call(decimate_kernel, out_shape=(piece, piece), in_specs=[pl.Bl...  1.17 us
  transfers between devices with their start and end apart: 12, of which 6 were waited for; matrix products, arithmetic and copies ran while one was open for 0% of the time, Pallas kernels for 16%

profile of v1, /device:TPU:0, one launch (start us, length us, event | category | flops | bytes accessed | tf_op | source)
XLA Modules:
  0.0 48.5 jit_solution(9258298853425753813)
XLA Ops:
  0.0 0.7 %copy-done.7 = bf16[64]{0:T(256)(128)(2,1)S(1)} copy-done((bf16[64]{0:T(256)(128)(2,1)S(1)}, bf16[64]{0:T(256)(128)(2,1)}, u32[]{:S(2)}) %copy-start.7) | copy-done | bytes 152
  0.9 0.6 %copy-done.1 = s32[8]{0:T(128)S(1)} copy-done((s32[8]{0:T(128)S(1)}, s32[8]{0:T(128)}, u32[]{:S(2)}) %copy-start.1) | copy-done | bytes 56
  1.5 1.2 %copy-done = bf16[8,8,8192]{2,1,0:T(8,128)(2,1)S(1)} copy-done((bf16[8,8,8192]{2,1,0:T(8,128)(2,1)S(1)}, bf16[8,8,8192]{2,1,0:T(8,128)(2,1)}, u32[]{:S(2)}) %copy-start) | copy-done | bytes 1048600
  2.7 1.2 %decimate.1 = (bf16[17,4,8,128]{3,2,1,0:T(8,128)(2,1)S(1)}, bf16[17,4,8,128]{3,2,1,0:T(8,128)(2,1)S(1)}) custom-call(s32[2]{0:T(128)S(1)} %pad_add_fusion.place_ref, s32[8]{0:T(128)S(1)} %copy-done.1, f32[1,640]{1,0:T(1,128)S(1)} %reshape.3.base_ref, bf16[8,8,8192]{2,1,0:T(8,128)(2,1)S(1)} %copy-done), custom_call_target="tpu_custom_call" | custom-call | flops 134217728 | bytes 1572864 | tf_op jit(solution)/shard_map/decimate/pallas_call | solution.py:155
  3.9 0.5 %collective-permute-start.2 = (bf16[17,4,8,128]{3,2,1,0:T(8,128)(2,1)S(1)}, bf16[17,4,8,128]{3,2,1,0:T(8,128)(2,1)S(1)}, u32[]{:S(2)}, u32[]{:S(2)}) collective-permute-start(bf16[17,4,8,128]{3,2,1,0:T(8,128)(2,1)S(1)} %get-tuple-element.10), channel_id=1, source_target_pairs={{0,1},{1,0},{2,3},{3,2},{4,5},{5,4},{6,7},{7,6},{8,9},{9,8},{10,11... | collective-permute-start | bytes 417800 | tf_op jit(solution)/shard_map/ppermute | solution.py:449
  4.4 2.6 %collective-permute-start.5 = (bf16[17,4,8,128]{3,2,1,0:T(8,128)(2,1)S(1)}, bf16[17,4,8,128]{3,2,1,0:T(8,128)(2,1)S(1)}, u32[]{:S(2)}, u32[]{:S(2)}) collective-permute-start(bf16[17,4,8,128]{3,2,1,0:T(8,128)(2,1)S(1)} %get-tuple-element.9.refs_0_), channel_id=1, source_target_pairs={{0,2},{2,0},{1,3},{3,1},{4,6},{6,4},{5,7},{7,5},{8,10},{10,8},{9,1... | collective-permute-start | bytes 417800 | tf_op jit(solution)/shard_map/ppermute | solution.py:449
  7.0 1.3 %collective-permute-start.6 = (bf16[17,4,8,128]{3,2,1,0:T(8,128)(2,1)S(1)}, bf16[17,4,8,128]{3,2,1,0:T(8,128)(2,1)S(1)}, u32[]{:S(2)}, u32[]{:S(2)}) collective-permute-start(bf16[17,4,8,128]{3,2,1,0:T(8,128)(2,1)S(1)} %collective-permute-done.2.refs_2_), channel_id=1, source_target_pairs={{0,2},{2,0},{1,3},{3,1},{4,6},{6,4},{5,7},{7,5},{8,10},{10,8},{9,1... | collective-permute-start | bytes 417800 | tf_op jit(solution)/shard_map/ppermute | solution.py:449
  8.3 3.3 %collective-permute-done.5.refs_1_ = bf16[17,4,8,128]{3,2,1,0:T(8,128)(2,1)S(1)} collective-permute-done((bf16[17,4,8,128]{3,2,1,0:T(8,128)(2,1)S(1)}, bf16[17,4,8,128]{3,2,1,0:T(8,128)(2,1)S(1)}, u32[]{:S(2)}, u32[]{:S(2)}) %collective-permute-start.5) | collective-permute-done | bytes 139296 | tf_op jit(solution)/shard_map/ppermute | solution.py:449
  11.5 2.7 %collective-permute-done.6.refs_3_ = bf16[17,4,8,128]{3,2,1,0:T(8,128)(2,1)S(1)} collective-permute-done((bf16[17,4,8,128]{3,2,1,0:T(8,128)(2,1)S(1)}, bf16[17,4,8,128]{3,2,1,0:T(8,128)(2,1)S(1)}, u32[]{:S(2)}, u32[]{:S(2)}) %collective-permute-start.6) | collective-permute-done | bytes 139296 | tf_op jit(solution)/shard_map/ppermute | solution.py:449
  14.3 2.9 %whiten.1.white_ref = bf16[2,2,4,17,8,128]{5,4,3,2,1,0:T(8,128)(2,1)S(1)} custom-call(s32[2]{0:T(128)S(1)} %pad_add_fusion.place_ref, bf16[17,4,8,128]{3,2,1,0:T(8,128)(2,1)S(1)} %get-tuple-element.9.refs_0_, bf16[17,4,8,128]{3,2,1,0:T(8,128)(2,1)S(1)} %collective-permute-done.5.refs_1_, bf16[17,4,8,128]{3,2,1,0:T(8,128)(2,1)S(1)} %collective-permute-done.2.refs_2_, ...), custom_call_target="tpu_custom_call" | custom-call | flops 3000000000 | bytes 1048576 | tf_op jit(solution)/shard_map/whiten/pallas_call | solution.py:462
  17.2 1.9 %collective-permute-start.8 = (bf16[17,4,8,128]{3,2,1,0:T(8,128)(2,1)S(1)}, bf16[17,4,8,128]{3,2,1,0:T(8,128)(2,1)S(1)}, u32[]{:S(2)}, u32[]{:S(2)}) collective-permute-start(bf16[17,4,8,128]{3,2,1,0:T(8,128)(2,1)S(1)} %get-tuple-element.9.refs_0_), channel_id=1, source_target_pairs={{0,4},{4,8},{8,12},{12,0},{1,5},{5,9},{9,13},{13,1},{2,6},{6,10},{... | collective-permute-start | bytes 417800 | tf_op jit(solution)/shard_map/ppermute | solution.py:449
  19.1 2.1 %collective-permute-start = (bf16[17,4,8,128]{3,2,1,0:T(8,128)(2,1)S(1)}, bf16[17,4,8,128]{3,2,1,0:T(8,128)(2,1)S(1)}, u32[]{:S(2)}, u32[]{:S(2)}) collective-permute-start(bf16[17,4,8,128]{3,2,1,0:T(8,128)(2,1)S(1)} %get-tuple-element.9.refs_0_), channel_id=1, source_target_pairs={{0,12},{4,0},{8,4},{12,8},{1,13},{5,1},{9,5},{13,9},{2,14},{6,2},{... | collective-permute-start | bytes 417800 | tf_op jit(solution)/shard_map/ppermute | solution.py:449
  21.2 3.8 %collective-permute-start.3 = (bf16[17,4,8,128]{3,2,1,0:T(8,128)(2,1)S(1)}, bf16[17,4,8,128]{3,2,1,0:T(8,128)(2,1)S(1)}, u32[]{:S(2)}, u32[]{:S(2)}) collective-permute-start(bf16[17,4,8,128]{3,2,1,0:T(8,128)(2,1)S(1)} %collective-permute-done.2.refs_2_), channel_id=1, source_target_pairs={{0,12},{4,0},{8,4},{12,8},{1,13},{5,1},{9,5},{13,9},{2,14},{6,2},{... | collective-permute-start | bytes 417800 | tf_op jit(solution)/shard_map/ppermute | solution.py:449
  25.1 0.7 %collective-permute-done.8.refs_0_ = bf16[17,4,8,128]{3,2,1,0:T(8,128)(2,1)S(1)} collective-permute-done((bf16[17,4,8,128]{3,2,1,0:T(8,128)(2,1)S(1)}, bf16[17,4,8,128]{3,2,1,0:T(8,128)(2,1)S(1)}, u32[]{:S(2)}, u32[]{:S(2)}) %collective-permute-start.8) | collective-permute-done | bytes 139296 | tf_op jit(solution)/shard_map/ppermute | solution.py:449
  25.7 1.6 %collective-permute-start.9 = (bf16[17,4,8,128]{3,2,1,0:T(8,128)(2,1)S(1)}, bf16[17,4,8,128]{3,2,1,0:T(8,128)(2,1)S(1)}, u32[]{:S(2)}, u32[]{:S(2)}) collective-permute-start(bf16[17,4,8,128]{3,2,1,0:T(8,128)(2,1)S(1)} %collective-permute-done.8.refs_0_), channel_id=1, source_target_pairs={{0,2},{2,0},{1,3},{3,1},{4,6},{6,4},{5,7},{7,5},{8,10},{10,8},{9,1... | collective-permute-start | bytes 417800 | tf_op jit(solution)/shard_map/ppermute | solution.py:449
  27.4 1.4 %collective-permute-done.refs_0_ = bf16[17,4,8,128]{3,2,1,0:T(8,128)(2,1)S(1)} collective-permute-done((bf16[17,4,8,128]{3,2,1,0:T(8,128)(2,1)S(1)}, bf16[17,4,8,128]{3,2,1,0:T(8,128)(2,1)S(1)}, u32[]{:S(2)}, u32[]{:S(2)}) %collective-permute-start) | collective-permute-done | bytes 139296 | tf_op jit(solution)/shard_map/ppermute | solution.py:449
  28.7 1.6 %collective-permute-start.1 = (bf16[17,4,8,128]{3,2,1,0:T(8,128)(2,1)S(1)}, bf16[17,4,8,128]{3,2,1,0:T(8,128)(2,1)S(1)}, u32[]{:S(2)}, u32[]{:S(2)}) collective-permute-start(bf16[17,4,8,128]{3,2,1,0:T(8,128)(2,1)S(1)} %collective-permute-done.refs_0_), channel_id=1, source_target_pairs={{0,2},{2,0},{1,3},{3,1},{4,6},{6,4},{5,7},{7,5},{8,10},{10,8},{9,1... | collective-permute-start | bytes 417800 | tf_op jit(solution)/shard_map/ppermute | solution.py:449
  30.4 1.4 %collective-permute-done.10.refs_2_ = bf16[17,4,8,128]{3,2,1,0:T(8,128)(2,1)S(1)} collective-permute-done((bf16[17,4,8,128]{3,2,1,0:T(8,128)(2,1)S(1)}, bf16[17,4,8,128]{3,2,1,0:T(8,128)(2,1)S(1)}, u32[]{:S(2)}, u32[]{:S(2)}) %collective-permute-start.10) | collective-permute-done | bytes 139296 | tf_op jit(solution)/shard_map/ppermute | solution.py:449
  31.7 1.6 %collective-permute-start.11 = (bf16[17,4,8,128]{3,2,1,0:T(8,128)(2,1)S(1)}, bf16[17,4,8,128]{3,2,1,0:T(8,128)(2,1)S(1)}, u32[]{:S(2)}, u32[]{:S(2)}) collective-permute-start(bf16[17,4,8,128]{3,2,1,0:T(8,128)(2,1)S(1)} %collective-permute-done.10.refs_2_), channel_id=1, source_target_pairs={{0,2},{2,0},{1,3},{3,1},{4,6},{6,4},{5,7},{7,5},{8,10},{10,8},{9,1... | collective-permute-start | bytes 417800 | tf_op jit(solution)/shard_map/ppermute | solution.py:449
  33.4 0.5 collective-permute-done.3.refs_2_
  33.8 1.5 %collective-permute-start.4 = (bf16[17,4,8,128]{3,2,1,0:T(8,128)(2,1)S(1)}, bf16[17,4,8,128]{3,2,1,0:T(8,128)(2,1)S(1)}, u32[]{:S(2)}, u32[]{:S(2)}) collective-permute-start(bf16[17,4,8,128]{3,2,1,0:T(8,128)(2,1)S(1)} %collective-permute-done.3.refs_2_), channel_id=1, source_target_pairs={{0,2},{2,0},{1,3},{3,1},{4,6},{6,4},{5,7},{7,5},{8,10},{10,8},{9,1... | collective-permute-start | bytes 417800 | tf_op jit(solution)/shard_map/ppermute | solution.py:449
  35.3 2.8 %own_pairs.1 = (bf16[2,2,4,17,8,128]{5,4,3,2,1,0:T(8,128)(2,1)S(1)}, f32[3,4,4,3840]{3,2,1,0:T(4,128)}) custom-call(s32[2]{0:T(128)S(1)} %pad_add_fusion.place_ref, s32[1,3]{1,0:T(1,128)S(1)} %copy-done.2, bf16[2,2,4,17,8,128]{5,4,3,2,1,0:T(8,128)(2,1)S(1)} %whiten.1.white_ref, bf16[2,2,4,17,8,128]{5,4,3,2,1,0:T(8,128)(2,1)S(1)} %collective-permute-done.7.other_ref, ...), custom_call_target="tpu_custom_call" | custom-call | flops 2000000000 | bytes 1048576 | tf_op jit(solution)/shard_map/own_pairs/pallas_call | solution.py:472
  38.2 5.1 %far_pairs.2.refs_9_ = f32[3,4,4,3840]{3,2,1,0:T(4,128)} custom-call(s32[2]{0:T(128)S(1)} %pad_add_fusion.place_ref, s32[1,3]{1,0:T(1,128)S(1)} %copy-done.2, bf16[17,4,8,128]{3,2,1,0:T(8,128)(2,1)S(1)} %collective-permute-done.8.refs_0_, bf16[17,4,8,128]{3,2,1,0:T(8,128)(2,1)S(1)} %collective-permute-done.9.refs_1_, ...), custom_call_target="tpu_custom_call", output_to_operand_aliasing={{}: (11, {})} | custom-call | flops 4000000000 | bytes 1048576 | tf_op jit(solution)/shard_map/far_pairs/pallas_call | solution.py:487
  43.3 5.1 %far_pairs.3 = f32[3,4,4,3840]{3,2,1,0:T(4,128)} custom-call(s32[2]{0:T(128)S(1)} %pad_add_fusion.place_ref, s32[1,3]{1,0:T(1,128)S(1)} %copy-done.2, bf16[17,4,8,128]{3,2,1,0:T(8,128)(2,1)S(1)} %collective-permute-done.refs_0_, bf16[17,4,8,128]{3,2,1,0:T(8,128)(2,1)S(1)} %collective-permute-done.1.refs_1_, ...), custom_call_target="tpu_custom_call", output_to_operand_aliasing={{}: (11, {})} | custom-call | flops 4000000000 | bytes 1048576 | tf_op jit(solution)/shard_map/far_pairs/pallas_call | solution.py:487
  (25 shorter events, 0.4 us)
Async XLA Ops:
  0.0 0.7 %copy-start.7 = (bf16[64]{0:T(256)(128)(2,1)S(1)}, bf16[64]{0:T(256)(128)(2,1)}, u32[]{:S(2)}) copy-start(bf16[64]{0:T(256)(128)(2,1)} %param.9) | copy-start | bytes 388
  0.8 0.7 %copy-start.1 = (s32[8]{0:T(128)S(1)}, s32[8]{0:T(128)}, u32[]{:S(2)}) copy-start(s32[8]{0:T(128)} %end_ref.1) | copy-start | bytes 100
  1.5 1.2 %copy-start = (bf16[8,8,8192]{2,1,0:T(8,128)(2,1)S(1)}, bf16[8,8,8192]{2,1,0:T(8,128)(2,1)}, u32[]{:S(2)}) copy-start(bf16[8,8,8192]{2,1,0:T(8,128)(2,1)} %rec_ref.1) | copy-start | bytes 3145732
  2.7 11.5 %copy-start.3 = (bf16[2,256,256]{2,1,0:T(8,128)(2,1)S(1)}, bf16[2,256,256]{2,1,0:T(8,128)(2,1)}, u32[]{:S(2)}) copy-start(bf16[2,256,256]{2,1,0:T(8,128)(2,1)} %constant.18.clone.refs_5_.refs_6_) | copy-start | bytes 786436
  2.7 11.5 %copy-start.5 = (f32[2,17,8,128]{3,2,1,0:T(8,128)S(1)}, f32[2,17,8,128]{3,2,1,0:T(8,128)}, u32[]{:S(2)}) copy-start(f32[2,17,8,128]{3,2,1,0:T(8,128)} %constant.17.clone.refs_4_.twist_ref.refs_5_) | copy-start | bytes 417796
  2.7 11.5 %copy-start.6 = (bf16[128,128]{1,0:T(8,128)(2,1)S(1)}, bf16[128,128]{1,0:T(8,128)(2,1)}, u32[]{:S(2)}) copy-start(bf16[128,128]{1,0:T(8,128)(2,1)} %constant.20.clone.refs_6_.refs_7_) | copy-start | bytes 98308
  3.9 3.1 %collective-permute-start.2 = (bf16[17,4,8,128]{3,2,1,0:T(8,128)(2,1)S(1)}, bf16[17,4,8,128]{3,2,1,0:T(8,128)(2,1)S(1)}, u32[]{:S(2)}, u32[]{:S(2)}) collective-permute-start(bf16[17,4,8,128]{3,2,1,0:T(8,128)(2,1)S(1)} %get-tuple-element.10), channel_id=1, source_target_pairs={{0,1},{1,0},{2,3},{3,2},{4,5},{5,4},{6,7},{7,6},{8,9},{9,8},{10,11... | collective-permute-start | bytes 417800 | tf_op jit(solution)/shard_map/ppermute | solution.py:449
  4.4 30.9 %copy-start.2 = (s32[1,3]{1,0:T(1,128)S(1)}, s32[1,3]{1,0:T(1,128)}, u32[]{:S(2)}) copy-start(s32[1,3]{1,0:T(1,128)} %mask_ref.5) | copy-start | bytes 40
  4.4 30.9 %copy-start.4 = (bf16[2,256,256]{2,1,0:T(8,128)(2,1)S(1)}, bf16[2,256,256]{2,1,0:T(8,128)(2,1)}, u32[]{:S(2)}) copy-start(bf16[2,256,256]{2,1,0:T(8,128)(2,1)} %constant.19.clone.inverse_ref.refs_8_) | copy-start | bytes 786436
  4.4 7.1 %collective-permute-start.5 = (bf16[17,4,8,128]{3,2,1,0:T(8,128)(2,1)S(1)}, bf16[17,4,8,128]{3,2,1,0:T(8,128)(2,1)S(1)}, u32[]{:S(2)}, u32[]{:S(2)}) collective-permute-start(bf16[17,4,8,128]{3,2,1,0:T(8,128)(2,1)S(1)} %get-tuple-element.9.refs_0_), channel_id=1, source_target_pairs={{0,2},{2,0},{1,3},{3,1},{4,6},{6,4},{5,7},{7,5},{8,10},{10,8},{9,1... | collective-permute-start | bytes 417800 | tf_op jit(solution)/shard_map/ppermute | solution.py:449
  7.0 7.2 %collective-permute-start.6 = (bf16[17,4,8,128]{3,2,1,0:T(8,128)(2,1)S(1)}, bf16[17,4,8,128]{3,2,1,0:T(8,128)(2,1)S(1)}, u32[]{:S(2)}, u32[]{:S(2)}) collective-permute-start(bf16[17,4,8,128]{3,2,1,0:T(8,128)(2,1)S(1)} %collective-permute-done.2.refs_2_), channel_id=1, source_target_pairs={{0,2},{2,0},{1,3},{3,1},{4,6},{6,4},{5,7},{7,5},{8,10},{10,8},{9,1... | collective-permute-start | bytes 417800 | tf_op jit(solution)/shard_map/ppermute | solution.py:449
  17.2 18.2 %collective-permute-start.7 = (bf16[2,2,4,17,8,128]{5,4,3,2,1,0:T(8,128)(2,1)S(1)}, bf16[2,2,4,17,8,128]{5,4,3,2,1,0:T(8,128)(2,1)S(1)}, u32[]{:S(2)}, u32[]{:S(2)}) collective-permute-start(bf16[2,2,4,17,8,128]{5,4,3,2,1,0:T(8,128)(2,1)S(1)} %whiten.1.white_ref), channel_id=1, source_target_pairs={{0,1},{1,0},{2,3},{3,2},{4,5},{5,4},{6,7},{7,6},{8,9},{9,8},{10,11... | collective-permute-start | bytes 1671176 | tf_op jit(solution)/shard_map/ppermute | solution.py:449
  17.2 8.5 %collective-permute-start.8 = (bf16[17,4,8,128]{3,2,1,0:T(8,128)(2,1)S(1)}, bf16[17,4,8,128]{3,2,1,0:T(8,128)(2,1)S(1)}, u32[]{:S(2)}, u32[]{:S(2)}) collective-permute-start(bf16[17,4,8,128]{3,2,1,0:T(8,128)(2,1)S(1)} %get-tuple-element.9.refs_0_), channel_id=1, source_target_pairs={{0,4},{4,8},{8,12},{12,0},{1,5},{5,9},{9,13},{13,1},{2,6},{6,10},{... | collective-permute-start | bytes 417800 | tf_op jit(solution)/shard_map/ppermute | solution.py:449
  19.1 9.6 %collective-permute-start = (bf16[17,4,8,128]{3,2,1,0:T(8,128)(2,1)S(1)}, bf16[17,4,8,128]{3,2,1,0:T(8,128)(2,1)S(1)}, u32[]{:S(2)}, u32[]{:S(2)}) collective-permute-start(bf16[17,4,8,128]{3,2,1,0:T(8,128)(2,1)S(1)} %get-tuple-element.9.refs_0_), channel_id=1, source_target_pairs={{0,12},{4,0},{8,4},{12,8},{1,13},{5,1},{9,5},{13,9},{2,14},{6,2},{... | collective-permute-start | bytes 417800 | tf_op jit(solution)/shard_map/ppermute | solution.py:449
  21.2 10.5 %collective-permute-start.10 = (bf16[17,4,8,128]{3,2,1,0:T(8,128)(2,1)S(1)}, bf16[17,4,8,128]{3,2,1,0:T(8,128)(2,1)S(1)}, u32[]{:S(2)}, u32[]{:S(2)}) collective-permute-start(bf16[17,4,8,128]{3,2,1,0:T(8,128)(2,1)S(1)} %collective-permute-done.2.refs_2_), channel_id=1, source_target_pairs={{0,4},{4,8},{8,12},{12,0},{1,5},{5,9},{9,13},{13,1},{2,6},{6,10},{... | collective-permute-start | bytes 417800 | tf_op jit(solution)/shard_map/ppermute | solution.py:449
  21.2 12.6 %collective-permute-start.3 = (bf16[17,4,8,128]{3,2,1,0:T(8,128)(2,1)S(1)}, bf16[17,4,8,128]{3,2,1,0:T(8,128)(2,1)S(1)}, u32[]{:S(2)}, u32[]{:S(2)}) collective-permute-start(bf16[17,4,8,128]{3,2,1,0:T(8,128)(2,1)S(1)} %collective-permute-done.2.refs_2_), channel_id=1, source_target_pairs={{0,12},{4,0},{8,4},{12,8},{1,13},{5,1},{9,5},{13,9},{2,14},{6,2},{... | collective-permute-start | bytes 417800 | tf_op jit(solution)/shard_map/ppermute | solution.py:449
  25.7 12.4 %collective-permute-start.9 = (bf16[17,4,8,128]{3,2,1,0:T(8,128)(2,1)S(1)}, bf16[17,4,8,128]{3,2,1,0:T(8,128)(2,1)S(1)}, u32[]{:S(2)}, u32[]{:S(2)}) collective-permute-start(bf16[17,4,8,128]{3,2,1,0:T(8,128)(2,1)S(1)} %collective-permute-done.8.refs_0_), channel_id=1, source_target_pairs={{0,2},{2,0},{1,3},{3,1},{4,6},{6,4},{5,7},{7,5},{8,10},{10,8},{9,1... | collective-permute-start | bytes 417800 | tf_op jit(solution)/shard_map/ppermute | solution.py:449
  28.7 14.6 %collective-permute-start.1 = (bf16[17,4,8,128]{3,2,1,0:T(8,128)(2,1)S(1)}, bf16[17,4,8,128]{3,2,1,0:T(8,128)(2,1)S(1)}, u32[]{:S(2)}, u32[]{:S(2)}) collective-permute-start(bf16[17,4,8,128]{3,2,1,0:T(8,128)(2,1)S(1)} %collective-permute-done.refs_0_), channel_id=1, source_target_pairs={{0,2},{2,0},{1,3},{3,1},{4,6},{6,4},{5,7},{7,5},{8,10},{10,8},{9,1... | collective-permute-start | bytes 417800 | tf_op jit(solution)/shard_map/ppermute | solution.py:449
  31.7 6.4 %collective-permute-start.11 = (bf16[17,4,8,128]{3,2,1,0:T(8,128)(2,1)S(1)}, bf16[17,4,8,128]{3,2,1,0:T(8,128)(2,1)S(1)}, u32[]{:S(2)}, u32[]{:S(2)}) collective-permute-start(bf16[17,4,8,128]{3,2,1,0:T(8,128)(2,1)S(1)} %collective-permute-done.10.refs_2_), channel_id=1, source_target_pairs={{0,2},{2,0},{1,3},{3,1},{4,6},{6,4},{5,7},{7,5},{8,10},{10,8},{9,1... | collective-permute-start | bytes 417800 | tf_op jit(solution)/shard_map/ppermute | solution.py:449
  33.8 9.5 %collective-permute-start.4 = (bf16[17,4,8,128]{3,2,1,0:T(8,128)(2,1)S(1)}, bf16[17,4,8,128]{3,2,1,0:T(8,128)(2,1)S(1)}, u32[]{:S(2)}, u32[]{:S(2)}) collective-permute-start(bf16[17,4,8,128]{3,2,1,0:T(8,128)(2,1)S(1)} %collective-permute-done.3.refs_2_), channel_id=1, source_target_pairs={{0,2},{2,0},{1,3},{3,1},{4,6},{6,4},{5,7},{7,5},{8,10},{10,8},{9,1... | collective-permute-start | bytes 417800 | tf_op jit(solution)/shard_map/ppermute | solution.py:449

commit v2 on v1

--- a/solution.py
+++ b/solution.py
@@ -112,30 +112,63 @@
     return dot(high, table_ref[0]) + dot(low, table_ref[0]) + dot(high, table_ref[1])
 
 
-def decimate_kernel(place_ref, end_ref, base_ref, rec_ref, keep_ref, send_ref, lhs_ref):
+def decimate_kernel(
+    place_ref, end_hbm, taps_hbm, rec_hbm, keep_ref, send_ref,
+    rec_ref, lhs_ref, taps_ref, end_ref, rec_sem, small_sem,
+):
     channels, windows, length = rec_ref.shape
     half = channels // 2
     rows = half * windows
     blocks = length // BLOCK
-    tap_table = pltpu.roll(
-        jnp.broadcast_to(base_ref[...], (LANES, BLOCK + LANES)), 0, 1, stride=4, stride_axis=0
-    ).astype(BF16)
+    pieces = rec_sem.shape[0]
+    piece = length // pieces
+    taps = taps_hbm.shape[1]
+    small = [
+        pltpu.make_async_copy(end_hbm, end_ref, small_sem.at[0]),
+        pltpu.make_async_copy(taps_hbm, taps_ref, small_sem.at[1]),
+    ]
+    copies = [
+        pltpu.make_async_copy(
+            rec_hbm.at[:, :, k * piece : (k + 1) * piece],
+            rec_ref.at[:, :, k * piece : (k + 1) * piece],
+            rec_sem.at[k],
+        )
+        for k in range(pieces)
+    ]
+    for copy in small + copies:
+        copy.start()
     row = lax.broadcasted_iota(jnp.int32, (windows, BLOCK), 0)
     lane = lax.broadcasted_iota(jnp.int32, (windows, BLOCK), 1)
+    tap = lax.broadcasted_iota(jnp.int32, (taps, BLOCK + LANES), 0)
+    at = lax.broadcasted_iota(jnp.int32, (taps, BLOCK + LANES), 1)
+    chosen = jnp.where(tap + at == LANES + 3, 1.0, 0.0).astype(BF16)
+    for copy in small:
+        copy.wait()
+    base = jnp.dot(
+        jnp.broadcast_to(taps_ref[...].astype(F32), (SUB, taps)).astype(BF16), chosen,
+        preferred_element_type=F32,
+    )
+    tap_table = pltpu.roll(
+        jnp.broadcast_to(base[0:1], (LANES, BLOCK + LANES)), 0, 1, stride=4, stride_axis=0
+    ).astype(BF16)
     end = jnp.zeros((windows, BLOCK), jnp.int32)
     for w in range(windows):
         end = jnp.where(row == w, end_ref[w], end)
     end = end - place_ref[0] * length - lane
-    for h, out_ref in ((0, keep_ref), (1, send_ref)):
-        side = place_ref[1] if h == 0 else 1 - place_ref[1]
+    for h in range(2):
         lhs_ref[h, 0, :, 0:LANES] = jnp.zeros((rows, LANES), BF16)
         lhs_ref[h, blocks, :, LANES:] = jnp.zeros((rows, BLOCK), BF16)
-        for b in range(blocks):
+    for b in range(blocks):
+        if b * BLOCK % piece == 0:
+            copies[b * BLOCK // piece].wait()
+        for h in range(2):
+            side = place_ref[1] if h == 0 else 1 - place_ref[1]
             x = rec_ref[pl.ds(side * half, half), :, b * BLOCK : (b + 1) * BLOCK].astype(F32)
             x = jnp.where((end > b * BLOCK)[None], x, 0.0)
             x = x.reshape(rows, BLOCK).astype(BF16)
             lhs_ref[h, b, :, LANES:] = x
             lhs_ref[h, b + 1, :, 0:LANES] = x[:, BLOCK - LANES :]
+    for h, out_ref in ((0, keep_ref), (1, send_ref)):
         out = lax.dot_general(
             lhs_ref[h].reshape((blocks + 1) * rows, BLOCK + LANES),
             tap_table,
@@ -147,28 +180,44 @@
 
 def decimate(records, filter_taps, segment_end, place):
     channels, windows, length = records.shape
-    taps = filter_taps.shape[0]
-    reverse = filter_taps.astype(F32)[::-1]
-    base = jnp.pad(reverse, (LANES + 4 - taps, BLOCK - 4)).reshape(1, BLOCK + LANES)
     blocks = length // BLOCK
     piece = jax.ShapeDtypeStruct((blocks + 1, channels // 2, windows, LANES), BF16)
     return pl.pallas_call(
         decimate_kernel,
         out_shape=(piece, piece),
-        in_specs=[
-            pl.BlockSpec(memory_space=pltpu.SMEM),
-            pl.BlockSpec(memory_space=pltpu.SMEM),
-            pl.BlockSpec(memory_space=VMEM),
-            pl.BlockSpec(memory_space=VMEM),
+        in_specs=[pl.BlockSpec(memory_space=pltpu.SMEM)] + [pl.BlockSpec(memory_space=pltpu.HBM)] * 3,
+        out_specs=(pl.BlockSpec(memory_space=VMEM),) * 2,
+        scratch_shapes=[
+            VMEM(records.shape, BF16),
+            VMEM((2, blocks + 1, channels // 2 * windows, BLOCK + LANES), BF16),
+            VMEM((1, filter_taps.shape[0]), BF16),
+            pltpu.SMEM(segment_end.shape, jnp.int32),
+            pltpu.SemaphoreType.DMA((4,)),
+            pltpu.SemaphoreType.DMA((2,)),
         ],
-        out_specs=(pl.BlockSpec(memory_space=VMEM),) * 2,
-        scratch_shapes=[VMEM((2, blocks + 1, channels // 2 * windows, BLOCK + LANES), BF16)],
         compiler_params=pltpu.CompilerParams(vmem_limit_bytes=24 << 20),
         cost_estimate=pl.CostEstimate(
             flops=2 * records.size // 4 * BLOCK, bytes_accessed=3 * records.size, transcendentals=0
         ),
         name="decimate",
-    )(place, segment_end, base, records)
+    )(place, *(pltpu.with_memory_space_constraint(a, pltpu.HBM) for a in (segment_end, filter_taps.reshape(1, -1), records)))
+
+
+def join_kernel(first_ref, second_ref, out_ref):
+    out_ref[0] = first_ref[...]
+    out_ref[1] = second_ref[...]
+
+
+def join(first, second):
+    vmem = pl.BlockSpec(memory_space=VMEM)
+    return pl.pallas_call(
+        join_kernel,
+        out_shape=jax.ShapeDtypeStruct((2, *first.shape), first.dtype),
+        in_specs=[vmem, vmem],
+        out_specs=vmem,
+        name="join",
+        **params(0.2),
+    )(first, second)
 
 
 def spectra(segments, flags, tables, work, store):
@@ -199,7 +248,7 @@
                 low_ref[g, q, :, part * LANES : (part + 1) * LANES] = low
         return carry
 
-    lax.fori_loop(0, groups, first, 0)
+    lax.fori_loop(0, groups, first, 0, unroll=True)
     count = groups * RESIDUES * SUB
     spec = three_pass(
         high_ref[...].reshape(count, 2 * LANES), low_ref[...].reshape(count, 2 * LANES), dft_ref
@@ -219,7 +268,7 @@
         power_ref[g] = inner + ends * lower
         return carry
 
-    lax.fori_loop(0, groups, powers, 0)
+    lax.fori_loop(0, groups, powers, 0, unroll=True)
     high, low = split(power_ref[...].reshape(groups * SUB, LANES))
     energy = jnp.dot(high, band_ref[...], preferred_element_type=F32) + jnp.dot(
         low, band_ref[...], preferred_element_type=F32
@@ -241,7 +290,7 @@
                 store(part, g, q, (value * factor).astype(BF16))
         return carry
 
-    lax.fori_loop(0, groups, whiten, 0)
+    lax.fori_loop(0, groups, whiten, 0, unroll=True)
 
 
 def gather_rows(values):
@@ -290,7 +339,7 @@
                 low_ref[group, q, :, part * LANES : (part + 1) * LANES] = low
         return carry
 
-    lax.fori_loop(0, RESIDUES, cross, 0)
+    lax.fori_loop(0, RESIDUES, cross, 0, unroll=True)
     count = pair_groups * RESIDUES * SUB
     total = three_pass(
         high_ref[...].reshape(count, 2 * LANES), low_ref[...].reshape(count, 2 * LANES), inverse_ref
@@ -321,7 +370,7 @@
                 ]
         return carry
 
-    lax.fori_loop(0, pair_groups, lags, 0)
+    lax.fori_loop(0, pair_groups, lags, 0, unroll=True)
 
 
 def write_out(lag_ref, out_ref, offset, sem):
@@ -336,39 +385,42 @@
 
 
 def whiten_kernel(span, place_ref, *refs):
-    pieces = refs[: 2 * span]
-    twist_ref, dft_ref, band_ref, white_ref = refs[2 * span : 2 * span + 4]
-    work = refs[2 * span + 4 :]
+    pieces = refs[:span]
+    twist_ref, dft_ref, band_ref = refs[span : span + 3]
+    white_refs = refs[span + 3 : span + 5]
+    work = refs[span + 5 :]
     flags = flags_of(place_ref, span)
     for c in range(2):
 
         def store(part, g, q, value, c=c):
-            white_ref[c, part, g, q] = value
-
-        spectra(pieces[c * span : (c + 1) * span], flags, (twist_ref, dft_ref, band_ref), work, store)
+            white_refs[c][part, g, q] = value
+
+        spectra([piece.at[c] for piece in pieces], flags, (twist_ref, dft_ref, band_ref), work, store)
 
 
 def own_pairs_kernel(
-    owned, offset, scale, place_ref, mask_ref, white_ref, other_ref, twist_ref, inverse_ref,
-    own_ref, out_ref, high_ref, low_ref, sum_ref, lag_ref, sem,
+    owned, offset, scale, place_ref, mask_ref, *refs,
 ):
-    groups = white_ref.shape[2]
+    white_refs, other_refs = refs[:2], refs[2:4]
+    twist_ref, inverse_ref, own_ref, out_ref, high_ref, low_ref, sum_ref, lag_ref, sem = refs[4:]
+    groups = white_refs[0].shape[1]
     first = place_ref[0] * owned
     inside = lax.rem(first, groups)
     here = lax.div(first, groups) == place_ref[1]
 
     @pl.when(here)
     def _():
-        own_ref[...] = white_ref[:, :, pl.ds(inside, owned)]
+        for c in range(2):
+            own_ref[c] = white_refs[c][:, pl.ds(inside, owned)]
 
     @pl.when(jnp.logical_not(here))
     def _():
         for c in range(2):
-            own_ref[c] = other_ref[1 - c, :, pl.ds(inside, owned)]
+            own_ref[c] = other_refs[1 - c][:, pl.ds(inside, owned)]
 
     correlate(
         lambda c, p, i, q: own_ref[c, p, i, q],
-        lambda c, p, j, q: white_ref[c, p, j, q],
+        lambda c, p, j, q: white_refs[c][p, j, q],
         2, owned, groups, (twist_ref, inverse_ref), (high_ref, low_ref, sum_ref),
         mask_ref[0, offset].astype(F32) * scale, lag_ref,
     )
@@ -376,11 +428,11 @@
 
 
 def far_pairs_kernel(span, owned, offset, scale, place_ref, mask_ref, *refs):
-    pieces = refs[: 2 * span]
-    own_ref, twist_ref, dft_ref, band_ref, inverse_ref, _, out_ref = refs[2 * span : 2 * span + 7]
+    pieces = refs[:span]
+    own_ref, twist_ref, dft_ref, band_ref, inverse_ref, _, out_ref = refs[span : span + 7]
     (
         white_ref, zhigh_ref, zlow_ref, spec_ref, power_ref, high_ref, low_ref, sum_ref, lag_ref, sem,
-    ) = refs[2 * span + 7 :]
+    ) = refs[span + 7 :]
     flags = flags_of(place_ref, span)
     groups = white_ref.shape[2]
     for c in range(2):
@@ -389,7 +441,7 @@
             white_ref[c, part, g, q] = value
 
         spectra(
-            pieces[c * span : (c + 1) * span], flags, (twist_ref, dft_ref, band_ref),
+            [piece.at[c] for piece in pieces], flags, (twist_ref, dft_ref, band_ref),
             (zhigh_ref, zlow_ref, spec_ref, power_ref), store,
         )
     correlate(
@@ -425,7 +477,7 @@
     return dict(
         compiler_params=pltpu.CompilerParams(vmem_limit_bytes=16 << 20),
         cost_estimate=pl.CostEstimate(
-            flops=int(microseconds * 1e9), bytes_accessed=1 << 20, transcendentals=0
+            flops=int(microseconds * 1e6), bytes_accessed=1 << 10, transcendentals=0
         ),
     )
 
@@ -452,50 +504,50 @@
         return [chunk] + [permute(chunk, "tm", -s) for s in range(1, span)]
 
     keep, send = decimate(records, filter_taps, segment_end, place)
-    chunks = [keep, permute(send, "win", 1)]
-    up = down = chunks
+    block = join(keep, permute(send, "win", 1))
+    up = down = block
     moved = []
     for _ in range(reach):
-        up = [permute(chunk, "chan", 1) for chunk in up]
-        down = [permute(chunk, "chan", -1) for chunk in down]
-        moved.append((up, down))
+        up, down = permute(up, "chan", 1), permute(down, "chan", -1)
+        moved.append([up, down])
+    mine = segments(block)
     white = pl.pallas_call(
         functools.partial(whiten_kernel, span),
-        out_shape=jax.ShapeDtypeStruct((2, 2, groups, RESIDUES, SUB, LANES), BF16),
-        in_specs=[smem] + [vmem] * (2 * span + 3),
-        out_specs=vmem,
+        out_shape=(jax.ShapeDtypeStruct((2, groups, RESIDUES, SUB, LANES), BF16),) * 2,
+        in_specs=[smem] + [vmem] * (span + 3),
+        out_specs=(vmem,) * 2,
         scratch_shapes=spectra_work(groups),
         name="whiten",
         **params(3),
-    )(place, *segments(chunks[0]), *segments(chunks[1]), twist, dft, band)
-    other = permute(white, "win", 1)
+    )(place, *mine, twist, dft, band)
+    other = [permute(part, "win", 1) for part in white]
     own, out = pl.pallas_call(
         functools.partial(own_pairs_kernel, owned, reach, scale),
         out_shape=(
             jax.ShapeDtypeStruct((2, 2, owned, RESIDUES, SUB, LANES), BF16),
             jax.ShapeDtypeStruct((2 * reach + 1, groups, owned, 2 * MAXLAG), F32),
         ),
-        in_specs=[smem, smem] + [vmem] * 4,
+        in_specs=[smem, smem] + [vmem] * 6,
         out_specs=(vmem, anywhere),
         scratch_shapes=lag_work(groups, owned),
         name="own_pairs",
         **params(2),
-    )(place, pair_mask, white, other, twist, inverse)
+    )(place, pair_mask, *white, *other, twist, inverse)
     for step, sides in enumerate(moved):
         for side, far in zip((-1, 1), sides):
             offset = reach + side * (step + 1)
             out = pl.pallas_call(
                 functools.partial(far_pairs_kernel, span, owned, offset, scale),
                 out_shape=jax.ShapeDtypeStruct(out.shape, out.dtype),
-                in_specs=[smem, smem] + [vmem] * (2 * span + 5) + [anywhere],
+                in_specs=[smem, smem] + [vmem] * (span + 5) + [anywhere],
                 out_specs=anywhere,
                 scratch_shapes=[VMEM((2, 2, groups, RESIDUES, SUB, LANES), BF16)]
                 + spectra_work(groups)
                 + lag_work(groups, owned),
-                input_output_aliases={2 * span + 7: 0},
+                input_output_aliases={span + 7: 0},
                 name="far_pairs",
                 **params(4),
-            )(place, pair_mask, *segments(far[0]), *segments(far[1]), own, twist, dft, band, inverse, out)
+            )(place, pair_mask, *segments(far), own, twist, dft, band, inverse, out)
     return out
 
 

time: 48.6 us -> 35.9 us (0.74)
  the two profiles are of different devices: /device:TPU:0 before, /device:TPU:16 now
where the time goes in v2:
time: 35.9 us; the launch traced here: 35.8 us
  Pallas kernels  15.7 us (44%)
  waiting for transfers between devices  13.7 us (38%)
  starting transfers between devices  6.25 us (17%)
    ppermute x8, waiting for transfers between devices, permute(): lax.ppermute(array, axis, [(i, (i + by) % count) for i in range(count)])  13.7 us
    pallas_call x2, Pallas kernels, shards(): pl.pallas_call(functools.partial(far_pairs_kernel, span, owned, offset, s...  8.36 us
    ppermute x8, starting transfers between devices, permute(): lax.ppermute(array, axis, [(i, (i + by) % count) for i in range(count)])  6.25 us
    pallas_call x1, Pallas kernels, shards(): pl.pallas_call(functools.partial(own_pairs_kernel, owned, reach, scale),...  2.5 us
    pallas_call x1, Pallas kernels, shards(): pl.pallas_call(functools.partial(whiten_kernel, span), out_shape=(jax.Sha...  2.4 us
    pallas_call x1, Pallas kernels, decimate(): pl.pallas_call(decimate_kernel, out_shape=(piece, piece), in_specs=[pl.Bl...  2.38 us
  transfers between devices with their start and end apart: 8, of which 4 were waited for; matrix products, arithmetic and copies ran while one was open for 0% of the time, Pallas kernels for 25%

profile of v2, /device:TPU:16, one launch (start us, length us, event | category | flops | bytes accessed | tf_op | source)
XLA Modules:
  0.0 35.8 jit_solution(16161541699781483737)
XLA Ops:
  0.0 0.1 pad_add_fusion.place_ref
  0.1 2.4 %decimate.1 = (bf16[17,4,8,128]{3,2,1,0:T(8,128)(2,1)S(1)}, bf16[17,4,8,128]{3,2,1,0:T(8,128)(2,1)S(1)}) custom-call(s32[2]{0:T(128)S(1)} %pad_add_fusion.place_ref, s32[8]{0:T(128)} %end_hbm.1, bf16[1,64]{1,0:T(2,128)(2,1)} %bitcast.3, bf16[8,8,8192]{2,1,0:T(8,128)(2,1)} %rec_hbm.1), custom_call_target="tpu_custom_call" | custom-call | flops 134217728 | bytes 1572864 | tf_op jit(solution)/shard_map/decimate/pallas_call | solution.py:185
  2.5 0.1 collective-permute-start
  2.5 1.3 %collective-permute-done.second_ref = bf16[17,4,8,128]{3,2,1,0:T(8,128)(2,1)S(1)} collective-permute-done((bf16[17,4,8,128]{3,2,1,0:T(8,128)(2,1)S(1)}, bf16[17,4,8,128]{3,2,1,0:T(8,128)(2,1)S(1)}, u32[]{:S(2)}, u32[]{:S(2)}) %collective-permute-start) | collective-permute-done | bytes 139296 | tf_op jit(solution)/shard_map/ppermute | solution.py:501
  3.9 0.0 copy-start.1
  3.9 1.6 %collective-permute-start.3 = (bf16[2,17,4,8,128]{4,3,2,1,0:T(8,128)(2,1)S(1)}, bf16[2,17,4,8,128]{4,3,2,1,0:T(8,128)(2,1)S(1)}, u32[]{:S(2)}, u32[]{:S(2)}) collective-permute-start(bf16[2,17,4,8,128]{4,3,2,1,0:T(8,128)(2,1)S(1)} %join.1.refs_0_), channel_id=1, source_target_pairs={{0,2},{2,0},{1,3},{3,1},{4,6},{6,4},{5,7},{7,5},{8,10},{10,8},{9,1... | collective-permute-start | bytes 835592 | tf_op jit(solution)/shard_map/ppermute | solution.py:501
  5.5 1.6 %collective-permute-start.6 = (bf16[2,17,4,8,128]{4,3,2,1,0:T(8,128)(2,1)S(1)}, bf16[2,17,4,8,128]{4,3,2,1,0:T(8,128)(2,1)S(1)}, u32[]{:S(2)}, u32[]{:S(2)}) collective-permute-start(bf16[2,17,4,8,128]{4,3,2,1,0:T(8,128)(2,1)S(1)} %join.1.refs_0_), channel_id=1, source_target_pairs={{0,4},{4,8},{8,12},{12,0},{1,5},{5,9},{9,13},{13,1},{2,6},{6,10},{... | collective-permute-start | bytes 835592 | tf_op jit(solution)/shard_map/ppermute | solution.py:501
  7.1 0.5 %collective-permute-start.1 = (bf16[2,17,4,8,128]{4,3,2,1,0:T(8,128)(2,1)S(1)}, bf16[2,17,4,8,128]{4,3,2,1,0:T(8,128)(2,1)S(1)}, u32[]{:S(2)}, u32[]{:S(2)}) collective-permute-start(bf16[2,17,4,8,128]{4,3,2,1,0:T(8,128)(2,1)S(1)} %join.1.refs_0_), channel_id=1, source_target_pairs={{0,12},{4,0},{8,4},{12,8},{1,13},{5,1},{9,5},{13,9},{2,14},{6,2},{... | collective-permute-start | bytes 835592 | tf_op jit(solution)/shard_map/ppermute | solution.py:501
  7.5 5.2 %collective-permute-done.3.refs_1_ = bf16[2,17,4,8,128]{4,3,2,1,0:T(8,128)(2,1)S(1)} collective-permute-done((bf16[2,17,4,8,128]{4,3,2,1,0:T(8,128)(2,1)S(1)}, bf16[2,17,4,8,128]{4,3,2,1,0:T(8,128)(2,1)S(1)}, u32[]{:S(2)}, u32[]{:S(2)}) %collective-permute-start.3) | collective-permute-done | bytes 278560 | tf_op jit(solution)/shard_map/ppermute | solution.py:501
  12.7 2.4 %whiten.1 = (bf16[2,4,17,8,128]{4,3,2,1,0:T(8,128)(2,1)S(1)}, bf16[2,4,17,8,128]{4,3,2,1,0:T(8,128)(2,1)S(1)}) custom-call(s32[2]{0:T(128)S(1)} %pad_add_fusion.place_ref, bf16[2,17,4,8,128]{4,3,2,1,0:T(8,128)(2,1)S(1)} %join.1.refs_0_, bf16[2,17,4,8,128]{4,3,2,1,0:T(8,128)(2,1)S(1)} %collective-permute-done.3.refs_1_, f32[2,17,8,128]{3,2,1,0:T(8,128)S(1)} %copy-done.2, ...), custom_call_target="tpu_custom_call" | custom-call | flops 3000000 | bytes 1024 | tf_op jit(solution)/shard_map/whiten/pallas_call | solution.py:514
  15.1 0.0 copy-start.4
  15.1 0.1 collective-permute-start.4
  15.2 0.5 %collective-permute-start.5 = (bf16[2,4,17,8,128]{4,3,2,1,0:T(8,128)(2,1)S(1)}, bf16[2,4,17,8,128]{4,3,2,1,0:T(8,128)(2,1)S(1)}, u32[]{:S(2)}, u32[]{:S(2)}) collective-permute-start(bf16[2,4,17,8,128]{4,3,2,1,0:T(8,128)(2,1)S(1)} %get-tuple-element.14.refs_1_), channel_id=1, source_target_pairs={{0,1},{1,0},{2,3},{3,2},{4,5},{5,4},{6,7},{7,6},{8,9},{9,8},{10,11... | collective-permute-start | bytes 835592 | tf_op jit(solution)/shard_map/ppermute | solution.py:501
  15.7 4.2 %collective-permute-done.6.refs_0_ = bf16[2,17,4,8,128]{4,3,2,1,0:T(8,128)(2,1)S(1)} collective-permute-done((bf16[2,17,4,8,128]{4,3,2,1,0:T(8,128)(2,1)S(1)}, bf16[2,17,4,8,128]{4,3,2,1,0:T(8,128)(2,1)S(1)}, u32[]{:S(2)}, u32[]{:S(2)}) %collective-permute-start.6) | collective-permute-done | bytes 278560 | tf_op jit(solution)/shard_map/ppermute | solution.py:501
  19.9 0.5 %collective-permute-start.7 = (bf16[2,17,4,8,128]{4,3,2,1,0:T(8,128)(2,1)S(1)}, bf16[2,17,4,8,128]{4,3,2,1,0:T(8,128)(2,1)S(1)}, u32[]{:S(2)}, u32[]{:S(2)}) collective-permute-start(bf16[2,17,4,8,128]{4,3,2,1,0:T(8,128)(2,1)S(1)} %collective-permute-done.6.refs_0_), channel_id=1, source_target_pairs={{0,2},{2,0},{1,3},{3,1},{4,6},{6,4},{5,7},{7,5},{8,10},{10,8},{9,1... | collective-permute-start | bytes 835592 | tf_op jit(solution)/shard_map/ppermute | solution.py:501
  20.4 0.0 collective-permute-done.1.refs_0_
  20.4 1.5 %collective-permute-start.2 = (bf16[2,17,4,8,128]{4,3,2,1,0:T(8,128)(2,1)S(1)}, bf16[2,17,4,8,128]{4,3,2,1,0:T(8,128)(2,1)S(1)}, u32[]{:S(2)}, u32[]{:S(2)}) collective-permute-start(bf16[2,17,4,8,128]{4,3,2,1,0:T(8,128)(2,1)S(1)} %collective-permute-done.1.refs_0_), channel_id=1, source_target_pairs={{0,2},{2,0},{1,3},{3,1},{4,6},{6,4},{5,7},{7,5},{8,10},{10,8},{9,1... | collective-permute-start | bytes 835592 | tf_op jit(solution)/shard_map/ppermute | solution.py:501
  21.9 0.0 collective-permute-done.4.refs_2_
  21.9 0.0 collective-permute-done.5.refs_3_
  21.9 2.5 %own_pairs.1 = (bf16[2,2,4,17,8,128]{5,4,3,2,1,0:T(8,128)(2,1)S(1)}, f32[3,4,4,3840]{3,2,1,0:T(4,128)}) custom-call(s32[2]{0:T(128)S(1)} %pad_add_fusion.place_ref, s32[1,3]{1,0:T(1,128)S(1)} %copy-done.4, bf16[2,4,17,8,128]{4,3,2,1,0:T(8,128)(2,1)S(1)} %get-tuple-element.13.refs_0_, bf16[2,4,17,8,128]{4,3,2,1,0:T(8,128)(2,1)S(1)} %get-tuple-element.14.refs_1_, ...), custom_call_target="tpu_custom_call" | custom-call | flops 2000000 | bytes 1024 | tf_op jit(solution)/shard_map/own_pairs/pallas_call | solution.py:524
  24.4 2.9 %collective-permute-done.7.refs_1_ = bf16[2,17,4,8,128]{4,3,2,1,0:T(8,128)(2,1)S(1)} collective-permute-done((bf16[2,17,4,8,128]{4,3,2,1,0:T(8,128)(2,1)S(1)}, bf16[2,17,4,8,128]{4,3,2,1,0:T(8,128)(2,1)S(1)}, u32[]{:S(2)}, u32[]{:S(2)}) %collective-permute-start.7) | collective-permute-done | bytes 278560 | tf_op jit(solution)/shard_map/ppermute | solution.py:501
  27.4 4.2 %far_pairs.2.refs_7_ = f32[3,4,4,3840]{3,2,1,0:T(4,128)} custom-call(s32[2]{0:T(128)S(1)} %pad_add_fusion.place_ref, s32[1,3]{1,0:T(1,128)S(1)} %copy-done.4, bf16[2,17,4,8,128]{4,3,2,1,0:T(8,128)(2,1)S(1)} %collective-permute-done.6.refs_0_, bf16[2,17,4,8,128]{4,3,2,1,0:T(8,128)(2,1)S(1)} %collective-permute-done.7.refs_1_, ...), custom_call_target="tpu_custom_call", output_to_operand_aliasing={{}: (9, {})} | custom-call | flops 4000000 | bytes 1024 | tf_op jit(solution)/shard_map/far_pairs/pallas_call | solution.py:539
  31.6 0.0 collective-permute-done.2.refs_1_
  31.6 4.2 %far_pairs.3 = f32[3,4,4,3840]{3,2,1,0:T(4,128)} custom-call(s32[2]{0:T(128)S(1)} %pad_add_fusion.place_ref, s32[1,3]{1,0:T(1,128)S(1)} %copy-done.4, bf16[2,17,4,8,128]{4,3,2,1,0:T(8,128)(2,1)S(1)} %collective-permute-done.1.refs_0_, bf16[2,17,4,8,128]{4,3,2,1,0:T(8,128)(2,1)S(1)} %collective-permute-done.2.refs_1_, ...), custom_call_target="tpu_custom_call", output_to_operand_aliasing={{}: (9, {})} | custom-call | flops 4000000 | bytes 1024 | tf_op jit(solution)/shard_map/far_pairs/pallas_call | solution.py:539
  (9 shorter events, 0.0 us)
Async XLA Ops:
  2.5 1.4 %collective-permute-start = (bf16[17,4,8,128]{3,2,1,0:T(8,128)(2,1)S(1)}, bf16[17,4,8,128]{3,2,1,0:T(8,128)(2,1)S(1)}, u32[]{:S(2)}, u32[]{:S(2)}) collective-permute-start(bf16[17,4,8,128]{3,2,1,0:T(8,128)(2,1)S(1)} %get-tuple-element.12), channel_id=1, source_target_pairs={{0,1},{1,0},{2,3},{3,2},{4,5},{5,4},{6,7},{7,6},{8,9},{9,8},{10,11... | collective-permute-start | bytes 417800 | tf_op jit(solution)/shard_map/ppermute | solution.py:501
  3.9 8.8 %copy-start = (bf16[2,256,256]{2,1,0:T(8,128)(2,1)S(1)}, bf16[2,256,256]{2,1,0:T(8,128)(2,1)}, u32[]{:S(2)}) copy-start(bf16[2,256,256]{2,1,0:T(8,128)(2,1)} %constant.15.clone.refs_3_.refs_4_) | copy-start | bytes 786436
  3.9 8.8 %copy-start.2 = (f32[2,17,8,128]{3,2,1,0:T(8,128)S(1)}, f32[2,17,8,128]{3,2,1,0:T(8,128)}, u32[]{:S(2)}) copy-start(f32[2,17,8,128]{3,2,1,0:T(8,128)} %constant.14.clone.refs_2_.refs_4_.refs_3_) | copy-start | bytes 417796
  3.9 8.8 %copy-start.3 = (bf16[128,128]{1,0:T(8,128)(2,1)S(1)}, bf16[128,128]{1,0:T(8,128)(2,1)}, u32[]{:S(2)}) copy-start(bf16[128,128]{1,0:T(8,128)(2,1)} %constant.17.clone.refs_4_.refs_5_) | copy-start | bytes 98308
  3.9 18.0 %copy-start.1 = (bf16[2,256,256]{2,1,0:T(8,128)(2,1)S(1)}, bf16[2,256,256]{2,1,0:T(8,128)(2,1)}, u32[]{:S(2)}) copy-start(bf16[2,256,256]{2,1,0:T(8,128)(2,1)} %constant.16.clone.refs_5_.refs_6_) | copy-start | bytes 786436
  3.9 8.8 %collective-permute-start.3 = (bf16[2,17,4,8,128]{4,3,2,1,0:T(8,128)(2,1)S(1)}, bf16[2,17,4,8,128]{4,3,2,1,0:T(8,128)(2,1)S(1)}, u32[]{:S(2)}, u32[]{:S(2)}) collective-permute-start(bf16[2,17,4,8,128]{4,3,2,1,0:T(8,128)(2,1)S(1)} %join.1.refs_0_), channel_id=1, source_target_pairs={{0,2},{2,0},{1,3},{3,1},{4,6},{6,4},{5,7},{7,5},{8,10},{10,8},{9,1... | collective-permute-start | bytes 835592 | tf_op jit(solution)/shard_map/ppermute | solution.py:501
  5.5 14.4 %collective-permute-start.6 = (bf16[2,17,4,8,128]{4,3,2,1,0:T(8,128)(2,1)S(1)}, bf16[2,17,4,8,128]{4,3,2,1,0:T(8,128)(2,1)S(1)}, u32[]{:S(2)}, u32[]{:S(2)}) collective-permute-start(bf16[2,17,4,8,128]{4,3,2,1,0:T(8,128)(2,1)S(1)} %join.1.refs_0_), channel_id=1, source_target_pairs={{0,4},{4,8},{8,12},{12,0},{1,5},{5,9},{9,13},{13,1},{2,6},{6,10},{... | collective-permute-start | bytes 835592 | tf_op jit(solution)/shard_map/ppermute | solution.py:501
  7.1 13.4 %collective-permute-start.1 = (bf16[2,17,4,8,128]{4,3,2,1,0:T(8,128)(2,1)S(1)}, bf16[2,17,4,8,128]{4,3,2,1,0:T(8,128)(2,1)S(1)}, u32[]{:S(2)}, u32[]{:S(2)}) collective-permute-start(bf16[2,17,4,8,128]{4,3,2,1,0:T(8,128)(2,1)S(1)} %join.1.refs_0_), channel_id=1, source_target_pairs={{0,12},{4,0},{8,4},{12,8},{1,13},{5,1},{9,5},{13,9},{2,14},{6,2},{... | collective-permute-start | bytes 835592 | tf_op jit(solution)/shard_map/ppermute | solution.py:501
  15.1 6.8 %copy-start.4 = (s32[1,3]{1,0:T(1,128)S(1)}, s32[1,3]{1,0:T(1,128)}, u32[]{:S(2)}) copy-start(s32[1,3]{1,0:T(1,128)} %mask_ref.5) | copy-start | bytes 40
  15.1 6.8 %collective-permute-start.4 = (bf16[2,4,17,8,128]{4,3,2,1,0:T(8,128)(2,1)S(1)}, bf16[2,4,17,8,128]{4,3,2,1,0:T(8,128)(2,1)S(1)}, u32[]{:S(2)}, u32[]{:S(2)}) collective-permute-start(bf16[2,4,17,8,128]{4,3,2,1,0:T(8,128)(2,1)S(1)} %get-tuple-element.13.refs_0_), channel_id=1, source_target_pairs={{0,1},{1,0},{2,3},{3,2},{4,5},{5,4},{6,7},{7,6},{8,9},{9,8},{10,11... | collective-permute-start | bytes 835592 | tf_op jit(solution)/shard_map/ppermute | solution.py:501
  15.2 6.7 %collective-permute-start.5 = (bf16[2,4,17,8,128]{4,3,2,1,0:T(8,128)(2,1)S(1)}, bf16[2,4,17,8,128]{4,3,2,1,0:T(8,128)(2,1)S(1)}, u32[]{:S(2)}, u32[]{:S(2)}) collective-permute-start(bf16[2,4,17,8,128]{4,3,2,1,0:T(8,128)(2,1)S(1)} %get-tuple-element.14.refs_1_), channel_id=1, source_target_pairs={{0,1},{1,0},{2,3},{3,2},{4,5},{5,4},{6,7},{7,6},{8,9},{9,8},{10,11... | collective-permute-start | bytes 835592 | tf_op jit(solution)/shard_map/ppermute | solution.py:501
  19.9 7.5 %collective-permute-start.7 = (bf16[2,17,4,8,128]{4,3,2,1,0:T(8,128)(2,1)S(1)}, bf16[2,17,4,8,128]{4,3,2,1,0:T(8,128)(2,1)S(1)}, u32[]{:S(2)}, u32[]{:S(2)}) collective-permute-start(bf16[2,17,4,8,128]{4,3,2,1,0:T(8,128)(2,1)S(1)} %collective-permute-done.6.refs_0_), channel_id=1, source_target_pairs={{0,2},{2,0},{1,3},{3,1},{4,6},{6,4},{5,7},{7,5},{8,10},{10,8},{9,1... | collective-permute-start | bytes 835592 | tf_op jit(solution)/shard_map/ppermute | solution.py:501
  20.4 11.2 %collective-permute-start.2 = (bf16[2,17,4,8,128]{4,3,2,1,0:T(8,128)(2,1)S(1)}, bf16[2,17,4,8,128]{4,3,2,1,0:T(8,128)(2,1)S(1)}, u32[]{:S(2)}, u32[]{:S(2)}) collective-permute-start(bf16[2,17,4,8,128]{4,3,2,1,0:T(8,128)(2,1)S(1)} %collective-permute-done.1.refs_0_), channel_id=1, source_target_pairs={{0,2},{2,0},{1,3},{3,1},{4,6},{6,4},{5,7},{7,5},{8,10},{10,8},{9,1... | collective-permute-start | bytes 835592 | tf_op jit(solution)/shard_map/ppermute | solution.py:501

commit v3 on v2

--- a/solution.py
+++ b/solution.py
@@ -10,6 +10,7 @@
 from jax.sharding import PartitionSpec as P
 
 MAXLAG = 1920
+COST = (5000, 5000, 500, 500, 500)
 BAND = 64
 EPSILON = 1e-06
 
@@ -113,9 +114,10 @@
 
 
 def decimate_kernel(
-    place_ref, end_hbm, taps_hbm, rec_hbm, keep_ref, send_ref,
-    rec_ref, lhs_ref, taps_ref, end_ref, rec_sem, small_sem,
+    by, place_ref, end_hbm, taps_hbm, rec_hbm, keep_ref, send_ref, *refs
 ):
+    rec_ref, lhs_ref, taps_ref, end_ref, rec_sem, small_sem = refs[-6:]
+    whole_ref = refs[0] if len(refs) == 7 else None
     channels, windows, length = rec_ref.shape
     half = channels // 2
     rows = half * windows
@@ -162,7 +164,7 @@
         if b * BLOCK % piece == 0:
             copies[b * BLOCK // piece].wait()
         for h in range(2):
-            side = place_ref[1] if h == 0 else 1 - place_ref[1]
+            side = place_ref[by] if h == 0 else 1 - place_ref[by]
             x = rec_ref[pl.ds(side * half, half), :, b * BLOCK : (b + 1) * BLOCK].astype(F32)
             x = jnp.where((end > b * BLOCK)[None], x, 0.0)
             x = x.reshape(rows, BLOCK).astype(BF16)
@@ -175,18 +177,22 @@
             (((1,), (1,)), ((), ())),
             preferred_element_type=F32,
         )
-        out_ref[...] = out.reshape(blocks + 1, half, windows, LANES).astype(BF16)
-
-
-def decimate(records, filter_taps, segment_end, place):
+        out = out.reshape(blocks + 1, half, windows, LANES).astype(BF16)
+        out_ref[...] = out
+        if whole_ref is not None:
+            whole_ref[place_ref[by] if h == 0 else 1 - place_ref[by]] = out
+
+
+def decimate(records, filter_taps, segment_end, place, by, whole):
     channels, windows, length = records.shape
     blocks = length // BLOCK
     piece = jax.ShapeDtypeStruct((blocks + 1, channels // 2, windows, LANES), BF16)
+    both = jax.ShapeDtypeStruct((2, *piece.shape), BF16)
     return pl.pallas_call(
-        decimate_kernel,
-        out_shape=(piece, piece),
+        functools.partial(decimate_kernel, by),
+        out_shape=(piece, piece, both) if whole else (piece, piece),
         in_specs=[pl.BlockSpec(memory_space=pltpu.SMEM)] + [pl.BlockSpec(memory_space=pltpu.HBM)] * 3,
-        out_specs=(pl.BlockSpec(memory_space=VMEM),) * 2,
+        out_specs=(pl.BlockSpec(memory_space=VMEM),) * (3 if whole else 2),
         scratch_shapes=[
             VMEM(records.shape, BF16),
             VMEM((2, blocks + 1, channels // 2 * windows, BLOCK + LANES), BF16),
@@ -220,18 +226,19 @@
     )(first, second)
 
 
-def spectra(segments, flags, tables, work, store):
+def spectra(load, flags, tables, work, store):
     twist_ref, dft_ref, band_ref = tables
     high_ref, low_ref, spec_ref, power_ref = work
-    depth, groups = segments[0].shape[0] - 1, segments[0].shape[1]
+    groups, span = high_ref.shape[0], len(flags)
+    depth = ROWS // span
 
     def first(g, carry):
         x = []
-        for s in range(len(segments)):
+        for s in range(span):
             for r in range(depth):
-                value = segments[s][r, g].astype(F32)
+                value = load(s, r, g).astype(F32)
                 if r == 0:
-                    value = value + segments[s - 1][depth, g].astype(F32) * flags[s]
+                    value = value + load((s - 1) % span, depth, g).astype(F32) * flags[s]
                 x.append(value)
         for q, (real, imag) in enumerate(real_transform(x)):
             if q == 0:
@@ -248,7 +255,8 @@
                 low_ref[g, q, :, part * LANES : (part + 1) * LANES] = low
         return carry
 
-    lax.fori_loop(0, groups, first, 0, unroll=True)
+    for g in range(groups):
+        first(g, 0)
     count = groups * RESIDUES * SUB
     spec = three_pass(
         high_ref[...].reshape(count, 2 * LANES), low_ref[...].reshape(count, 2 * LANES), dft_ref
@@ -268,7 +276,8 @@
         power_ref[g] = inner + ends * lower
         return carry
 
-    lax.fori_loop(0, groups, powers, 0, unroll=True)
+    for g in range(groups):
+        powers(g, 0)
     high, low = split(power_ref[...].reshape(groups * SUB, LANES))
     energy = jnp.dot(high, band_ref[...], preferred_element_type=F32) + jnp.dot(
         low, band_ref[...], preferred_element_type=F32
@@ -290,7 +299,8 @@
                 store(part, g, q, (value * factor).astype(BF16))
         return carry
 
-    lax.fori_loop(0, groups, whiten, 0, unroll=True)
+    for g in range(groups):
+        whiten(g, 0)
 
 
 def gather_rows(values):
@@ -312,65 +322,71 @@
     return jnp.where(lower, pltpu.roll(value, SUB - step, 0), pltpu.roll(value, step, 0))
 
 
+def cross_rows(owned, js, windows, part_of_own, part_of_remote):
+    groups = []
+    loaded = [[[part_of_own(w, p, i).astype(F32) for p in range(2)] for i in range(owned)] for w in range(windows)]
+    for first in range(0, js * owned, SUB):
+        real, imag = [], []
+        for pair in range(first, first + SUB):
+            j, i = pair // owned, pair % owned
+            re = im = None
+            for w in range(windows):
+                ar, ai = loaded[w][i]
+                br, bi = (part_of_remote(w, p, j).astype(F32) for p in range(2))
+                r = ar * br + ai * bi
+                m = ai * br - ar * bi
+                re = r if re is None else re + r
+                im = m if im is None else im + m
+            real.append(re)
+            imag.append(im)
+        groups.append((gather_rows(real), gather_rows(imag)))
+    return groups
+
+
+def lag_rows_of(sum_ref, group, twist_ref, weight):
+    x = []
+    for q in range(RESIDUES):
+        real, imag = sum_ref[group, q, :, :LANES], sum_ref[group, q, :, LANES:]
+        if q == 0:
+            x.append((real, None))
+            continue
+        cos, sin = twist_ref[0, q], twist_ref[1, q]
+        turned = real * cos - imag * sin
+        if q == RESIDUES - 1:
+            x.append((turned, None))
+        else:
+            x.append((0.5 * turned, 0.5 * (real * sin + imag * cos)))
+    out = real_inverse(x)
+    count = MAXLAG // LANES
+    return [out[a] * weight for a in (*range(ROWS - count, ROWS), *range(count))]
+
+
 def correlate(own_load, remote_load, chunks, owned, remotes, tables, work, weight, lag_ref):
     twist_ref, inverse_ref = tables
     high_ref, low_ref, sum_ref = work
     pair_groups = remotes * owned // SUB
-
-    def cross(q, carry):
-        own = [[[own_load(c, p, i, q).astype(F32) for p in range(2)] for i in range(owned)] for c in range(chunks)]
-        for group in range(pair_groups):
-            real, imag = [], []
-            for pair in range(group * SUB, (group + 1) * SUB):
-                j, i = pair // owned, pair % owned
-                re = im = None
-                for c in range(chunks):
-                    ar, ai = own[c][i]
-                    br, bi = (remote_load(c, p, j, q).astype(F32) for p in range(2))
-                    r = ar * br + ai * bi
-                    m = ai * br - ar * bi
-                    re = r if re is None else re + r
-                    im = m if im is None else im + m
-                real.append(re)
-                imag.append(im)
-            for part, values in enumerate((real, imag)):
-                high, low = split(gather_rows(values))
+    for q in range(RESIDUES):
+        rows = cross_rows(
+            owned, remotes, chunks,
+            lambda w, p, i: own_load(w, p, i, q), lambda w, p, j: remote_load(w, p, j, q),
+        )
+        for group, parts in enumerate(rows):
+            for part, value in enumerate(parts):
+                high, low = split(value)
                 high_ref[group, q, :, part * LANES : (part + 1) * LANES] = high
                 low_ref[group, q, :, part * LANES : (part + 1) * LANES] = low
-        return carry
-
-    lax.fori_loop(0, RESIDUES, cross, 0, unroll=True)
     count = pair_groups * RESIDUES * SUB
     total = three_pass(
         high_ref[...].reshape(count, 2 * LANES), low_ref[...].reshape(count, 2 * LANES), inverse_ref
     )
     sum_ref[...] = total.reshape(pair_groups, RESIDUES, SUB, 2 * LANES)
-    lag_rows = MAXLAG // LANES
     per = SUB // owned
-
-    def lags(group, carry):
-        x = []
-        for q in range(RESIDUES):
-            real, imag = sum_ref[group, q, :, :LANES], sum_ref[group, q, :, LANES:]
-            if q == 0:
-                x.append((real, None))
-                continue
-            cos, sin = twist_ref[0, q], twist_ref[1, q]
-            turned = real * cos - imag * sin
-            if q == RESIDUES - 1:
-                x.append((turned, None))
-            else:
-                x.append((0.5 * turned, 0.5 * (real * sin + imag * cos)))
-        out = real_inverse(x)
-        for place, a in enumerate((*range(ROWS - lag_rows, ROWS), *range(lag_rows))):
-            value = out[a] * weight
+    for group in range(pair_groups):
+        for place, value in enumerate(lag_rows_of(sum_ref, group, twist_ref, weight)):
             for j in range(per):
                 lag_ref[group * per + j, :, place * LANES : (place + 1) * LANES] = value[
                     j * owned : (j + 1) * owned
                 ]
-        return carry
-
-    lax.fori_loop(0, pair_groups, lags, 0, unroll=True)
 
 
 def write_out(lag_ref, out_ref, offset, sem):
@@ -395,7 +411,10 @@
         def store(part, g, q, value, c=c):
             white_refs[c][part, g, q] = value
 
-        spectra([piece.at[c] for piece in pieces], flags, (twist_ref, dft_ref, band_ref), work, store)
+        def load(s, r, g, c=c):
+            return pieces[s][c, r, g]
+
+        spectra(load, flags, (twist_ref, dft_ref, band_ref), work, store)
 
 
 def own_pairs_kernel(
@@ -440,8 +459,11 @@
         def store(part, g, q, value, c=c):
             white_ref[c, part, g, q] = value
 
+        def load(s, r, g, c=c):
+            return pieces[s][c, r, g]
+
         spectra(
-            [piece.at[c] for piece in pieces], flags, (twist_ref, dft_ref, band_ref),
+            load, flags, (twist_ref, dft_ref, band_ref),
             (zhigh_ref, zlow_ref, spec_ref, power_ref), store,
         )
     correlate(
@@ -451,6 +473,162 @@
         mask_ref[0, offset].astype(F32) * scale, lag_ref,
     )
     write_out(lag_ref, out_ref, offset, sem)
+
+
+def own_spectra_kernel(place_ref, mine_ref, theirs_ref, twist_ref, dft_ref, band_ref, away_ref, here_ref, *work):
+    flags = flags_of(place_ref, 2)
+    for side, white_ref in ((1 - place_ref[1], away_ref), (place_ref[1], here_ref)):
+
+        def load(s, r, g, side=side):
+            return (mine_ref, theirs_ref)[s][side, r, g]
+
+        def store(part, g, q, value, white_ref=white_ref):
+            white_ref[part, g, q] = value
+
+        spectra(load, flags, (twist_ref, dft_ref, band_ref), work, store)
+
+
+def far_spectra_kernel(place_ref, mine_ref, relayed_ref, twist_ref, dft_ref, band_ref, white_ref, *work):
+    def load(s, r, g):
+        return (mine_ref, relayed_ref)[s][r, g]
+
+    def store(part, g, q, value):
+        white_ref[part, g, q] = value
+
+    spectra(load, flags_of(place_ref, 2), (twist_ref, dft_ref, band_ref), work, store)
+
+
+def far_cross_kernel(mine_ref, theirs_ref, far_ref, fars_ref, across_ref, back_ref):
+    own, far = (mine_ref, theirs_ref), (far_ref, fars_ref)
+    for q in range(RESIDUES):
+        rows = cross_rows(4, 4, 2, lambda w, p, i: own[w][p, i, q], lambda w, p, j: far[w][p, j, q])
+        for group, parts in enumerate(rows):
+            for part, value in enumerate(parts):
+                at = slice(part * LANES, (part + 1) * LANES)
+                value = value.astype(BF16)
+                across_ref[group, q, :, at] = value
+                back_ref[group, q, :, at] = value if part == 0 else -value
+
+
+def near_pairs_kernel(
+    offset, scale, place_ref, mask_ref, away_ref, here_ref, others_here_ref, others_away_ref,
+    twist_ref, inverse_ref, out_ref, own_ref, high_ref, low_ref, sum_ref, lag_ref, sem,
+):
+    same = place_ref[0] == place_ref[1]
+
+    @pl.when(same)
+    def _():
+        own_ref[0] = here_ref[...]
+        own_ref[1] = others_away_ref[...]
+
+    @pl.when(jnp.logical_not(same))
+    def _():
+        own_ref[0] = away_ref[...]
+        own_ref[1] = others_here_ref[...]
+
+    half = (here_ref, others_away_ref)
+    correlate(
+        lambda w, p, i, q: own_ref[w, p, i, q],
+        lambda w, p, j, q: half[w][p, j, q],
+        2, 4, 4, (twist_ref, inverse_ref), (high_ref, low_ref, sum_ref),
+        mask_ref[0, offset].astype(F32) * scale, lag_ref,
+    )
+    write_out(lag_ref, out_ref, offset, sem)
+
+
+def lags_kernel(offset, scale, mirrored, mask_ref, cross_ref, twist_ref, inverse_ref, _, out_ref, sum_ref, lag_ref, sem):
+    rows = cross_ref[...].reshape(2 * RESIDUES * SUB, 2 * LANES)
+    total = jnp.dot(rows, inverse_ref[0], preferred_element_type=F32) + jnp.dot(
+        rows, inverse_ref[1], preferred_element_type=F32
+    )
+    sum_ref[...] = total.reshape(2, RESIDUES, SUB, 2 * LANES)
+    weight = mask_ref[0, offset].astype(F32) * scale
+    for group in range(2):
+        for place, value in enumerate(lag_rows_of(sum_ref, group, twist_ref, weight)):
+            at = slice(place * LANES, (place + 1) * LANES)
+            if mirrored:
+                for row in range(SUB):
+                    lag_ref[row % 4, group * 2 + row // 4, at] = value[row]
+            else:
+                for j in range(2):
+                    lag_ref[group * 2 + j, :, at] = value[4 * j : 4 * j + 4]
+    write_out(lag_ref, out_ref, offset, sem)
+
+
+def mirrored(records, filter_taps, segment_end, pair_mask, place, tables, scale):
+    twist, dft, inverse, band = tables
+    smem, vmem = pl.BlockSpec(memory_space=pltpu.SMEM), pl.BlockSpec(memory_space=VMEM)
+    anywhere = pl.BlockSpec(memory_space=pl.ANY)
+    blocks = lax.axis_size("chan")
+    white = jax.ShapeDtypeStruct((2, 4, RESIDUES, SUB, LANES), BF16)
+    spec = jax.ShapeDtypeStruct((2, RESIDUES, SUB, 2 * LANES), BF16)
+    shape = jax.ShapeDtypeStruct((3, 4, 4, 2 * MAXLAG), F32)
+
+    def exchange(array, axis):
+        return lax.ppermute(array, axis, [(0, 1), (1, 0)])
+
+    def along(array, by):
+        return lax.ppermute(array, "chan", [(i, (i + by) % blocks) for i in range(blocks)])
+
+    def across(array):
+        pairs = [(0, 0), (1, 2), (2, 1), (3, 3)]
+        return lax.ppermute(array, ("tm", "win"), pairs)
+
+    keep, send, both = decimate(records, filter_taps, segment_end, place, 0, True)
+    far_send, far_keep = along(send, 1), along(keep, 1)
+    theirs = exchange(both, "tm")
+    relayed = exchange(far_send, "tm")
+    away, here = pl.pallas_call(
+        own_spectra_kernel,
+        out_shape=(white, white),
+        in_specs=[smem] + [vmem] * 5,
+        out_specs=(vmem, vmem),
+        scratch_shapes=spectra_work(4),
+        name="own_spectra",
+        **params(COST[0]),
+    )(place, both, theirs, twist, dft, band)
+    (away, here), relayed = lax.optimization_barrier(((away, here), relayed))
+    others_away, others_here = exchange(away, "win"), exchange(here, "win")
+    far = pl.pallas_call(
+        far_spectra_kernel,
+        out_shape=white,
+        in_specs=[smem] + [vmem] * 5,
+        out_specs=vmem,
+        scratch_shapes=spectra_work(4),
+        name="far_spectra",
+        **params(COST[1]),
+    )(place, far_keep, relayed, twist, dft, band)
+    fars = exchange(far, "win")
+    crossed, back = pl.pallas_call(
+        far_cross_kernel,
+        out_shape=(spec, spec),
+        in_specs=[vmem] * 4,
+        out_specs=(vmem, vmem),
+        name="far_cross",
+        **params(COST[2]),
+    )(here, others_away, far, fars)
+    crossed, back = across(crossed), along(back, -1)
+    out = pl.pallas_call(
+        functools.partial(near_pairs_kernel, 1, scale),
+        out_shape=shape,
+        in_specs=[smem, smem] + [vmem] * 6,
+        out_specs=anywhere,
+        scratch_shapes=[VMEM((2, 2, 4, RESIDUES, SUB, LANES), BF16)] + lag_work(4, 4),
+        name="near_pairs",
+        **params(COST[3]),
+    )(place, pair_mask, away, here, others_here, others_away, twist, inverse)
+    for offset, cross in ((0, crossed), (2, back)):
+        out = pl.pallas_call(
+            functools.partial(lags_kernel, offset, scale, offset == 2),
+            out_shape=shape,
+            in_specs=[smem] + [vmem] * 3 + [anywhere],
+            out_specs=anywhere,
+            scratch_shapes=lag_work(4, 4)[2:],
+            input_output_aliases={4: 0},
+            name="lags",
+            **params(COST[4]),
+        )(pair_mask, cross, twist, inverse, out)
+    return out
 
 
 def spectra_work(groups):
@@ -503,8 +681,11 @@
     def segments(chunk):
         return [chunk] + [permute(chunk, "tm", -s) for s in range(1, span)]
 
-    keep, send = decimate(records, filter_taps, segment_end, place)
-    block = join(keep, permute(send, "win", 1))
+    if span == 2 and reach == 1 and groups == 4:
+        return mirrored(records, filter_taps, segment_end, pair_mask, place, (twist, dft, inverse, band), scale)
+    keep, send = decimate(records, filter_taps, segment_end, place, 1, False)
+    received = permute(send, "win", 1)
+    block = join(keep, received)
     up = down = block
     moved = []
     for _ in range(reach):

time: 35.9 us -> 32.9 us (0.916)
  the two profiles are of different devices: /device:TPU:16 before, /device:TPU:1 now
where the time goes in v3:
time: 32.9 us; the launch traced here: 32.7 us
  starting transfers between devices  13.8 us (42%)
  Pallas kernels  12.7 us (39%)
  waiting for transfers between devices  6.01 us (18%)
    ppermute x5, starting transfers between devices, exchange(): return lax.ppermute(array, axis, [(0, 1), (1, 0)])  7.23 us
    ppermute x3, starting transfers between devices, along(): lax.ppermute(array, 'chan', [(i, (i + by) % blocks) for i in range(blocks)])  4.43 us
    ppermute x3, waiting for transfers between devices, along(): lax.ppermute(array, 'chan', [(i, (i + by) % blocks) for i in range(blocks)])  3.56 us
    pallas_call x2, Pallas kernels, mirrored(): pl.pallas_call(functools.partial(lags_kernel, offset, scale, offset == 2)...  3.22 us
    pallas_call x1, Pallas kernels, mirrored(): pl.pallas_call(functools.partial(near_pairs_kernel, 1, scale), out_shape=...  2.49 us
    pallas_call x1, Pallas kernels, mirrored(): pl.pallas_call(own_spectra_kernel, out_shape=(white, white), in_specs=[sm...  2.42 us
    pallas_call x1, Pallas kernels, decimate(): pl.pallas_call(functools.partial(decimate_kernel, by), out_shape=(piece,...  2.37 us
    ppermute x5, waiting for transfers between devices, exchange(): return lax.ppermute(array, axis, [(0, 1), (1, 0)])  2.33 us
  transfers between devices with their start and end apart: 9, of which 5 were waited for; matrix products, arithmetic and copies ran while one was open for 0% of the time, Pallas kernels for 23%

profile of v3, /device:TPU:1, one launch (start us, length us, event | category | flops | bytes accessed | tf_op | source)
XLA Modules:
  0.0 32.7 jit_solution(14148086661760679366)
XLA Ops:
  0.0 0.1 pad_add_fusion.place_ref
  0.1 2.4 %decimate.1 = (bf16[17,4,8,128]{3,2,1,0:T(8,128)(2,1)S(1)}, bf16[17,4,8,128]{3,2,1,0:T(8,128)(2,1)S(1)}, bf16[2,17,4,8,128]{4,3,2,1,0:T(8,128)(2,1)S(1)}) custom-call(s32[2]{0:T(128)S(1)} %pad_add_fusion.place_ref, s32[8]{0:T(128)} %end_hbm.1, bf16[1,64]{1,0:T(2,128)(2,1)} %bitcast.3, bf16[8,8,8192]{2,1,0:T(8,128)(2,1)} %rec_hbm.1), custom_call_target="tpu_custom_call" | custom-call | flops 134217728 | bytes 1572864 | tf_op jit(solution)/shard_map/decimate/pallas_call | solution.py:191
  2.5 2.1 %collective-permute-start = (bf16[2,17,4,8,128]{4,3,2,1,0:T(8,128)(2,1)S(1)}, bf16[2,17,4,8,128]{4,3,2,1,0:T(8,128)(2,1)S(1)}, u32[]{:S(2)}, u32[]{:S(2)}) collective-permute-start(bf16[2,17,4,8,128]{4,3,2,1,0:T(8,128)(2,1)S(1)} %get-tuple-element.15.mine_ref), channel_id=1, source_target_pairs={{0,2},{2,0},{1,3},{3,1},{4,6},{6,4},{5,7},{7,5},{8,10},{10,8},{9,1... | collective-permute-start | bytes 835592 | tf_op jit(solution)/shard_map/ppermute | solution.py:568
  4.6 1.3 %collective-permute-start.1 = (bf16[17,4,8,128]{3,2,1,0:T(8,128)(2,1)S(1)}, bf16[17,4,8,128]{3,2,1,0:T(8,128)(2,1)S(1)}, u32[]{:S(2)}, u32[]{:S(2)}) collective-permute-start(bf16[17,4,8,128]{3,2,1,0:T(8,128)(2,1)S(1)} %get-tuple-element.18), channel_id=1, source_target_pairs={{0,4},{4,8},{8,12},{12,0},{1,5},{5,9},{9,13},{13,1},{2,6},{6,10},{... | collective-permute-start | bytes 417800 | tf_op jit(solution)/shard_map/ppermute | solution.py:571
  5.9 1.3 %collective-permute-start.4 = (bf16[17,4,8,128]{3,2,1,0:T(8,128)(2,1)S(1)}, bf16[17,4,8,128]{3,2,1,0:T(8,128)(2,1)S(1)}, u32[]{:S(2)}, u32[]{:S(2)}) collective-permute-start(bf16[17,4,8,128]{3,2,1,0:T(8,128)(2,1)S(1)} %get-tuple-element.21), channel_id=1, source_target_pairs={{0,4},{4,8},{8,12},{12,0},{1,5},{5,9},{9,13},{13,1},{2,6},{6,10},{... | collective-permute-start | bytes 417800 | tf_op jit(solution)/shard_map/ppermute | solution.py:571
  7.2 3.6 %collective-permute-done.1 = bf16[17,4,8,128]{3,2,1,0:T(8,128)(2,1)S(1)} collective-permute-done((bf16[17,4,8,128]{3,2,1,0:T(8,128)(2,1)S(1)}, bf16[17,4,8,128]{3,2,1,0:T(8,128)(2,1)S(1)}, u32[]{:S(2)}, u32[]{:S(2)}) %collective-permute-start.1) | collective-permute-done | bytes 139296 | tf_op jit(solution)/shard_map/ppermute | solution.py:571
  10.7 0.5 %collective-permute-start.2 = (bf16[17,4,8,128]{3,2,1,0:T(8,128)(2,1)S(1)}, bf16[17,4,8,128]{3,2,1,0:T(8,128)(2,1)S(1)}, u32[]{:S(2)}, u32[]{:S(2)}) collective-permute-start(bf16[17,4,8,128]{3,2,1,0:T(8,128)(2,1)S(1)} %collective-permute-done.1), channel_id=1, source_target_pairs={{0,2},{2,0},{1,3},{3,1},{4,6},{6,4},{5,7},{7,5},{8,10},{10,8},{9,1... | collective-permute-start | bytes 417800 | tf_op jit(solution)/shard_map/ppermute | solution.py:568
  11.2 2.4 %own_spectra.1 = (bf16[2,4,17,8,128]{4,3,2,1,0:T(8,128)(2,1)S(1)}, bf16[2,4,17,8,128]{4,3,2,1,0:T(8,128)(2,1)S(1)}) custom-call(s32[2]{0:T(128)S(1)} %pad_add_fusion.place_ref, bf16[2,17,4,8,128]{4,3,2,1,0:T(8,128)(2,1)S(1)} %get-tuple-element.15.mine_ref, bf16[2,17,4,8,128]{4,3,2,1,0:T(8,128)(2,1)S(1)} %collective-permute-done.theirs_ref, ...), custom_call_target="tpu_custom_call" | custom-call | flops 5000000000 | bytes 1024 | tf_op jit(solution)/shard_map/own_spectra/pallas_call | solution.py:581
  13.7 1.3 %collective-permute-done.2.relayed_ref = bf16[17,4,8,128]{3,2,1,0:T(8,128)(2,1)S(1)} collective-permute-done((bf16[17,4,8,128]{3,2,1,0:T(8,128)(2,1)S(1)}, bf16[17,4,8,128]{3,2,1,0:T(8,128)(2,1)S(1)}, u32[]{:S(2)}, u32[]{:S(2)}) %collective-permute-start.2) | collective-permute-done | bytes 139296 | tf_op jit(solution)/shard_map/ppermute | solution.py:568
  14.9 1.3 %far_spectra.1.far_ref = bf16[2,4,17,8,128]{4,3,2,1,0:T(8,128)(2,1)S(1)} custom-call(s32[2]{0:T(128)S(1)} %pad_add_fusion.place_ref, bf16[17,4,8,128]{3,2,1,0:T(8,128)(2,1)S(1)} %collective-permute-done.4.mine_ref, bf16[17,4,8,128]{3,2,1,0:T(8,128)(2,1)S(1)} %collective-permute-done.2.relayed_ref, f32[2,17,8,128]{3,2,1,0:T(8,128)S(1)} %copy-done.1, ...), custom_call_target="tpu_custom_call" | custom-call | flops 5000000000 | bytes 1024 | tf_op jit(solution)/shard_map/far_spectra/pallas_call | solution.py:592
  16.2 0.0 copy-start
  16.2 4.1 %collective-permute-start.5 = (bf16[2,4,17,8,128]{4,3,2,1,0:T(8,128)(2,1)S(1)}, bf16[2,4,17,8,128]{4,3,2,1,0:T(8,128)(2,1)S(1)}, u32[]{:S(2)}, u32[]{:S(2)}) collective-permute-start(bf16[2,4,17,8,128]{4,3,2,1,0:T(8,128)(2,1)S(1)} %far_spectra.1.far_ref), channel_id=1, source_target_pairs={{0,1},{1,0},{2,3},{3,2},{4,5},{5,4},{6,7},{7,6},{8,9},{9,8},{10,11... | collective-permute-start | bytes 835592 | tf_op jit(solution)/shard_map/ppermute | solution.py:568
  20.3 0.1 collective-permute-start.3
  20.4 0.4 %collective-permute-start.8 = (bf16[2,4,17,8,128]{4,3,2,1,0:T(8,128)(2,1)S(1)}, bf16[2,4,17,8,128]{4,3,2,1,0:T(8,128)(2,1)S(1)}, u32[]{:S(2)}, u32[]{:S(2)}) collective-permute-start(bf16[2,4,17,8,128]{4,3,2,1,0:T(8,128)(2,1)S(1)} %get-tuple-element.19.mine_ref.here_ref), channel_id=1, source_target_pairs={{0,1},{1,0},{2,3},{3,2},{4,5},{5,4},{6,7},{7,6},{8,9},{9,8},{10,11... | collective-permute-start | bytes 835592 | tf_op jit(solution)/shard_map/ppermute | solution.py:568
  20.8 0.7 %collective-permute-done.5.fars_ref = bf16[2,4,17,8,128]{4,3,2,1,0:T(8,128)(2,1)S(1)} collective-permute-done((bf16[2,4,17,8,128]{4,3,2,1,0:T(8,128)(2,1)S(1)}, bf16[2,4,17,8,128]{4,3,2,1,0:T(8,128)(2,1)S(1)}, u32[]{:S(2)}, u32[]{:S(2)}) %collective-permute-start.5) | collective-permute-done | bytes 278560 | tf_op jit(solution)/shard_map/ppermute | solution.py:568
  21.5 0.4 %collective-permute-done.3.theirs_ref.others_away_ref = bf16[2,4,17,8,128]{4,3,2,1,0:T(8,128)(2,1)S(1)} collective-permute-done((bf16[2,4,17,8,128]{4,3,2,1,0:T(8,128)(2,1)S(1)}, bf16[2,4,17,8,128]{4,3,2,1,0:T(8,128)(2,1)S(1)}, u32[]{:S(2)}, u32[]{:S(2)}) %collective-permute-start.3) | collective-permute-done | bytes 278560 | tf_op jit(solution)/shard_map/ppermute | solution.py:568
  21.9 0.9 %far_cross.1 = (bf16[2,17,8,256]{3,2,1,0:T(8,128)(2,1)S(1)}, bf16[2,17,8,256]{3,2,1,0:T(8,128)(2,1)S(1)}) custom-call(bf16[2,4,17,8,128]{4,3,2,1,0:T(8,128)(2,1)S(1)} %get-tuple-element.19.mine_ref.here_ref, bf16[2,4,17,8,128]{4,3,2,1,0:T(8,128)(2,1)S(1)} %collective-permute-done.3.theirs_ref.others_away_ref, ...), custom_call_target="tpu_custom_call" | custom-call | flops 500000000 | bytes 1024 | tf_op jit(solution)/shard_map/far_cross/pallas_call | solution.py:602
  22.8 0.0 copy-start.2
  22.8 2.2 %collective-permute-start.7 = (bf16[2,17,8,256]{3,2,1,0:T(8,128)(2,1)S(1)}, bf16[2,17,8,256]{3,2,1,0:T(8,128)(2,1)S(1)}, u32[]{:S(2)}, u32[]{:S(2)}) collective-permute-start(bf16[2,17,8,256]{3,2,1,0:T(8,128)(2,1)S(1)} %get-tuple-element.24), channel_id=1, source_target_pairs={{0,0},{1,2},{2,1},{3,3},{4,4},{5,6},{6,5},{7,7},{8,8},{9,10},{10,9... | collective-permute-start | bytes 417800 | tf_op jit(solution)/shard_map/ppermute | solution.py:575
  25.0 1.8 %collective-permute-start.6 = (bf16[2,17,8,256]{3,2,1,0:T(8,128)(2,1)S(1)}, bf16[2,17,8,256]{3,2,1,0:T(8,128)(2,1)S(1)}, u32[]{:S(2)}, u32[]{:S(2)}) collective-permute-start(bf16[2,17,8,256]{3,2,1,0:T(8,128)(2,1)S(1)} %get-tuple-element.23), channel_id=1, source_target_pairs={{0,12},{4,0},{8,4},{12,8},{1,13},{5,1},{9,5},{13,9},{2,14},{6,2},{... | collective-permute-start | bytes 417800 | tf_op jit(solution)/shard_map/ppermute | solution.py:571
  26.9 2.5 %near_pairs.1._ = f32[3,4,4,3840]{3,2,1,0:T(4,128)} custom-call(s32[2]{0:T(128)S(1)} %pad_add_fusion.place_ref, s32[1,3]{1,0:T(1,128)S(1)} %copy-done.2, bf16[2,4,17,8,128]{4,3,2,1,0:T(8,128)(2,1)S(1)} %get-tuple-element.20.away_ref, bf16[2,4,17,8,128]{4,3,2,1,0:T(8,128)(2,1)S(1)} %get-tuple-element.19.mine_ref.here_ref, ...), custom_call_target="tpu_custom_call" | custom-call | flops 500000000 | bytes 1024 | tf_op jit(solution)/shard_map/near_pairs/pallas_call | solution.py:611
  29.4 0.1 collective-permute-done.7.cross_ref
  29.5 1.6 %lags.2._ = f32[3,4,4,3840]{3,2,1,0:T(4,128)} custom-call(s32[1,3]{1,0:T(1,128)S(1)} %copy-done.2, bf16[2,17,8,256]{3,2,1,0:T(8,128)(2,1)S(1)} %collective-permute-done.7.cross_ref, f32[2,17,8,128]{3,2,1,0:T(8,128)S(1)} %copy-done.1, bf16[2,256,256]{2,1,0:T(8,128)(2,1)S(1)} %copy-done, f32[3,4,4,3840]{3,2,1,0:T(4,128)} %near_pairs.1._), custom_call_target="tpu_custom_call", output_to_operand_aliasing={{}: (4, {})} | custom-call | flops 500000000 | bytes 1024 | tf_op jit(solution)/shard_map/lags/pallas_call | solution.py:621
  31.1 1.7 %lags.3 = f32[3,4,4,3840]{3,2,1,0:T(4,128)} custom-call(s32[1,3]{1,0:T(1,128)S(1)} %copy-done.2, bf16[2,17,8,256]{3,2,1,0:T(8,128)(2,1)S(1)} %collective-permute-done.6.cross_ref, f32[2,17,8,128]{3,2,1,0:T(8,128)S(1)} %copy-done.1, bf16[2,256,256]{2,1,0:T(8,128)(2,1)S(1)} %copy-done, f32[3,4,4,3840]{3,2,1,0:T(4,128)} %lags.2._), custom_call_target="tpu_custom_call", output_to_operand_aliasing={{}: (4, {})} | custom-call | flops 500000000 | bytes 1024 | tf_op jit(solution)/shard_map/lags/pallas_call | solution.py:621
  (12 shorter events, 0.0 us)
Async XLA Ops:
  0.1 11.1 %copy-start.1 = (f32[2,17,8,128]{3,2,1,0:T(8,128)S(1)}, f32[2,17,8,128]{3,2,1,0:T(8,128)}, u32[]{:S(2)}) copy-start(f32[2,17,8,128]{3,2,1,0:T(8,128)} %constant.14.clone.twist_ref) | copy-start | bytes 417796
  0.1 11.1 %copy-start.3 = (bf16[2,256,256]{2,1,0:T(8,128)(2,1)S(1)}, bf16[2,256,256]{2,1,0:T(8,128)(2,1)}, u32[]{:S(2)}) copy-start(bf16[2,256,256]{2,1,0:T(8,128)(2,1)} %constant.15.clone.dft_ref) | copy-start | bytes 786436
  0.1 11.2 %copy-start.4 = (bf16[128,128]{1,0:T(8,128)(2,1)S(1)}, bf16[128,128]{1,0:T(8,128)(2,1)}, u32[]{:S(2)}) copy-start(bf16[128,128]{1,0:T(8,128)(2,1)} %constant.17.clone.band_ref) | copy-start | bytes 98308
  2.5 8.8 %collective-permute-start = (bf16[2,17,4,8,128]{4,3,2,1,0:T(8,128)(2,1)S(1)}, bf16[2,17,4,8,128]{4,3,2,1,0:T(8,128)(2,1)S(1)}, u32[]{:S(2)}, u32[]{:S(2)}) collective-permute-start(bf16[2,17,4,8,128]{4,3,2,1,0:T(8,128)(2,1)S(1)} %get-tuple-element.15.mine_ref), channel_id=1, source_target_pairs={{0,2},{2,0},{1,3},{3,1},{4,6},{6,4},{5,7},{7,5},{8,10},{10,8},{9,1... | collective-permute-start | bytes 835592 | tf_op jit(solution)/shard_map/ppermute | solution.py:568
  4.6 6.1 %collective-permute-start.1 = (bf16[17,4,8,128]{3,2,1,0:T(8,128)(2,1)S(1)}, bf16[17,4,8,128]{3,2,1,0:T(8,128)(2,1)S(1)}, u32[]{:S(2)}, u32[]{:S(2)}) collective-permute-start(bf16[17,4,8,128]{3,2,1,0:T(8,128)(2,1)S(1)} %get-tuple-element.18), channel_id=1, source_target_pairs={{0,4},{4,8},{8,12},{12,0},{1,5},{5,9},{9,13},{13,1},{2,6},{6,10},{... | collective-permute-start | bytes 417800 | tf_op jit(solution)/shard_map/ppermute | solution.py:571
  5.9 9.1 %collective-permute-start.4 = (bf16[17,4,8,128]{3,2,1,0:T(8,128)(2,1)S(1)}, bf16[17,4,8,128]{3,2,1,0:T(8,128)(2,1)S(1)}, u32[]{:S(2)}, u32[]{:S(2)}) collective-permute-start(bf16[17,4,8,128]{3,2,1,0:T(8,128)(2,1)S(1)} %get-tuple-element.21), channel_id=1, source_target_pairs={{0,4},{4,8},{8,12},{12,0},{1,5},{5,9},{9,13},{13,1},{2,6},{6,10},{... | collective-permute-start | bytes 417800 | tf_op jit(solution)/shard_map/ppermute | solution.py:571
  10.7 4.2 %collective-permute-start.2 = (bf16[17,4,8,128]{3,2,1,0:T(8,128)(2,1)S(1)}, bf16[17,4,8,128]{3,2,1,0:T(8,128)(2,1)S(1)}, u32[]{:S(2)}, u32[]{:S(2)}) collective-permute-start(bf16[17,4,8,128]{3,2,1,0:T(8,128)(2,1)S(1)} %collective-permute-done.1), channel_id=1, source_target_pairs={{0,2},{2,0},{1,3},{3,1},{4,6},{6,4},{5,7},{7,5},{8,10},{10,8},{9,1... | collective-permute-start | bytes 417800 | tf_op jit(solution)/shard_map/ppermute | solution.py:568
  16.2 10.7 %copy-start = (bf16[2,256,256]{2,1,0:T(8,128)(2,1)S(1)}, bf16[2,256,256]{2,1,0:T(8,128)(2,1)}, u32[]{:S(2)}) copy-start(bf16[2,256,256]{2,1,0:T(8,128)(2,1)} %constant.16.clone.inverse_ref) | copy-start | bytes 786436
  16.2 5.3 %collective-permute-start.5 = (bf16[2,4,17,8,128]{4,3,2,1,0:T(8,128)(2,1)S(1)}, bf16[2,4,17,8,128]{4,3,2,1,0:T(8,128)(2,1)S(1)}, u32[]{:S(2)}, u32[]{:S(2)}) collective-permute-start(bf16[2,4,17,8,128]{4,3,2,1,0:T(8,128)(2,1)S(1)} %far_spectra.1.far_ref), channel_id=1, source_target_pairs={{0,1},{1,0},{2,3},{3,2},{4,5},{5,4},{6,7},{7,6},{8,9},{9,8},{10,11... | collective-permute-start | bytes 835592 | tf_op jit(solution)/shard_map/ppermute | solution.py:568
  20.3 1.6 %collective-permute-start.3 = (bf16[2,4,17,8,128]{4,3,2,1,0:T(8,128)(2,1)S(1)}, bf16[2,4,17,8,128]{4,3,2,1,0:T(8,128)(2,1)S(1)}, u32[]{:S(2)}, u32[]{:S(2)}) collective-permute-start(bf16[2,4,17,8,128]{4,3,2,1,0:T(8,128)(2,1)S(1)} %get-tuple-element.20.away_ref), channel_id=1, source_target_pairs={{0,1},{1,0},{2,3},{3,2},{4,5},{5,4},{6,7},{7,6},{8,9},{9,8},{10,11... | collective-permute-start | bytes 835592 | tf_op jit(solution)/shard_map/ppermute | solution.py:568
  20.4 6.4 %collective-permute-start.8 = (bf16[2,4,17,8,128]{4,3,2,1,0:T(8,128)(2,1)S(1)}, bf16[2,4,17,8,128]{4,3,2,1,0:T(8,128)(2,1)S(1)}, u32[]{:S(2)}, u32[]{:S(2)}) collective-permute-start(bf16[2,4,17,8,128]{4,3,2,1,0:T(8,128)(2,1)S(1)} %get-tuple-element.19.mine_ref.here_ref), channel_id=1, source_target_pairs={{0,1},{1,0},{2,3},{3,2},{4,5},{5,4},{6,7},{7,6},{8,9},{9,8},{10,11... | collective-permute-start | bytes 835592 | tf_op jit(solution)/shard_map/ppermute | solution.py:568
  22.8 4.0 %copy-start.2 = (s32[1,3]{1,0:T(1,128)S(1)}, s32[1,3]{1,0:T(1,128)}, u32[]{:S(2)}) copy-start(s32[1,3]{1,0:T(1,128)} %mask_ref.5) | copy-start | bytes 40
  22.8 6.6 %collective-permute-start.7 = (bf16[2,17,8,256]{3,2,1,0:T(8,128)(2,1)S(1)}, bf16[2,17,8,256]{3,2,1,0:T(8,128)(2,1)S(1)}, u32[]{:S(2)}, u32[]{:S(2)}) collective-permute-start(bf16[2,17,8,256]{3,2,1,0:T(8,128)(2,1)S(1)} %get-tuple-element.24), channel_id=1, source_target_pairs={{0,0},{1,2},{2,1},{3,3},{4,4},{5,6},{6,5},{7,7},{8,8},{9,10},{10,9... | collective-permute-start | bytes 417800 | tf_op jit(solution)/shard_map/ppermute | solution.py:575
  25.0 6.0 %collective-permute-start.6 = (bf16[2,17,8,256]{3,2,1,0:T(8,128)(2,1)S(1)}, bf16[2,17,8,256]{3,2,1,0:T(8,128)(2,1)S(1)}, u32[]{:S(2)}, u32[]{:S(2)}) collective-permute-start(bf16[2,17,8,256]{3,2,1,0:T(8,128)(2,1)S(1)} %get-tuple-element.23), channel_id=1, source_target_pairs={{0,12},{4,0},{8,4},{12,8},{1,13},{5,1},{9,5},{13,9},{2,14},{6,2},{... | collective-permute-start | bytes 417800 | tf_op jit(solution)/shard_map/ppermute | solution.py:571

commit v4 on v3

--- a/solution.py
+++ b/solution.py
@@ -114,10 +114,9 @@
 
 
 def decimate_kernel(
-    by, place_ref, end_hbm, taps_hbm, rec_hbm, keep_ref, send_ref, *refs
+    by, place_ref, end_hbm, taps_hbm, rec_hbm, keep_ref, send_ref,
+    rec_ref, lhs_ref, taps_ref, end_ref, rec_sem, small_sem,
 ):
-    rec_ref, lhs_ref, taps_ref, end_ref, rec_sem, small_sem = refs[-6:]
-    whole_ref = refs[0] if len(refs) == 7 else None
     channels, windows, length = rec_ref.shape
     half = channels // 2
     rows = half * windows
@@ -177,22 +176,18 @@
             (((1,), (1,)), ((), ())),
             preferred_element_type=F32,
         )
-        out = out.reshape(blocks + 1, half, windows, LANES).astype(BF16)
-        out_ref[...] = out
-        if whole_ref is not None:
-            whole_ref[place_ref[by] if h == 0 else 1 - place_ref[by]] = out
-
-
-def decimate(records, filter_taps, segment_end, place, by, whole):
+        out_ref[...] = out.reshape(blocks + 1, half, windows, LANES).astype(BF16)
+
+
+def decimate(records, filter_taps, segment_end, place, by):
     channels, windows, length = records.shape
     blocks = length // BLOCK
     piece = jax.ShapeDtypeStruct((blocks + 1, channels // 2, windows, LANES), BF16)
-    both = jax.ShapeDtypeStruct((2, *piece.shape), BF16)
     return pl.pallas_call(
         functools.partial(decimate_kernel, by),
-        out_shape=(piece, piece, both) if whole else (piece, piece),
+        out_shape=(piece, piece),
         in_specs=[pl.BlockSpec(memory_space=pltpu.SMEM)] + [pl.BlockSpec(memory_space=pltpu.HBM)] * 3,
-        out_specs=(pl.BlockSpec(memory_space=VMEM),) * (3 if whole else 2),
+        out_specs=(pl.BlockSpec(memory_space=VMEM),) * 2,
         scratch_shapes=[
             VMEM(records.shape, BF16),
             VMEM((2, blocks + 1, channels // 2 * windows, BLOCK + LANES), BF16),
@@ -475,15 +470,20 @@
     write_out(lag_ref, out_ref, offset, sem)
 
 
-def own_spectra_kernel(place_ref, mine_ref, theirs_ref, twist_ref, dft_ref, band_ref, away_ref, here_ref, *work):
+def own_spectra_kernel(
+    place_ref, keep_ref, send_ref, their_keep_ref, their_send_ref, twist_ref, dft_ref, band_ref, white_ref, *work
+):
     flags = flags_of(place_ref, 2)
-    for side, white_ref in ((1 - place_ref[1], away_ref), (place_ref[1], here_ref)):
-
-        def load(s, r, g, side=side):
-            return (mine_ref, theirs_ref)[s][side, r, g]
-
-        def store(part, g, q, value, white_ref=white_ref):
-            white_ref[part, g, q] = value
+    for at, side in enumerate((1 - place_ref[1], place_ref[1])):
+        kept = side == place_ref[0]
+
+        def load(s, r, g, kept=kept):
+            if s == 0:
+                return jnp.where(kept, keep_ref[r, g], send_ref[r, g])
+            return jnp.where(kept, their_send_ref[r, g], their_keep_ref[r, g])
+
+        def store(part, g, q, value, at=at):
+            white_ref[at, part, g, q] = value
 
         spectra(load, flags, (twist_ref, dft_ref, band_ref), work, store)
 
@@ -498,61 +498,80 @@
     spectra(load, flags_of(place_ref, 2), (twist_ref, dft_ref, band_ref), work, store)
 
 
-def far_cross_kernel(mine_ref, theirs_ref, far_ref, fars_ref, across_ref, back_ref):
-    own, far = (mine_ref, theirs_ref), (far_ref, fars_ref)
+def far_cross_kernel(white_ref, others_ref, far_ref, fars_ref, back_ref):
+    own, far = (white_ref.at[1], others_ref.at[0]), (far_ref, fars_ref)
     for q in range(RESIDUES):
-        rows = cross_rows(4, 4, 2, lambda w, p, i: own[w][p, i, q], lambda w, p, j: far[w][p, j, q])
+        rows = cross_rows(4, 4, 2, lambda w, p, j: far[w][p, j, q], lambda w, p, i: own[w][p, i, q])
         for group, parts in enumerate(rows):
             for part, value in enumerate(parts):
                 at = slice(part * LANES, (part + 1) * LANES)
-                value = value.astype(BF16)
-                across_ref[group, q, :, at] = value
-                back_ref[group, q, :, at] = value if part == 0 else -value
+                back_ref[group, q, :, at] = value.astype(BF16)
 
 
 def near_pairs_kernel(
-    offset, scale, place_ref, mask_ref, away_ref, here_ref, others_here_ref, others_away_ref,
-    twist_ref, inverse_ref, out_ref, own_ref, high_ref, low_ref, sum_ref, lag_ref, sem,
+    offset, scale, place_ref, mask_ref, white_ref, others_ref,
+    twist_ref, inverse_ref, lag_ref, own_ref, high_ref, low_ref, sum_ref,
 ):
     same = place_ref[0] == place_ref[1]
 
     @pl.when(same)
     def _():
-        own_ref[0] = here_ref[...]
-        own_ref[1] = others_away_ref[...]
+        own_ref[0] = white_ref[1]
+        own_ref[1] = others_ref[0]
 
     @pl.when(jnp.logical_not(same))
     def _():
-        own_ref[0] = away_ref[...]
-        own_ref[1] = others_here_ref[...]
-
-    half = (here_ref, others_away_ref)
+        own_ref[0] = white_ref[0]
+        own_ref[1] = others_ref[1]
+
+    half = (white_ref.at[1], others_ref.at[0])
     correlate(
         lambda w, p, i, q: own_ref[w, p, i, q],
         lambda w, p, j, q: half[w][p, j, q],
         2, 4, 4, (twist_ref, inverse_ref), (high_ref, low_ref, sum_ref),
         mask_ref[0, offset].astype(F32) * scale, lag_ref,
     )
-    write_out(lag_ref, out_ref, offset, sem)
-
-
-def lags_kernel(offset, scale, mirrored, mask_ref, cross_ref, twist_ref, inverse_ref, _, out_ref, sum_ref, lag_ref, sem):
+
+
+def lag_sums(cross_ref, inverse_ref, sum_ref, conjugate=False):
     rows = cross_ref[...].reshape(2 * RESIDUES * SUB, 2 * LANES)
+    if conjugate:
+        rows = jnp.concatenate([rows[:, :LANES], -rows[:, LANES:]], axis=1)
     total = jnp.dot(rows, inverse_ref[0], preferred_element_type=F32) + jnp.dot(
         rows, inverse_ref[1], preferred_element_type=F32
     )
     sum_ref[...] = total.reshape(2, RESIDUES, SUB, 2 * LANES)
+
+
+def across_lags_kernel(offset, scale, mask_ref, cross_ref, twist_ref, inverse_ref, lag_ref, sum_ref):
+    lag_sums(cross_ref, inverse_ref, sum_ref, True)
     weight = mask_ref[0, offset].astype(F32) * scale
     for group in range(2):
         for place, value in enumerate(lag_rows_of(sum_ref, group, twist_ref, weight)):
-            at = slice(place * LANES, (place + 1) * LANES)
-            if mirrored:
-                for row in range(SUB):
-                    lag_ref[row % 4, group * 2 + row // 4, at] = value[row]
-            else:
-                for j in range(2):
-                    lag_ref[group * 2 + j, :, at] = value[4 * j : 4 * j + 4]
-    write_out(lag_ref, out_ref, offset, sem)
+            for row in range(SUB):
+                lag_ref[row % 4, group * 2 + row // 4, place * LANES : (place + 1) * LANES] = value[row]
+
+
+def back_lags_kernel(
+    scale, mask_ref, cross_ref, near_ref, across_ref, twist_ref, inverse_ref, out_ref, sum_ref, lag_ref, sem
+):
+    copies = [
+        pltpu.make_async_copy(across_ref, out_ref.at[0], sem.at[0]),
+        pltpu.make_async_copy(near_ref, out_ref.at[1], sem.at[1]),
+    ]
+    for copy in copies:
+        copy.start()
+    lag_sums(cross_ref, inverse_ref, sum_ref)
+    weight = mask_ref[0, 2].astype(F32) * scale
+    for group in range(2):
+        for place, value in enumerate(lag_rows_of(sum_ref, group, twist_ref, weight)):
+            for j in range(2):
+                lag_ref[group * 2 + j, :, place * LANES : (place + 1) * LANES] = value[4 * j : 4 * j + 4]
+        half = pl.ds(2 * group, 2)
+        copies.append(pltpu.make_async_copy(lag_ref.at[half], out_ref.at[2, half], sem.at[2 + group]))
+        copies[-1].start()
+    for copy in copies:
+        copy.wait()
 
 
 def mirrored(records, filter_taps, segment_end, pair_mask, place, tables, scale):
@@ -562,7 +581,6 @@
     blocks = lax.axis_size("chan")
     white = jax.ShapeDtypeStruct((2, 4, RESIDUES, SUB, LANES), BF16)
     spec = jax.ShapeDtypeStruct((2, RESIDUES, SUB, 2 * LANES), BF16)
-    shape = jax.ShapeDtypeStruct((3, 4, 4, 2 * MAXLAG), F32)
 
     def exchange(array, axis):
         return lax.ppermute(array, axis, [(0, 1), (1, 0)])
@@ -574,21 +592,21 @@
         pairs = [(0, 0), (1, 2), (2, 1), (3, 3)]
         return lax.ppermute(array, ("tm", "win"), pairs)
 
-    keep, send, both = decimate(records, filter_taps, segment_end, place, 0, True)
+    keep, send = decimate(records, filter_taps, segment_end, place, 0)
     far_send, far_keep = along(send, 1), along(keep, 1)
-    theirs = exchange(both, "tm")
+    their_send, their_keep = exchange(send, "tm"), exchange(keep, "tm")
     relayed = exchange(far_send, "tm")
-    away, here = pl.pallas_call(
+    own = pl.pallas_call(
         own_spectra_kernel,
-        out_shape=(white, white),
-        in_specs=[smem] + [vmem] * 5,
-        out_specs=(vmem, vmem),
+        out_shape=jax.ShapeDtypeStruct((2, *white.shape), BF16),
+        in_specs=[smem] + [vmem] * 7,
+        out_specs=vmem,
         scratch_shapes=spectra_work(4),
         name="own_spectra",
         **params(COST[0]),
-    )(place, both, theirs, twist, dft, band)
-    (away, here), relayed = lax.optimization_barrier(((away, here), relayed))
-    others_away, others_here = exchange(away, "win"), exchange(here, "win")
+    )(place, keep, send, their_keep, their_send, twist, dft, band)
+    own, relayed = lax.optimization_barrier((own, relayed))
+    others = exchange(own, "win")
     far = pl.pallas_call(
         far_spectra_kernel,
         out_shape=white,
@@ -599,36 +617,43 @@
         **params(COST[1]),
     )(place, far_keep, relayed, twist, dft, band)
     fars = exchange(far, "win")
-    crossed, back = pl.pallas_call(
+    cross = pl.pallas_call(
         far_cross_kernel,
-        out_shape=(spec, spec),
+        out_shape=spec,
         in_specs=[vmem] * 4,
-        out_specs=(vmem, vmem),
+        out_specs=vmem,
         name="far_cross",
         **params(COST[2]),
-    )(here, others_away, far, fars)
-    crossed, back = across(crossed), along(back, -1)
-    out = pl.pallas_call(
+    )(own, others, far, fars)
+    back, crossed = along(cross, -1), across(cross)
+    lag = jax.ShapeDtypeStruct((4, 4, 2 * MAXLAG), F32)
+    near = pl.pallas_call(
         functools.partial(near_pairs_kernel, 1, scale),
-        out_shape=shape,
-        in_specs=[smem, smem] + [vmem] * 6,
-        out_specs=anywhere,
-        scratch_shapes=[VMEM((2, 2, 4, RESIDUES, SUB, LANES), BF16)] + lag_work(4, 4),
+        out_shape=lag,
+        in_specs=[smem, smem] + [vmem] * 4,
+        out_specs=vmem,
+        scratch_shapes=[VMEM((2, 2, 4, RESIDUES, SUB, LANES), BF16)] + lag_work(4, 4)[:3],
         name="near_pairs",
         **params(COST[3]),
-    )(place, pair_mask, away, here, others_here, others_away, twist, inverse)
-    for offset, cross in ((0, crossed), (2, back)):
-        out = pl.pallas_call(
-            functools.partial(lags_kernel, offset, scale, offset == 2),
-            out_shape=shape,
-            in_specs=[smem] + [vmem] * 3 + [anywhere],
-            out_specs=anywhere,
-            scratch_shapes=lag_work(4, 4)[2:],
-            input_output_aliases={4: 0},
-            name="lags",
-            **params(COST[4]),
-        )(pair_mask, cross, twist, inverse, out)
-    return out
+    )(place, pair_mask, own, others, twist, inverse)
+    side = pl.pallas_call(
+        functools.partial(across_lags_kernel, 0, scale),
+        out_shape=lag,
+        in_specs=[smem] + [vmem] * 3,
+        out_specs=vmem,
+        scratch_shapes=lag_work(4, 4)[2:3],
+        name="across_lags",
+        **params(COST[4]),
+    )(pair_mask, crossed, twist, inverse)
+    return pl.pallas_call(
+        functools.partial(back_lags_kernel, scale),
+        out_shape=jax.ShapeDtypeStruct((3, 4, 4, 2 * MAXLAG), F32),
+        in_specs=[smem] + [vmem] * 5,
+        out_specs=anywhere,
+        scratch_shapes=lag_work(4, 4)[2:4] + [pltpu.SemaphoreType.DMA((4,))],
+        name="back_lags",
+        **params(COST[4]),
+    )(pair_mask, back, near, side, twist, inverse)
 
 
 def spectra_work(groups):
@@ -683,7 +708,7 @@
 
     if span == 2 and reach == 1 and groups == 4:
         return mirrored(records, filter_taps, segment_end, pair_mask, place, (twist, dft, inverse, band), scale)
-    keep, send = decimate(records, filter_taps, segment_end, place, 1, False)
+    keep, send = decimate(records, filter_taps, segment_end, place, 1)
     received = permute(send, "win", 1)
     block = join(keep, received)
     up = down = block

time: 32.9 us -> 31.2 us (0.948)
  Pallas kernels: 12.7 us -> 11.3 us
  waiting for transfers between devices: 6.01 us -> 5.54 us
    ppermute x5, starting transfers between devices: 7.23 us -> 4.43 us  [exchange(): return lax.ppermute(array, axis, [(0, 1), (1, 0)])]
    ppermute x3, starting transfers between devices: 4.43 us -> 6.24 us  [along(): lax.ppermute(array, 'chan', [(i, (i + by) % blocks) for i in range(blocks)])]
    ppermute x1, starting transfers between devices: 2.17 us -> 3.37 us  [across(): return lax.ppermute(array, ('tm', 'win'), pairs)]
    ppermute x3, waiting for transfers between devices: 3.56 us -> 2.65 us  [along(): lax.ppermute(array, 'chan', [(i, (i + by) % blocks) for i in range(blocks)])]
    pallas_call x1, Pallas kernels: 2.49 us -> 1.79 us  [mirrored(): pl.pallas_call(functools.partial(near_pairs_kernel, 1, scale), out_shape=...]
    pallas_call x4, Pallas kernels: 6.55 us -> 5.87 us  [the longest x1 2.49 us: mirrored(): pl.pallas_call(own_spectra_kernel, out_shape=jax.ShapeDtypeStruct((2, *wh...]
    ppermute x5, waiting for transfers between devices: 2.33 us -> 2.88 us  [exchange(): return lax.ppermute(array, axis, [(0, 1), (1, 0)])]
  transfers between devices with their start and end apart: 9 -> 9, of which waited for: 5 -> 4; matrix products, arithmetic and copies ran while one was open for 0% -> 0% of each run, Pallas kernels for 23% -> 21%
where the time goes in v4:
time: 31.2 us; the launch traced here: 31.1 us
  starting transfers between devices  14 us (45%)
  Pallas kernels  11.3 us (36%)
  waiting for transfers between devices  5.54 us (18%)
    ppermute x3, starting transfers between devices, along(): lax.ppermute(array, 'chan', [(i, (i + by) % blocks) for i in range(blocks)])  6.24 us
    ppermute x5, starting transfers between devices, exchange(): return lax.ppermute(array, axis, [(0, 1), (1, 0)])  4.43 us
    ppermute x1, starting transfers between devices, across(): return lax.ppermute(array, ('tm', 'win'), pairs)  3.37 us
    ppermute x5, waiting for transfers between devices, exchange(): return lax.ppermute(array, axis, [(0, 1), (1, 0)])  2.88 us
    ppermute x3, waiting for transfers between devices, along(): lax.ppermute(array, 'chan', [(i, (i + by) % blocks) for i in range(blocks)])  2.65 us
    pallas_call x1, Pallas kernels, mirrored(): pl.pallas_call(own_spectra_kernel, out_shape=jax.ShapeDtypeStruct((2, *wh...  2.49 us
    pallas_call x1, Pallas kernels, decimate(): pl.pallas_call(functools.partial(decimate_kernel, by), out_shape=(piece,...  2.37 us
    pallas_call x1, Pallas kernels, mirrored(): pl.pallas_call(functools.partial(near_pairs_kernel, 1, scale), out_shape=...  1.79 us
  transfers between devices with their start and end apart: 9, of which 4 were waited for; matrix products, arithmetic and copies ran while one was open for 0% of the time, Pallas kernels for 21%

profile of v4, /device:TPU:1, one launch (start us, length us, event | category | flops | bytes accessed | tf_op | source)
XLA Modules:
  0.0 31.1 jit_solution(7524250432081761977)
XLA Ops:
  0.0 0.1 pad_add_fusion.place_ref
  0.1 2.4 %decimate.1 = (bf16[17,4,8,128]{3,2,1,0:T(8,128)(2,1)S(1)}, bf16[17,4,8,128]{3,2,1,0:T(8,128)(2,1)S(1)}) custom-call(s32[2]{0:T(128)S(1)} %pad_add_fusion.place_ref, s32[8]{0:T(128)} %end_hbm.1, bf16[1,64]{1,0:T(2,128)(2,1)} %bitcast.3, bf16[8,8,8192]{2,1,0:T(8,128)(2,1)} %rec_hbm.1), custom_call_target="tpu_custom_call" | custom-call | flops 134217728 | bytes 1572864 | tf_op jit(solution)/shard_map/decimate/pallas_call | solution.py:186
  2.5 2.2 %collective-permute-start.2 = (bf16[17,4,8,128]{3,2,1,0:T(8,128)(2,1)S(1)}, bf16[17,4,8,128]{3,2,1,0:T(8,128)(2,1)S(1)}, u32[]{:S(2)}, u32[]{:S(2)}) collective-permute-start(bf16[17,4,8,128]{3,2,1,0:T(8,128)(2,1)S(1)} %get-tuple-element.10.send_ref), channel_id=1, source_target_pairs={{0,4},{4,8},{8,12},{12,0},{1,5},{5,9},{9,13},{13,1},{2,6},{6,10},{... | collective-permute-start | bytes 417800 | tf_op jit(solution)/shard_map/ppermute | solution.py:589
  4.6 1.2 %collective-permute-start = (bf16[17,4,8,128]{3,2,1,0:T(8,128)(2,1)S(1)}, bf16[17,4,8,128]{3,2,1,0:T(8,128)(2,1)S(1)}, u32[]{:S(2)}, u32[]{:S(2)}) collective-permute-start(bf16[17,4,8,128]{3,2,1,0:T(8,128)(2,1)S(1)} %get-tuple-element.9.keep_ref), channel_id=1, source_target_pairs={{0,2},{2,0},{1,3},{3,1},{4,6},{6,4},{5,7},{7,5},{8,10},{10,8},{9,1... | collective-permute-start | bytes 417800 | tf_op jit(solution)/shard_map/ppermute | solution.py:586
  5.9 0.3 collective-permute-start.1
  6.1 1.3 %collective-permute-start.5 = (bf16[17,4,8,128]{3,2,1,0:T(8,128)(2,1)S(1)}, bf16[17,4,8,128]{3,2,1,0:T(8,128)(2,1)S(1)}, u32[]{:S(2)}, u32[]{:S(2)}) collective-permute-start(bf16[17,4,8,128]{3,2,1,0:T(8,128)(2,1)S(1)} %get-tuple-element.9.keep_ref), channel_id=1, source_target_pairs={{0,4},{4,8},{8,12},{12,0},{1,5},{5,9},{9,13},{13,1},{2,6},{6,10},{... | collective-permute-start | bytes 417800 | tf_op jit(solution)/shard_map/ppermute | solution.py:589
  7.4 2.6 %collective-permute-done.2 = bf16[17,4,8,128]{3,2,1,0:T(8,128)(2,1)S(1)} collective-permute-done((bf16[17,4,8,128]{3,2,1,0:T(8,128)(2,1)S(1)}, bf16[17,4,8,128]{3,2,1,0:T(8,128)(2,1)S(1)}, u32[]{:S(2)}, u32[]{:S(2)}) %collective-permute-start.2) | collective-permute-done | bytes 139296 | tf_op jit(solution)/shard_map/ppermute | solution.py:589
  10.1 1.0 %collective-permute-start.3 = (bf16[17,4,8,128]{3,2,1,0:T(8,128)(2,1)S(1)}, bf16[17,4,8,128]{3,2,1,0:T(8,128)(2,1)S(1)}, u32[]{:S(2)}, u32[]{:S(2)}) collective-permute-start(bf16[17,4,8,128]{3,2,1,0:T(8,128)(2,1)S(1)} %collective-permute-done.2), channel_id=1, source_target_pairs={{0,2},{2,0},{1,3},{3,1},{4,6},{6,4},{5,7},{7,5},{8,10},{10,8},{9,1... | collective-permute-start | bytes 417800 | tf_op jit(solution)/shard_map/ppermute | solution.py:586
  11.0 0.0 collective-permute-done.their_keep_ref
  11.0 0.8 %collective-permute-done.1.their_send_ref = bf16[17,4,8,128]{3,2,1,0:T(8,128)(2,1)S(1)} collective-permute-done((bf16[17,4,8,128]{3,2,1,0:T(8,128)(2,1)S(1)}, bf16[17,4,8,128]{3,2,1,0:T(8,128)(2,1)S(1)}, u32[]{:S(2)}, u32[]{:S(2)}) %collective-permute-start.1) | collective-permute-done | bytes 139296 | tf_op jit(solution)/shard_map/ppermute | solution.py:586
  11.9 2.5 %own_spectra.1.white_ref = bf16[2,2,4,17,8,128]{5,4,3,2,1,0:T(8,128)(2,1)S(1)} custom-call(s32[2]{0:T(128)S(1)} %pad_add_fusion.place_ref, bf16[17,4,8,128]{3,2,1,0:T(8,128)(2,1)S(1)} %get-tuple-element.9.keep_ref, bf16[17,4,8,128]{3,2,1,0:T(8,128)(2,1)S(1)} %get-tuple-element.10.send_ref, bf16[17,4,8,128]{3,2,1,0:T(8,128)(2,1)S(1)} %collective-permute-done.their_keep_ref, ...), custom_call_target="tpu_custom_call" | custom-call | flops 5000000000 | bytes 1024 | tf_op jit(solution)/shard_map/own_spectra/pallas_call | solution.py:599
  14.4 0.5 %collective-permute-done.3.relayed_ref = bf16[17,4,8,128]{3,2,1,0:T(8,128)(2,1)S(1)} collective-permute-done((bf16[17,4,8,128]{3,2,1,0:T(8,128)(2,1)S(1)}, bf16[17,4,8,128]{3,2,1,0:T(8,128)(2,1)S(1)}, u32[]{:S(2)}, u32[]{:S(2)}) %collective-permute-start.3) | collective-permute-done | bytes 139296 | tf_op jit(solution)/shard_map/ppermute | solution.py:586
  14.9 1.9 %collective-permute-start.4 = (bf16[2,2,4,17,8,128]{5,4,3,2,1,0:T(8,128)(2,1)S(1)}, bf16[2,2,4,17,8,128]{5,4,3,2,1,0:T(8,128)(2,1)S(1)}, u32[]{:S(2)}, u32[]{:S(2)}) collective-permute-start(bf16[2,2,4,17,8,128]{5,4,3,2,1,0:T(8,128)(2,1)S(1)} %own_spectra.1.white_ref), channel_id=1, source_target_pairs={{0,1},{1,0},{2,3},{3,2},{4,5},{5,4},{6,7},{7,6},{8,9},{9,8},{10,11... | collective-permute-start | bytes 1671176 | tf_op jit(solution)/shard_map/ppermute | solution.py:586
  16.8 1.3 %far_spectra.1.far_ref = bf16[2,4,17,8,128]{4,3,2,1,0:T(8,128)(2,1)S(1)} custom-call(s32[2]{0:T(128)S(1)} %pad_add_fusion.place_ref, bf16[17,4,8,128]{3,2,1,0:T(8,128)(2,1)S(1)} %collective-permute-done.5.mine_ref, bf16[17,4,8,128]{3,2,1,0:T(8,128)(2,1)S(1)} %collective-permute-done.3.relayed_ref, f32[2,17,8,128]{3,2,1,0:T(8,128)S(1)} %copy-done.3, ...), custom_call_target="tpu_custom_call" | custom-call | flops 5000000000 | bytes 1024 | tf_op jit(solution)/shard_map/far_spectra/pallas_call | solution.py:610
  18.1 0.0 copy-start
  18.1 0.0 copy-start.1
  18.1 0.1 collective-permute-start.6
  18.2 1.5 %collective-permute-done.6.fars_ref = bf16[2,4,17,8,128]{4,3,2,1,0:T(8,128)(2,1)S(1)} collective-permute-done((bf16[2,4,17,8,128]{4,3,2,1,0:T(8,128)(2,1)S(1)}, bf16[2,4,17,8,128]{4,3,2,1,0:T(8,128)(2,1)S(1)}, u32[]{:S(2)}, u32[]{:S(2)}) %collective-permute-start.6) | collective-permute-done | bytes 278560 | tf_op jit(solution)/shard_map/ppermute | solution.py:586
  19.7 0.9 %far_cross.1 = bf16[2,17,8,256]{3,2,1,0:T(8,128)(2,1)S(1)} custom-call(bf16[2,2,4,17,8,128]{5,4,3,2,1,0:T(8,128)(2,1)S(1)} %own_spectra.1.white_ref, bf16[2,2,4,17,8,128]{5,4,3,2,1,0:T(8,128)(2,1)S(1)} %collective-permute-done.4.others_ref, bf16[2,4,17,8,128]{4,3,2,1,0:T(8,128)(2,1)S(1)} %far_spectra.1.far_ref, ...), custom_call_target="tpu_custom_call" | custom-call | flops 500000000 | bytes 1024 | tf_op jit(solution)/shard_map/far_cross/pallas_call | solution.py:620
  20.6 3.4 %collective-permute-start.8 = (bf16[2,17,8,256]{3,2,1,0:T(8,128)(2,1)S(1)}, bf16[2,17,8,256]{3,2,1,0:T(8,128)(2,1)S(1)}, u32[]{:S(2)}, u32[]{:S(2)}) collective-permute-start(bf16[2,17,8,256]{3,2,1,0:T(8,128)(2,1)S(1)} %far_cross.1), channel_id=1, source_target_pairs={{0,0},{1,2},{2,1},{3,3},{4,4},{5,6},{6,5},{7,7},{8,8},{9,10},{10,9... | collective-permute-start | bytes 417800 | tf_op jit(solution)/shard_map/ppermute | solution.py:593
  24.0 2.8 %collective-permute-start.7 = (bf16[2,17,8,256]{3,2,1,0:T(8,128)(2,1)S(1)}, bf16[2,17,8,256]{3,2,1,0:T(8,128)(2,1)S(1)}, u32[]{:S(2)}, u32[]{:S(2)}) collective-permute-start(bf16[2,17,8,256]{3,2,1,0:T(8,128)(2,1)S(1)} %far_cross.1), channel_id=1, source_target_pairs={{0,12},{4,0},{8,4},{12,8},{1,13},{5,1},{9,5},{13,9},{2,14},{6,2},{... | collective-permute-start | bytes 417800 | tf_op jit(solution)/shard_map/ppermute | solution.py:589
  26.8 1.8 %near_pairs.1.near_ref = f32[4,4,3840]{2,1,0:T(4,128)S(1)} custom-call(s32[2]{0:T(128)S(1)} %pad_add_fusion.place_ref, s32[1,3]{1,0:T(1,128)S(1)} %copy-done, bf16[2,2,4,17,8,128]{5,4,3,2,1,0:T(8,128)(2,1)S(1)} %own_spectra.1.white_ref, bf16[2,2,4,17,8,128]{5,4,3,2,1,0:T(8,128)(2,1)S(1)} %collective-permute-done.4.others_ref, ...), custom_call_target="tpu_custom_call" | custom-call | flops 500000000 | bytes 1024 | tf_op jit(solution)/shard_map/near_pairs/pallas_call | solution.py:630
  28.6 0.9 %across_lags.1.across_ref = f32[4,4,3840]{2,1,0:T(4,128)S(1)} custom-call(s32[1,3]{1,0:T(1,128)S(1)} %copy-done, bf16[2,17,8,256]{3,2,1,0:T(8,128)(2,1)S(1)} %collective-permute-done.8.cross_ref, f32[2,17,8,128]{3,2,1,0:T(8,128)S(1)} %copy-done.3, bf16[2,256,256]{2,1,0:T(8,128)(2,1)S(1)} %copy-done.1), custom_call_target="tpu_custom_call" | custom-call | flops 500000000 | bytes 1024 | tf_op jit(solution)/shard_map/across_lags/pallas_call | solution.py:639
  29.5 1.5 %back_lags.1 = f32[3,4,4,3840]{3,2,1,0:T(4,128)} custom-call(s32[1,3]{1,0:T(1,128)S(1)} %copy-done, bf16[2,17,8,256]{3,2,1,0:T(8,128)(2,1)S(1)} %collective-permute-done.7.cross_ref, f32[4,4,3840]{2,1,0:T(4,128)S(1)} %near_pairs.1.near_ref, f32[4,4,3840]{2,1,0:T(4,128)S(1)} %across_lags.1.across_ref, f32[2,17,8,128]{3,2,1,0:T(8,128)S(1)} %copy-done.3, ...), custom_call_target="tpu_custom_call" | custom-call | flops 500000000 | bytes 1024 | tf_op jit(solution)/shard_map/back_lags/pallas_call | solution.py:648
  (12 shorter events, 0.0 us)
Async XLA Ops:
  0.1 11.8 %copy-start.2 = (bf16[2,256,256]{2,1,0:T(8,128)(2,1)S(1)}, bf16[2,256,256]{2,1,0:T(8,128)(2,1)}, u32[]{:S(2)}) copy-start(bf16[2,256,256]{2,1,0:T(8,128)(2,1)} %constant.15.clone.dft_ref) | copy-start | bytes 786436
  0.1 11.8 %copy-start.3 = (f32[2,17,8,128]{3,2,1,0:T(8,128)S(1)}, f32[2,17,8,128]{3,2,1,0:T(8,128)}, u32[]{:S(2)}) copy-start(f32[2,17,8,128]{3,2,1,0:T(8,128)} %constant.14.clone.twist_ref) | copy-start | bytes 417796
  0.1 11.8 %copy-start.4 = (bf16[128,128]{1,0:T(8,128)(2,1)S(1)}, bf16[128,128]{1,0:T(8,128)(2,1)}, u32[]{:S(2)}) copy-start(bf16[128,128]{1,0:T(8,128)(2,1)} %constant.17.clone.band_ref) | copy-start | bytes 98308
  2.5 7.6 %collective-permute-start.2 = (bf16[17,4,8,128]{3,2,1,0:T(8,128)(2,1)S(1)}, bf16[17,4,8,128]{3,2,1,0:T(8,128)(2,1)S(1)}, u32[]{:S(2)}, u32[]{:S(2)}) collective-permute-start(bf16[17,4,8,128]{3,2,1,0:T(8,128)(2,1)S(1)} %get-tuple-element.10.send_ref), channel_id=1, source_target_pairs={{0,4},{4,8},{8,12},{12,0},{1,5},{5,9},{9,13},{13,1},{2,6},{6,10},{... | collective-permute-start | bytes 417800 | tf_op jit(solution)/shard_map/ppermute | solution.py:589
  4.6 6.4 %collective-permute-start = (bf16[17,4,8,128]{3,2,1,0:T(8,128)(2,1)S(1)}, bf16[17,4,8,128]{3,2,1,0:T(8,128)(2,1)S(1)}, u32[]{:S(2)}, u32[]{:S(2)}) collective-permute-start(bf16[17,4,8,128]{3,2,1,0:T(8,128)(2,1)S(1)} %get-tuple-element.9.keep_ref), channel_id=1, source_target_pairs={{0,2},{2,0},{1,3},{3,1},{4,6},{6,4},{5,7},{7,5},{8,10},{10,8},{9,1... | collective-permute-start | bytes 417800 | tf_op jit(solution)/shard_map/ppermute | solution.py:586
  5.9 6.0 %collective-permute-start.1 = (bf16[17,4,8,128]{3,2,1,0:T(8,128)(2,1)S(1)}, bf16[17,4,8,128]{3,2,1,0:T(8,128)(2,1)S(1)}, u32[]{:S(2)}, u32[]{:S(2)}) collective-permute-start(bf16[17,4,8,128]{3,2,1,0:T(8,128)(2,1)S(1)} %get-tuple-element.10.send_ref), channel_id=1, source_target_pairs={{0,2},{2,0},{1,3},{3,1},{4,6},{6,4},{5,7},{7,5},{8,10},{10,8},{9,1... | collective-permute-start | bytes 417800 | tf_op jit(solution)/shard_map/ppermute | solution.py:586
  6.1 10.7 %collective-permute-start.5 = (bf16[17,4,8,128]{3,2,1,0:T(8,128)(2,1)S(1)}, bf16[17,4,8,128]{3,2,1,0:T(8,128)(2,1)S(1)}, u32[]{:S(2)}, u32[]{:S(2)}) collective-permute-start(bf16[17,4,8,128]{3,2,1,0:T(8,128)(2,1)S(1)} %get-tuple-element.9.keep_ref), channel_id=1, source_target_pairs={{0,4},{4,8},{8,12},{12,0},{1,5},{5,9},{9,13},{13,1},{2,6},{6,10},{... | collective-permute-start | bytes 417800 | tf_op jit(solution)/shard_map/ppermute | solution.py:589
  10.1 4.8 %collective-permute-start.3 = (bf16[17,4,8,128]{3,2,1,0:T(8,128)(2,1)S(1)}, bf16[17,4,8,128]{3,2,1,0:T(8,128)(2,1)S(1)}, u32[]{:S(2)}, u32[]{:S(2)}) collective-permute-start(bf16[17,4,8,128]{3,2,1,0:T(8,128)(2,1)S(1)} %collective-permute-done.2), channel_id=1, source_target_pairs={{0,2},{2,0},{1,3},{3,1},{4,6},{6,4},{5,7},{7,5},{8,10},{10,8},{9,1... | collective-permute-start | bytes 417800 | tf_op jit(solution)/shard_map/ppermute | solution.py:586
  14.9 4.8 %collective-permute-start.4 = (bf16[2,2,4,17,8,128]{5,4,3,2,1,0:T(8,128)(2,1)S(1)}, bf16[2,2,4,17,8,128]{5,4,3,2,1,0:T(8,128)(2,1)S(1)}, u32[]{:S(2)}, u32[]{:S(2)}) collective-permute-start(bf16[2,2,4,17,8,128]{5,4,3,2,1,0:T(8,128)(2,1)S(1)} %own_spectra.1.white_ref), channel_id=1, source_target_pairs={{0,1},{1,0},{2,3},{3,2},{4,5},{5,4},{6,7},{7,6},{8,9},{9,8},{10,11... | collective-permute-start | bytes 1671176 | tf_op jit(solution)/shard_map/ppermute | solution.py:586
  18.1 8.7 %copy-start = (s32[1,3]{1,0:T(1,128)S(1)}, s32[1,3]{1,0:T(1,128)}, u32[]{:S(2)}) copy-start(s32[1,3]{1,0:T(1,128)} %mask_ref.5) | copy-start | bytes 40
  18.1 8.7 %copy-start.1 = (bf16[2,256,256]{2,1,0:T(8,128)(2,1)S(1)}, bf16[2,256,256]{2,1,0:T(8,128)(2,1)}, u32[]{:S(2)}) copy-start(bf16[2,256,256]{2,1,0:T(8,128)(2,1)} %constant.16.clone.inverse_ref) | copy-start | bytes 786436
  18.1 1.6 %collective-permute-start.6 = (bf16[2,4,17,8,128]{4,3,2,1,0:T(8,128)(2,1)S(1)}, bf16[2,4,17,8,128]{4,3,2,1,0:T(8,128)(2,1)S(1)}, u32[]{:S(2)}, u32[]{:S(2)}) collective-permute-start(bf16[2,4,17,8,128]{4,3,2,1,0:T(8,128)(2,1)S(1)} %far_spectra.1.far_ref), channel_id=1, source_target_pairs={{0,1},{1,0},{2,3},{3,2},{4,5},{5,4},{6,7},{7,6},{8,9},{9,8},{10,11... | collective-permute-start | bytes 835592 | tf_op jit(solution)/shard_map/ppermute | solution.py:586
  20.6 7.9 %collective-permute-start.8 = (bf16[2,17,8,256]{3,2,1,0:T(8,128)(2,1)S(1)}, bf16[2,17,8,256]{3,2,1,0:T(8,128)(2,1)S(1)}, u32[]{:S(2)}, u32[]{:S(2)}) collective-permute-start(bf16[2,17,8,256]{3,2,1,0:T(8,128)(2,1)S(1)} %far_cross.1), channel_id=1, source_target_pairs={{0,0},{1,2},{2,1},{3,3},{4,4},{5,6},{6,5},{7,7},{8,8},{9,10},{10,9... | collective-permute-start | bytes 417800 | tf_op jit(solution)/shard_map/ppermute | solution.py:593
  24.0 5.5 %collective-permute-start.7 = (bf16[2,17,8,256]{3,2,1,0:T(8,128)(2,1)S(1)}, bf16[2,17,8,256]{3,2,1,0:T(8,128)(2,1)S(1)}, u32[]{:S(2)}, u32[]{:S(2)}) collective-permute-start(bf16[2,17,8,256]{3,2,1,0:T(8,128)(2,1)S(1)} %far_cross.1), channel_id=1, source_target_pairs={{0,12},{4,0},{8,4},{12,8},{1,13},{5,1},{9,5},{13,9},{2,14},{6,2},{... | collective-permute-start | bytes 417800 | tf_op jit(solution)/shard_map/ppermute | solution.py:589

commit v5 on v4

--- a/solution.py
+++ b/solution.py
@@ -367,13 +367,19 @@
         )
         for group, parts in enumerate(rows):
             for part, value in enumerate(parts):
-                high, low = split(value)
-                high_ref[group, q, :, part * LANES : (part + 1) * LANES] = high
-                low_ref[group, q, :, part * LANES : (part + 1) * LANES] = low
+                at = slice(part * LANES, (part + 1) * LANES)
+                if low_ref is None:
+                    high_ref[group, q, :, at] = value.astype(BF16)
+                else:
+                    high_ref[group, q, :, at], low_ref[group, q, :, at] = split(value)
     count = pair_groups * RESIDUES * SUB
-    total = three_pass(
-        high_ref[...].reshape(count, 2 * LANES), low_ref[...].reshape(count, 2 * LANES), inverse_ref
-    )
+    rows = high_ref[...].reshape(count, 2 * LANES)
+    if low_ref is None:
+        total = jnp.dot(rows, inverse_ref[0], preferred_element_type=F32) + jnp.dot(
+            rows, inverse_ref[1], preferred_element_type=F32
+        )
+    else:
+        total = three_pass(rows, low_ref[...].reshape(count, 2 * LANES), inverse_ref)
     sum_ref[...] = total.reshape(pair_groups, RESIDUES, SUB, 2 * LANES)
     per = SUB // owned
     for group in range(pair_groups):
@@ -510,7 +516,7 @@
 
 def near_pairs_kernel(
     offset, scale, place_ref, mask_ref, white_ref, others_ref,
-    twist_ref, inverse_ref, lag_ref, own_ref, high_ref, low_ref, sum_ref,
+    twist_ref, inverse_ref, lag_ref, own_ref, high_ref, sum_ref,
 ):
     same = place_ref[0] == place_ref[1]
 
@@ -528,7 +534,7 @@
     correlate(
         lambda w, p, i, q: own_ref[w, p, i, q],
         lambda w, p, j, q: half[w][p, j, q],
-        2, 4, 4, (twist_ref, inverse_ref), (high_ref, low_ref, sum_ref),
+        2, 4, 4, (twist_ref, inverse_ref), (high_ref, None, sum_ref),
         mask_ref[0, offset].astype(F32) * scale, lag_ref,
     )
 
@@ -632,7 +638,7 @@
         out_shape=lag,
         in_specs=[smem, smem] + [vmem] * 4,
         out_specs=vmem,
-        scratch_shapes=[VMEM((2, 2, 4, RESIDUES, SUB, LANES), BF16)] + lag_work(4, 4)[:3],
+        scratch_shapes=[VMEM((2, 2, 4, RESIDUES, SUB, LANES), BF16)] + lag_work(4, 4)[1:3],
         name="near_pairs",
         **params(COST[3]),
     )(place, pair_mask, own, others, twist, inverse)

time: 31.2 us -> 31.1 us (level)
  no operation moved by 1% of the time
where the time goes in v5:
time: 31.1 us; the launch traced here: 31 us
  starting transfers between devices  14 us (45%)
  Pallas kernels  11.2 us (36%)
  waiting for transfers between devices  5.54 us (18%)
    ppermute x3, starting transfers between devices, along(): lax.ppermute(array, 'chan', [(i, (i + by) % blocks) for i in range(blocks)])  6.24 us
    ppermute x5, starting transfers between devices, exchange(): return lax.ppermute(array, axis, [(0, 1), (1, 0)])  4.43 us
    ppermute x1, starting transfers between devices, across(): return lax.ppermute(array, ('tm', 'win'), pairs)  3.37 us
    ppermute x5, waiting for transfers between devices, exchange(): return lax.ppermute(array, axis, [(0, 1), (1, 0)])  2.88 us
    ppermute x3, waiting for transfers between devices, along(): lax.ppermute(array, 'chan', [(i, (i + by) % blocks) for i in range(blocks)])  2.65 us
    pallas_call x1, Pallas kernels, mirrored(): pl.pallas_call(own_spectra_kernel, out_shape=jax.ShapeDtypeStruct((2, *wh...  2.49 us
    pallas_call x1, Pallas kernels, decimate(): pl.pallas_call(functools.partial(decimate_kernel, by), out_shape=(piece,...  2.37 us
    pallas_call x1, Pallas kernels, mirrored(): pl.pallas_call(functools.partial(near_pairs_kernel, 1, scale), out_shape=...  1.67 us
  transfers between devices with their start and end apart: 9, of which 4 were waited for; matrix products, arithmetic and copies ran while one was open for 0% of the time, Pallas kernels for 21%

profile of v5, /device:TPU:1, one launch (start us, length us, event | category | flops | bytes accessed | tf_op | source)
XLA Modules:
  0.0 31.0 jit_solution(14687790345616939416)
XLA Ops:
  0.0 0.1 pad_add_fusion.place_ref
  0.1 2.4 %decimate.1 = (bf16[17,4,8,128]{3,2,1,0:T(8,128)(2,1)S(1)}, bf16[17,4,8,128]{3,2,1,0:T(8,128)(2,1)S(1)}) custom-call(s32[2]{0:T(128)S(1)} %pad_add_fusion.place_ref, s32[8]{0:T(128)} %end_hbm.1, bf16[1,64]{1,0:T(2,128)(2,1)} %bitcast.3, bf16[8,8,8192]{2,1,0:T(8,128)(2,1)} %rec_hbm.1), custom_call_target="tpu_custom_call" | custom-call | flops 134217728 | bytes 1572864 | tf_op jit(solution)/shard_map/decimate/pallas_call | solution.py:186
  2.5 2.2 %collective-permute-start.2 = (bf16[17,4,8,128]{3,2,1,0:T(8,128)(2,1)S(1)}, bf16[17,4,8,128]{3,2,1,0:T(8,128)(2,1)S(1)}, u32[]{:S(2)}, u32[]{:S(2)}) collective-permute-start(bf16[17,4,8,128]{3,2,1,0:T(8,128)(2,1)S(1)} %get-tuple-element.10.send_ref), channel_id=1, source_target_pairs={{0,4},{4,8},{8,12},{12,0},{1,5},{5,9},{9,13},{13,1},{2,6},{6,10},{... | collective-permute-start | bytes 417800 | tf_op jit(solution)/shard_map/ppermute | solution.py:595
  4.6 1.2 %collective-permute-start = (bf16[17,4,8,128]{3,2,1,0:T(8,128)(2,1)S(1)}, bf16[17,4,8,128]{3,2,1,0:T(8,128)(2,1)S(1)}, u32[]{:S(2)}, u32[]{:S(2)}) collective-permute-start(bf16[17,4,8,128]{3,2,1,0:T(8,128)(2,1)S(1)} %get-tuple-element.9.keep_ref), channel_id=1, source_target_pairs={{0,2},{2,0},{1,3},{3,1},{4,6},{6,4},{5,7},{7,5},{8,10},{10,8},{9,1... | collective-permute-start | bytes 417800 | tf_op jit(solution)/shard_map/ppermute | solution.py:592
  5.9 0.3 collective-permute-start.1
  6.1 1.3 %collective-permute-start.5 = (bf16[17,4,8,128]{3,2,1,0:T(8,128)(2,1)S(1)}, bf16[17,4,8,128]{3,2,1,0:T(8,128)(2,1)S(1)}, u32[]{:S(2)}, u32[]{:S(2)}) collective-permute-start(bf16[17,4,8,128]{3,2,1,0:T(8,128)(2,1)S(1)} %get-tuple-element.9.keep_ref), channel_id=1, source_target_pairs={{0,4},{4,8},{8,12},{12,0},{1,5},{5,9},{9,13},{13,1},{2,6},{6,10},{... | collective-permute-start | bytes 417800 | tf_op jit(solution)/shard_map/ppermute | solution.py:595
  7.4 2.6 %collective-permute-done.2 = bf16[17,4,8,128]{3,2,1,0:T(8,128)(2,1)S(1)} collective-permute-done((bf16[17,4,8,128]{3,2,1,0:T(8,128)(2,1)S(1)}, bf16[17,4,8,128]{3,2,1,0:T(8,128)(2,1)S(1)}, u32[]{:S(2)}, u32[]{:S(2)}) %collective-permute-start.2) | collective-permute-done | bytes 139296 | tf_op jit(solution)/shard_map/ppermute | solution.py:595
  10.1 1.0 %collective-permute-start.3 = (bf16[17,4,8,128]{3,2,1,0:T(8,128)(2,1)S(1)}, bf16[17,4,8,128]{3,2,1,0:T(8,128)(2,1)S(1)}, u32[]{:S(2)}, u32[]{:S(2)}) collective-permute-start(bf16[17,4,8,128]{3,2,1,0:T(8,128)(2,1)S(1)} %collective-permute-done.2), channel_id=1, source_target_pairs={{0,2},{2,0},{1,3},{3,1},{4,6},{6,4},{5,7},{7,5},{8,10},{10,8},{9,1... | collective-permute-start | bytes 417800 | tf_op jit(solution)/shard_map/ppermute | solution.py:592
  11.0 0.0 collective-permute-done.their_keep_ref
  11.0 0.8 %collective-permute-done.1.their_send_ref = bf16[17,4,8,128]{3,2,1,0:T(8,128)(2,1)S(1)} collective-permute-done((bf16[17,4,8,128]{3,2,1,0:T(8,128)(2,1)S(1)}, bf16[17,4,8,128]{3,2,1,0:T(8,128)(2,1)S(1)}, u32[]{:S(2)}, u32[]{:S(2)}) %collective-permute-start.1) | collective-permute-done | bytes 139296 | tf_op jit(solution)/shard_map/ppermute | solution.py:592
  11.9 2.5 %own_spectra.1.white_ref = bf16[2,2,4,17,8,128]{5,4,3,2,1,0:T(8,128)(2,1)S(1)} custom-call(s32[2]{0:T(128)S(1)} %pad_add_fusion.place_ref, bf16[17,4,8,128]{3,2,1,0:T(8,128)(2,1)S(1)} %get-tuple-element.9.keep_ref, bf16[17,4,8,128]{3,2,1,0:T(8,128)(2,1)S(1)} %get-tuple-element.10.send_ref, bf16[17,4,8,128]{3,2,1,0:T(8,128)(2,1)S(1)} %collective-permute-done.their_keep_ref, ...), custom_call_target="tpu_custom_call" | custom-call | flops 5000000000 | bytes 1024 | tf_op jit(solution)/shard_map/own_spectra/pallas_call | solution.py:605
  14.4 0.5 %collective-permute-done.3.relayed_ref = bf16[17,4,8,128]{3,2,1,0:T(8,128)(2,1)S(1)} collective-permute-done((bf16[17,4,8,128]{3,2,1,0:T(8,128)(2,1)S(1)}, bf16[17,4,8,128]{3,2,1,0:T(8,128)(2,1)S(1)}, u32[]{:S(2)}, u32[]{:S(2)}) %collective-permute-start.3) | collective-permute-done | bytes 139296 | tf_op jit(solution)/shard_map/ppermute | solution.py:592
  14.9 1.9 %collective-permute-start.4 = (bf16[2,2,4,17,8,128]{5,4,3,2,1,0:T(8,128)(2,1)S(1)}, bf16[2,2,4,17,8,128]{5,4,3,2,1,0:T(8,128)(2,1)S(1)}, u32[]{:S(2)}, u32[]{:S(2)}) collective-permute-start(bf16[2,2,4,17,8,128]{5,4,3,2,1,0:T(8,128)(2,1)S(1)} %own_spectra.1.white_ref), channel_id=1, source_target_pairs={{0,1},{1,0},{2,3},{3,2},{4,5},{5,4},{6,7},{7,6},{8,9},{9,8},{10,11... | collective-permute-start | bytes 1671176 | tf_op jit(solution)/shard_map/ppermute | solution.py:592
  16.8 1.3 %far_spectra.1.far_ref = bf16[2,4,17,8,128]{4,3,2,1,0:T(8,128)(2,1)S(1)} custom-call(s32[2]{0:T(128)S(1)} %pad_add_fusion.place_ref, bf16[17,4,8,128]{3,2,1,0:T(8,128)(2,1)S(1)} %collective-permute-done.5.mine_ref, bf16[17,4,8,128]{3,2,1,0:T(8,128)(2,1)S(1)} %collective-permute-done.3.relayed_ref, f32[2,17,8,128]{3,2,1,0:T(8,128)S(1)} %copy-done.3, ...), custom_call_target="tpu_custom_call" | custom-call | flops 5000000000 | bytes 1024 | tf_op jit(solution)/shard_map/far_spectra/pallas_call | solution.py:616
  18.1 0.0 copy-start
  18.1 0.0 copy-start.1
  18.1 0.1 collective-permute-start.6
  18.2 1.5 %collective-permute-done.6.fars_ref = bf16[2,4,17,8,128]{4,3,2,1,0:T(8,128)(2,1)S(1)} collective-permute-done((bf16[2,4,17,8,128]{4,3,2,1,0:T(8,128)(2,1)S(1)}, bf16[2,4,17,8,128]{4,3,2,1,0:T(8,128)(2,1)S(1)}, u32[]{:S(2)}, u32[]{:S(2)}) %collective-permute-start.6) | collective-permute-done | bytes 278560 | tf_op jit(solution)/shard_map/ppermute | solution.py:592
  19.7 0.9 %far_cross.1 = bf16[2,17,8,256]{3,2,1,0:T(8,128)(2,1)S(1)} custom-call(bf16[2,2,4,17,8,128]{5,4,3,2,1,0:T(8,128)(2,1)S(1)} %own_spectra.1.white_ref, bf16[2,2,4,17,8,128]{5,4,3,2,1,0:T(8,128)(2,1)S(1)} %collective-permute-done.4.others_ref, bf16[2,4,17,8,128]{4,3,2,1,0:T(8,128)(2,1)S(1)} %far_spectra.1.far_ref, ...), custom_call_target="tpu_custom_call" | custom-call | flops 500000000 | bytes 1024 | tf_op jit(solution)/shard_map/far_cross/pallas_call | solution.py:626
  20.6 3.4 %collective-permute-start.8 = (bf16[2,17,8,256]{3,2,1,0:T(8,128)(2,1)S(1)}, bf16[2,17,8,256]{3,2,1,0:T(8,128)(2,1)S(1)}, u32[]{:S(2)}, u32[]{:S(2)}) collective-permute-start(bf16[2,17,8,256]{3,2,1,0:T(8,128)(2,1)S(1)} %far_cross.1), channel_id=1, source_target_pairs={{0,0},{1,2},{2,1},{3,3},{4,4},{5,6},{6,5},{7,7},{8,8},{9,10},{10,9... | collective-permute-start | bytes 417800 | tf_op jit(solution)/shard_map/ppermute | solution.py:599
  24.0 2.8 %collective-permute-start.7 = (bf16[2,17,8,256]{3,2,1,0:T(8,128)(2,1)S(1)}, bf16[2,17,8,256]{3,2,1,0:T(8,128)(2,1)S(1)}, u32[]{:S(2)}, u32[]{:S(2)}) collective-permute-start(bf16[2,17,8,256]{3,2,1,0:T(8,128)(2,1)S(1)} %far_cross.1), channel_id=1, source_target_pairs={{0,12},{4,0},{8,4},{12,8},{1,13},{5,1},{9,5},{13,9},{2,14},{6,2},{... | collective-permute-start | bytes 417800 | tf_op jit(solution)/shard_map/ppermute | solution.py:595
  26.8 1.7 %near_pairs.1.near_ref = f32[4,4,3840]{2,1,0:T(4,128)S(1)} custom-call(s32[2]{0:T(128)S(1)} %pad_add_fusion.place_ref, s32[1,3]{1,0:T(1,128)S(1)} %copy-done, bf16[2,2,4,17,8,128]{5,4,3,2,1,0:T(8,128)(2,1)S(1)} %own_spectra.1.white_ref, bf16[2,2,4,17,8,128]{5,4,3,2,1,0:T(8,128)(2,1)S(1)} %collective-permute-done.4.others_ref, ...), custom_call_target="tpu_custom_call" | custom-call | flops 500000000 | bytes 1024 | tf_op jit(solution)/shard_map/near_pairs/pallas_call | solution.py:636
  28.4 1.0 %across_lags.1.across_ref = f32[4,4,3840]{2,1,0:T(4,128)S(1)} custom-call(s32[1,3]{1,0:T(1,128)S(1)} %copy-done, bf16[2,17,8,256]{3,2,1,0:T(8,128)(2,1)S(1)} %collective-permute-done.8.cross_ref, f32[2,17,8,128]{3,2,1,0:T(8,128)S(1)} %copy-done.3, bf16[2,256,256]{2,1,0:T(8,128)(2,1)S(1)} %copy-done.1), custom_call_target="tpu_custom_call" | custom-call | flops 500000000 | bytes 1024 | tf_op jit(solution)/shard_map/across_lags/pallas_call | solution.py:645
  29.4 1.5 %back_lags.1 = f32[3,4,4,3840]{3,2,1,0:T(4,128)} custom-call(s32[1,3]{1,0:T(1,128)S(1)} %copy-done, bf16[2,17,8,256]{3,2,1,0:T(8,128)(2,1)S(1)} %collective-permute-done.7.cross_ref, f32[4,4,3840]{2,1,0:T(4,128)S(1)} %near_pairs.1.near_ref, f32[4,4,3840]{2,1,0:T(4,128)S(1)} %across_lags.1.across_ref, f32[2,17,8,128]{3,2,1,0:T(8,128)S(1)} %copy-done.3, ...), custom_call_target="tpu_custom_call" | custom-call | flops 500000000 | bytes 1024 | tf_op jit(solution)/shard_map/back_lags/pallas_call | solution.py:654
  (12 shorter events, 0.0 us)
Async XLA Ops:
  0.1 11.8 %copy-start.2 = (bf16[2,256,256]{2,1,0:T(8,128)(2,1)S(1)}, bf16[2,256,256]{2,1,0:T(8,128)(2,1)}, u32[]{:S(2)}) copy-start(bf16[2,256,256]{2,1,0:T(8,128)(2,1)} %constant.15.clone.dft_ref) | copy-start | bytes 786436
  0.1 11.8 %copy-start.3 = (f32[2,17,8,128]{3,2,1,0:T(8,128)S(1)}, f32[2,17,8,128]{3,2,1,0:T(8,128)}, u32[]{:S(2)}) copy-start(f32[2,17,8,128]{3,2,1,0:T(8,128)} %constant.14.clone.twist_ref) | copy-start | bytes 417796
  0.1 11.8 %copy-start.4 = (bf16[128,128]{1,0:T(8,128)(2,1)S(1)}, bf16[128,128]{1,0:T(8,128)(2,1)}, u32[]{:S(2)}) copy-start(bf16[128,128]{1,0:T(8,128)(2,1)} %constant.17.clone.band_ref) | copy-start | bytes 98308
  2.5 7.6 %collective-permute-start.2 = (bf16[17,4,8,128]{3,2,1,0:T(8,128)(2,1)S(1)}, bf16[17,4,8,128]{3,2,1,0:T(8,128)(2,1)S(1)}, u32[]{:S(2)}, u32[]{:S(2)}) collective-permute-start(bf16[17,4,8,128]{3,2,1,0:T(8,128)(2,1)S(1)} %get-tuple-element.10.send_ref), channel_id=1, source_target_pairs={{0,4},{4,8},{8,12},{12,0},{1,5},{5,9},{9,13},{13,1},{2,6},{6,10},{... | collective-permute-start | bytes 417800 | tf_op jit(solution)/shard_map/ppermute | solution.py:595
  4.6 6.4 %collective-permute-start = (bf16[17,4,8,128]{3,2,1,0:T(8,128)(2,1)S(1)}, bf16[17,4,8,128]{3,2,1,0:T(8,128)(2,1)S(1)}, u32[]{:S(2)}, u32[]{:S(2)}) collective-permute-start(bf16[17,4,8,128]{3,2,1,0:T(8,128)(2,1)S(1)} %get-tuple-element.9.keep_ref), channel_id=1, source_target_pairs={{0,2},{2,0},{1,3},{3,1},{4,6},{6,4},{5,7},{7,5},{8,10},{10,8},{9,1... | collective-permute-start | bytes 417800 | tf_op jit(solution)/shard_map/ppermute | solution.py:592
  5.9 6.0 %collective-permute-start.1 = (bf16[17,4,8,128]{3,2,1,0:T(8,128)(2,1)S(1)}, bf16[17,4,8,128]{3,2,1,0:T(8,128)(2,1)S(1)}, u32[]{:S(2)}, u32[]{:S(2)}) collective-permute-start(bf16[17,4,8,128]{3,2,1,0:T(8,128)(2,1)S(1)} %get-tuple-element.10.send_ref), channel_id=1, source_target_pairs={{0,2},{2,0},{1,3},{3,1},{4,6},{6,4},{5,7},{7,5},{8,10},{10,8},{9,1... | collective-permute-start | bytes 417800 | tf_op jit(solution)/shard_map/ppermute | solution.py:592
  6.1 10.7 %collective-permute-start.5 = (bf16[17,4,8,128]{3,2,1,0:T(8,128)(2,1)S(1)}, bf16[17,4,8,128]{3,2,1,0:T(8,128)(2,1)S(1)}, u32[]{:S(2)}, u32[]{:S(2)}) collective-permute-start(bf16[17,4,8,128]{3,2,1,0:T(8,128)(2,1)S(1)} %get-tuple-element.9.keep_ref), channel_id=1, source_target_pairs={{0,4},{4,8},{8,12},{12,0},{1,5},{5,9},{9,13},{13,1},{2,6},{6,10},{... | collective-permute-start | bytes 417800 | tf_op jit(solution)/shard_map/ppermute | solution.py:595
  10.1 4.8 %collective-permute-start.3 = (bf16[17,4,8,128]{3,2,1,0:T(8,128)(2,1)S(1)}, bf16[17,4,8,128]{3,2,1,0:T(8,128)(2,1)S(1)}, u32[]{:S(2)}, u32[]{:S(2)}) collective-permute-start(bf16[17,4,8,128]{3,2,1,0:T(8,128)(2,1)S(1)} %collective-permute-done.2), channel_id=1, source_target_pairs={{0,2},{2,0},{1,3},{3,1},{4,6},{6,4},{5,7},{7,5},{8,10},{10,8},{9,1... | collective-permute-start | bytes 417800 | tf_op jit(solution)/shard_map/ppermute | solution.py:592
  14.9 4.8 %collective-permute-start.4 = (bf16[2,2,4,17,8,128]{5,4,3,2,1,0:T(8,128)(2,1)S(1)}, bf16[2,2,4,17,8,128]{5,4,3,2,1,0:T(8,128)(2,1)S(1)}, u32[]{:S(2)}, u32[]{:S(2)}) collective-permute-start(bf16[2,2,4,17,8,128]{5,4,3,2,1,0:T(8,128)(2,1)S(1)} %own_spectra.1.white_ref), channel_id=1, source_target_pairs={{0,1},{1,0},{2,3},{3,2},{4,5},{5,4},{6,7},{7,6},{8,9},{9,8},{10,11... | collective-permute-start | bytes 1671176 | tf_op jit(solution)/shard_map/ppermute | solution.py:592
  18.1 8.7 %copy-start = (s32[1,3]{1,0:T(1,128)S(1)}, s32[1,3]{1,0:T(1,128)}, u32[]{:S(2)}) copy-start(s32[1,3]{1,0:T(1,128)} %mask_ref.5) | copy-start | bytes 40
  18.1 8.7 %copy-start.1 = (bf16[2,256,256]{2,1,0:T(8,128)(2,1)S(1)}, bf16[2,256,256]{2,1,0:T(8,128)(2,1)}, u32[]{:S(2)}) copy-start(bf16[2,256,256]{2,1,0:T(8,128)(2,1)} %constant.16.clone.inverse_ref) | copy-start | bytes 786436
  18.1 1.6 %collective-permute-start.6 = (bf16[2,4,17,8,128]{4,3,2,1,0:T(8,128)(2,1)S(1)}, bf16[2,4,17,8,128]{4,3,2,1,0:T(8,128)(2,1)S(1)}, u32[]{:S(2)}, u32[]{:S(2)}) collective-permute-start(bf16[2,4,17,8,128]{4,3,2,1,0:T(8,128)(2,1)S(1)} %far_spectra.1.far_ref), channel_id=1, source_target_pairs={{0,1},{1,0},{2,3},{3,2},{4,5},{5,4},{6,7},{7,6},{8,9},{9,8},{10,11... | collective-permute-start | bytes 835592 | tf_op jit(solution)/shard_map/ppermute | solution.py:592
  20.6 7.8 %collective-permute-start.8 = (bf16[2,17,8,256]{3,2,1,0:T(8,128)(2,1)S(1)}, bf16[2,17,8,256]{3,2,1,0:T(8,128)(2,1)S(1)}, u32[]{:S(2)}, u32[]{:S(2)}) collective-permute-start(bf16[2,17,8,256]{3,2,1,0:T(8,128)(2,1)S(1)} %far_cross.1), channel_id=1, source_target_pairs={{0,0},{1,2},{2,1},{3,3},{4,4},{5,6},{6,5},{7,7},{8,8},{9,10},{10,9... | collective-permute-start | bytes 417800 | tf_op jit(solution)/shard_map/ppermute | solution.py:599
  24.0 5.4 %collective-permute-start.7 = (bf16[2,17,8,256]{3,2,1,0:T(8,128)(2,1)S(1)}, bf16[2,17,8,256]{3,2,1,0:T(8,128)(2,1)S(1)}, u32[]{:S(2)}, u32[]{:S(2)}) collective-permute-start(bf16[2,17,8,256]{3,2,1,0:T(8,128)(2,1)S(1)} %far_cross.1), channel_id=1, source_target_pairs={{0,12},{4,0},{8,4},{12,8},{1,13},{5,1},{9,5},{13,9},{2,14},{6,2},{... | collective-permute-start | bytes 417800 | tf_op jit(solution)/shard_map/ppermute | solution.py:595
